TPU v7x, 256 devices: a whole 4x4x8 slice. The times are simulated.
256 devices in a mesh: lat: 32 (over x_lo, z, core), ch: 8 (over y, x_hi).
Axes of the slice: x: 4 (x_hi: 2, x_lo: 2; x = x_hi * 2 + x_lo), y: 4, z: 8, core: 2. Of those that a mesh axis runs over, the one named last changes fastest.
Arguments:
- spectrum: bfloat16 [512, 64, 2, 2, 256], P('lat', 'ch'), may hold values from -0.01953125 to 0.01953125
- legendre: bfloat16 [640, 256, 512], P('lat'), as said below
- block_slots: int32 [32], replicated, may hold values from 0 to 31, each once
- kernel_values: bfloat16 [3, 640, 6, 9], P(None, 'lat'), may hold values from -2 to 2
- near_rows: int32 [640, 6], P('lat'), may hold values from 0 to 639, as said below
- mix_weights: bfloat16 [3, 64, 64], replicated, may hold values from -0.4375 to 0.4375
Outputs:
- convolved: bfloat16 [64, 640, 1440], P('ch', 'lat')
Inputs may be any that keep to these rules, and one draw needn't show every extreme that they name: legendre[r, k, m] is zero where m + 2 * k + p >= 512, with p = 0 for r < 320 and p = 1 otherwise. near_rows[r, q] lies within 2 rows of r; slot 0 holds max(r - 2, 0) and slot 1 holds min(r + 2, 639). `block_slots`: each order block appears once.
All inputs are finite; a program needn't handle non-finite values.
Results may differ from a plain program's by a relative error of at most 0.005.
Values may be sent and summed in bfloat16 or wider, within the bound.
No kernel may reach another device: no remote copies, remote signals or barrier semaphores. Data moves between devices by JAX's collectives and lax.ppermute only.
A program may use at most 320 MiB of HBM per device.

v0:
```python
import math

import jax
import jax.numpy as jnp
from jax import lax
from jax.sharding import PartitionSpec as P

NLON = 1440
LMAX = 512
ORDER_BLOCK = 16
KER = 3
REACH = 2
LON_REACH = 4
TAPS = 9


def padded_2(shard, sides, width):
    for axis, dim in sides:
        count, length = (lax.axis_size(axis), shard.shape[dim])
        up = [(i, (i + 1) % count) for i in range(count - 1)]
        down = [(j, i) for i, j in up]
        last = lax.slice_in_dim(shard, length - width, length, axis=dim)
        first = lax.slice_in_dim(shard, 0, width, axis=dim)
        before = lax.ppermute(last, axis, up)
        after = lax.ppermute(first, axis, down)
        shard = jnp.concatenate([before, shard, after], axis=dim)
    return shard


def fourier_table():
    orders = jnp.arange(LMAX, dtype=jnp.int32)
    places = jnp.arange(NLON, dtype=jnp.int32)
    phases = orders[:, None] * places[None, :] % NLON
    angles = phases.astype(jnp.float32) * (2.0 * math.pi / NLON)
    weight = jnp.where(orders == 0, 1.0, 2.0).astype(jnp.float32)[:, None]
    return jnp.concatenate([weight * jnp.cos(angles), -weight * jnp.sin(angles)], axis=0)


def per_device(spectrum, legendre, block_slots, kernel_values, near_rows, mix_weights):
    lat_count = lax.axis_size("lat")
    lat_index = lax.axis_index("lat")
    ch_index = lax.axis_index("ch")
    row_count = legendre.shape[0]
    chan_dev = spectrum.shape[1]
    northern = lat_index < lat_count // 2
    parity = jnp.where(northern, 0, 1).astype(jnp.int32)
    zero_sum = jnp.zeros((row_count, chan_dev, 2, LMAX), jnp.float32)
    chosen = lax.dynamic_index_in_dim(
        lax.all_gather(spectrum, "lat", axis=0, tiled=True), parity, 2, keepdims=False
    )
    slot_rows = jnp.arange(chosen.shape[0], dtype=jnp.int32)
    order_ids = block_slots[slot_rows // ORDER_BLOCK] * ORDER_BLOCK + slot_rows % ORDER_BLOCK
    columns = jnp.take(legendre, order_ids, axis=2)
    contribution = jnp.einsum("rkn,ncxk->rcxn", columns, chosen, preferred_element_type=jnp.float32)
    partial_sum = zero_sum.at[:, :, :, order_ids].add(contribution)
    split_sums = partial_sum.reshape(row_count, chan_dev, 2, lat_count, LMAX // lat_count)
    by_source = lax.all_to_all(split_sums, "lat", split_axis=3, concat_axis=3, tiled=True)
    flipped = by_source[:, :, :, ::-1]
    returned = lax.all_to_all(flipped, "lat", split_axis=3, concat_axis=3, tiled=True)
    mirrored = returned.reshape(row_count, chan_dev, 2, LMAX)
    mirror_sign = jnp.where(northern, -1.0, 1.0).astype(jnp.float32)
    spectral = partial_sum + mirror_sign * mirrored[::-1]
    grid_field = jnp.dot(
        spectral.reshape(row_count * chan_dev, 2 * LMAX),
        fourier_table(),
        precision=lax.Precision.HIGHEST,
        preferred_element_type=jnp.float32,
    )
    grid_field = grid_field.reshape(row_count, chan_dev, NLON).astype(jnp.bfloat16)
    local_rows = near_rows - (lat_index * row_count - REACH)
    padded = padded_2(grid_field, (("lat", 0),), REACH)
    gathered = jnp.take(padded, local_rows, axis=0)
    spread = jnp.zeros((KER, row_count, chan_dev, NLON), jnp.float32)
    for offset in range(TAPS):
        rolled = jnp.roll(gathered, LON_REACH - offset, axis=3)
        spread = spread + jnp.einsum(
            "kiq,iqcx->kicx",
            kernel_values[:, :, :, offset],
            rolled,
            preferred_element_type=jnp.float32,
        )
    own_weights = lax.dynamic_slice_in_dim(mix_weights, ch_index * chan_dev, chan_dev, 1)
    weight_cols = own_weights.astype(jnp.float32)
    return lax.psum_scatter(
        jnp.einsum("kcd,kicx->dix", weight_cols, spread, precision=lax.Precision.HIGHEST),
        "ch",
        scatter_dimension=0,
        tiled=True,
    ).astype(jnp.bfloat16)


def solution(mesh):
    return jax.shard_map(
        per_device,
        mesh=mesh,
        in_specs=(
            P("lat", "ch", None, None, None),
            P("lat", None, None),
            P(),
            P(None, "lat", None, None),
            P("lat", None),
            P(),
        ),
        out_specs=P("ch", "lat", None),
        check_vma=False,
    )
```

profile of v0, /device:TPU:8, one launch (start us, length us, event | category | flops | bytes accessed | tf_op | source)
XLA Modules:
  0.0 489.2 jit_solution(12187650134679098284)
XLA Ops:
  8.3 8.9 %copy.18 = bf16[20,256,512]{1,0,2:T(8,128)(2,1)} copy(bf16[20,256,512]{2,1,0:T(8,128)(2,1)} %param.7) | data formatting | bytes 10485760 | tf_op args[1]
  24.0 16.1 %compare_and_fusion.1 = (pred[512]{0:T(512)(128)(4,1)S(1)}, s32[512]{0:T(512)S(1)}) fusion(pred[512]{0:T(512)(128)(4,1)S(1)} %compare_reduce_fusion, pred[512]{0:T(512)(128)(4,1)S(1)} %compare_reduce_fusion.1, pred[512]{0:T(512)(128)(4,1)S(1)} %compare_reduce_fusion.2, pred[512]{0:T(512)(128)(4,1)S(1)} %compare_reduce_fusion.3, ...), kind=kLoop, calls=%fused_computation.126 | loop fusion | flops 19968 | bytes 17508 | tf_op jit(solution)/shard_map/jit(_take)/and | solution.py:53
  40.2 6.4 %gather_fusion = bf16[512,20,256]{2,1,0:T(8,128)(2,1)} fusion(bf16[20,256,512]{1,0,2:T(8,128)(2,1)} %copy.18, s32[1024]{0:T(1024)S(1)} %pad_clamp_fusion.1), kind=kCustom, calls=%fused_computation | custom fusion | bytes 10487808 | tf_op jit(solution)/shard_map/jit(_take)/gather | solution.py:53
  46.6 38.0 %all-gather.2.cloned.1.call-done = bf16[512,8,2,2,256]{4,1,3,2,0:T(8,128)(2,1)} async-done(((bf16[16,8,2,2,256]{4,1,3,2,0:T(8,128)(2,1)}), bf16[512,8,2,2,256]{4,1,3,2,0:T(8,128)(2,1)}) %all-gather.2.cloned.1.call-update) | async-done | bytes 8388624 | tf_op jit(solution)/shard_map/all_gather | solution.py:49
  84.6 7.8 %fusion = f32[512,20,8,2]{1,2,3,0:T(8,128)} fusion(bf16[512,20,256]{2,1,0:T(8,128)(2,1)} %gather_fusion, pred[512]{0:T(512)(128)(4,1)S(1)} %get-tuple-element.7, bf16[512,8,2,2,256]{4,1,3,2,0:T(8,128)(2,1)} %all-gather.2.cloned.1.call-done, s32[]{:T(128)S(6)} %select_n.109), kind=kOutput, calls=%fused_computation.3 | convolution fusion | flops 86507520 | bytes 11141636 | tf_op jit(solution)/shard_map/rkn,ncxk->rcxn/dot_general | solution.py:54
  94.6 61.8 %scatter_fusion = f32[20,8,2,512]{0,1,3,2:T(8,128)} fusion(f32[20,8,2,512]{0,1,3,2:T(8,128)} %broadcast_in_dim.39, s32[512]{0:T(512)S(1)} %bitcast.115, f32[512,20,8,2]{1,2,3,0:T(8,128)} %fusion), kind=kCustom, calls=%fused_computation.2 | custom fusion | flops 163840 | bytes 1968128 | tf_op jit(solution)/shard_map/scatter-add | solution.py:55
  161.1 6.5 %reshape.292 = f32[32,1,5120]{2,1,0:T(1,128)} reshape(f32[32,2,16,8,20]{4,3,2,1,0:T(8,128)} %bitcast.113) | data formatting | bytes 1310720
  167.6 6.6 %all-to-all-start = ((f32[32,1,5120]{2,1,0:T(1,128)}), f32[32,1,5120]{2,1,0:T(1,128)S(1)}, u32[]{:S(2)}, u32[]{:S(2)}) async-start(f32[32,1,5120]{2,1,0:T(1,128)} %reshape.292), calls=%async_computation | async-start | bytes 1310720 | tf_op jit(solution)/shard_map/all_to_all | solution.py:57
  174.2 20.8 %all-to-all-done = f32[32,1,5120]{2,1,0:T(1,128)S(1)} async-done(((f32[32,1,5120]{2,1,0:T(1,128)}), f32[32,1,5120]{2,1,0:T(1,128)S(1)}, u32[]{:S(2)}, u32[]{:S(2)}) %all-to-all-start) | async-done | bytes 655392 | tf_op jit(solution)/shard_map/all_to_all | solution.py:57
  197.7 6.2 %reshape.293 = f32[32,2,16,8,20]{4,3,2,1,0:T(8,128)} reshape(f32[32,5120]{1,0:T(8,128)S(1)} %reduce.50) | data formatting | bytes 1310720
  208.6 6.5 %reshape.294 = f32[32,1,5120]{2,1,0:T(1,128)} reshape(f32[32,2,16,8,20]{4,3,2,1,0:T(8,128)} %reverse_bitcast_fusion) | data formatting | bytes 1310720
  221.3 13.3 %sine_multiply_fusion = (f32[512,1440]{0,1:T(8,128)S(1)}, f32[512,1440]{0,1:T(8,128)}) fusion(f32[512]{0:T(512)S(1)} %fusion.66, f32[512]{0:T(512)S(1)} %fusion.65), kind=kLoop, calls=%fused_computation.54 | loop fusion | flops 8110080 | bytes 5902336 | tf_op jit(solution)/shard_map/mul | solution.py:36
  234.6 5.9 %all-to-all-done.1 = f32[32,1,5120]{2,1,0:T(1,128)} async-done(((f32[32,1,5120]{2,1,0:T(1,128)}), f32[32,1,5120]{2,1,0:T(1,128)}, u32[]{:S(2)}, u32[]{:S(2)}) %all-to-all-start.1) | async-done | bytes 655392 | tf_op jit(solution)/shard_map/all_to_all | solution.py:59
  244.6 7.2 %reshape.295 = f32[32,2,16,8,20]{4,3,2,1,0:T(8,128)} reshape(f32[32,5120]{1,0:T(8,128)} %reduce.51) | data formatting | bytes 1310720
  251.8 4.7 copy.21
  256.5 7.3 %rev.7 = f32[20,8,2,512]{0,1,3,2:T(8,128)} reverse(f32[20,8,2,512]{0,1,3,2:T(8,128)} %bitcast.112), dimensions={0} | reverse | bytes 1310720 | tf_op jit(solution)/shard_map/rev | solution.py:62
  263.8 5.8 %multiply_add_fusion = f32[20,8,2,512]{0,1,3,2:T(8,128)} fusion(f32[20,8,2,512]{0,1,3,2:T(8,128)} %scatter_fusion, f32[20,8,2,512]{0,1,3,2:T(8,128)} %rev.7, f32[]{:T(128)S(6)} %select_n.113), kind=kLoop, calls=%fused_computation.14 | loop fusion | flops 327680 | bytes 1966084 | tf_op jit(solution)/shard_map/add | solution.py:62
  273.4 7.5 %fusion.48 = bf16[20,8,1440]{2,1,0:T(8,128)(2,1)S(1)} fusion(f32[20,8,1024]{2,1,0:T(8,128)} %copy.22, f32[512,1440]{0,1:T(8,128)S(1)} %get-tuple-element.68, f32[512,1440]{0,1:T(8,128)} %get-tuple-element.69), kind=kOutput, calls=%fused_computation.60 | convolution fusion | flops 2832860160 | bytes 7014400 | tf_op jit(solution)/shard_map/dot_general | solution.py:63
  312.9 5.2 %fusion.25 = f32[20,8,1440,3]{2,3,1,0:T(4,128)} fusion(bf16[20,6,8,1]{3,1,2,0:T(8,128)(2,1)S(1)} %get-tuple-element.22, bf16[20,6,8,1439]{3,1,2,0:T(8,128)(2,1)} %get-tuple-element.24, bf16[3,20,6,1]{2,0,1,3:T(4,128)(2,1)S(1)} %copy-done.4), kind=kOutput, calls=%fused_computation.32 | convolution fusion | flops 13824000 | bytes 5530320 | tf_op jit(solution)/shard_map/kiq,iqcx->kicx/dot_general | solution.py:76
  318.1 5.5 %fusion.17 = f32[20,8,1440,3]{2,3,1,0:T(4,128)} fusion(bf16[20,6,8,1438]{3,1,2,0:T(8,128)(2,1)} %get-tuple-element.19, bf16[20,6,8,2]{3,1,2,0:T(8,128)(2,1)S(1)} %get-tuple-element.17, bf16[3,20,6,1]{2,0,1,3:T(4,128)(2,1)S(1)} %copy-done.5), kind=kOutput, calls=%fused_computation.24 | convolution fusion | flops 13824000 | bytes 5530320 | tf_op jit(solution)/shard_map/kiq,iqcx->kicx/dot_general | solution.py:76
  323.6 5.3 %fusion.29 = f32[20,8,1440,3]{2,3,1,0:T(4,128)} fusion(bf16[20,6,8,2]{3,1,2,0:T(8,128)(2,1)S(1)} %get-tuple-element.18, bf16[20,6,8,1438]{3,1,2,0:T(8,128)(2,1)} %get-tuple-element.20, bf16[3,20,6,1]{2,0,1,3:T(4,128)(2,1)S(1)} %copy-done.2), kind=kOutput, calls=%fused_computation.36 | convolution fusion | flops 13824000 | bytes 5530320 | tf_op jit(solution)/shard_map/kiq,iqcx->kicx/dot_general | solution.py:76
  342.0 13.6 %add_bitcast_fusion = f32[3,20,8,1440]{3,0,2,1:T(4,128)} fusion(f32[20,8,1440,3]{2,3,1,0:T(4,128)} %fusion.37, f32[20,8,1440,3]{2,3,1,0:T(4,128)} %fusion.33, f32[20,8,1440,3]{2,3,1,0:T(4,128)} %fusion.29, f32[20,8,1440,3]{2,3,1,0:T(4,128)} %fusion.25, f32[20,8,1440,3]{2,3,1,0:T(4,128)S(1)} %fusion.21, f32[20,8,1440,3]{2,3,1,0:T(4,128)} %fusion.17, ...), kind=kOutput, calls=%fused_computation.49 | convolution fusion | flops 15206400 | bytes 27648840 | tf_op jit(solution)/shard_map/kiq,iqcx->kicx/dot_general | solution.py:76
  355.6 8.7 %convolution_bitcast_fusion = f32[64,20,1440]{2,0,1:T(8,128)} fusion(f32[3,20,8,1440]{3,0,2,1:T(4,128)} %add_bitcast_fusion, bf16[3,64,64]{2,1,0:T(8,128)(2,1)S(1)} %copy-done, s32[]{:T(128)S(6)} %select_n.103), kind=kOutput, calls=%fused_computation.11 | convolution fusion | flops 530841600 | bytes 10143748 | tf_op jit(solution)/shard_map/kcd,kicx->dix/dot_general | solution.py:85
  364.3 115.4 %reduce-scatter.2.cloned.1.call-done = f32[8,20,1440]{2,0,1:T(8,128)} async-done(((f32[64,20,1440]{2,0,1:T(8,128)}), f32[8,20,1440]{2,0,1:T(8,128)}) %reduce-scatter.2.cloned.1.call-update) | async-done | bytes 921616 | tf_op jit(solution)/shard_map/reduce_scatter | solution.py:84
  (106 shorter events, 83.7 us)
Async XLA Ops:
  6.5 349.1 %copy-start = (bf16[3,64,64]{2,1,0:T(8,128)(2,1)S(1)}, bf16[3,64,64]{2,1,0:T(8,128)(2,1)}, u32[]{:S(2)}) copy-start(bf16[3,64,64]{2,1,0:T(8,128)(2,1)} %param.11) | copy-start | bytes 73732
  6.5 78.1 %all-gather.2.cloned.1.call-start = ((), (), s32[]{:S(2)}) async-start(), calls=%async_computation.3 | async-start | bytes 8650752 | tf_op jit(solution)/shard_map/all_gather | solution.py:49
  8.3 9.8 %copy-start.1 = (s32[32]{0:T(128)S(1)}, s32[32]{0:T(128)}, u32[]{:S(2)}) copy-start(s32[32]{0:T(128)} %param.8) | copy-start | bytes 388
  167.6 27.5 %all-to-all-start = ((f32[32,1,5120]{2,1,0:T(1,128)}), f32[32,1,5120]{2,1,0:T(1,128)S(1)}, u32[]{:S(2)}, u32[]{:S(2)}) async-start(f32[32,1,5120]{2,1,0:T(1,128)} %reshape.292), calls=%async_computation | async-start | bytes 1310720 | tf_op jit(solution)/shard_map/all_to_all | solution.py:57
  208.6 11.3 %copy-start.10 = (s32[20,6]{0,1:T(8,128)S(1)}, s32[20,6]{0,1:T(8,128)}, u32[]{:S(2)}) copy-start(s32[20,6]{0,1:T(8,128)} %param.10) | copy-start | bytes 1444
  208.6 12.0 %copy-start.8 = (bf16[3,20,6,9]{1,2,3,0:T(8,128)(2,1)S(1)}, bf16[3,20,6,9]{1,2,3,0:T(8,128)(2,1)}, u32[]{:S(2)}) copy-start(bf16[3,20,6,9]{1,2,3,0:T(8,128)(2,1)} %param.9) | copy-start | bytes 19444
  215.1 25.4 %all-to-all-start.1 = ((f32[32,1,5120]{2,1,0:T(1,128)}), f32[32,1,5120]{2,1,0:T(1,128)}, u32[]{:S(2)}, u32[]{:S(2)}) async-start(f32[32,1,5120]{2,1,0:T(1,128)} %reshape.294), calls=%async_computation.1 | async-start | bytes 1310720 | tf_op jit(solution)/shard_map/all_to_all | solution.py:59
  219.7 260.1 %reduce-scatter.2.cloned.1.call-start = ((), (), s32[]{:S(2)}) async-start(), calls=%async_computation.4 | async-start | bytes 8847360 | tf_op jit(solution)/shard_map/reduce_scatter | solution.py:84
  273.4 10.4 %copy-start.11 = (s32[120]{0:T(128)S(1)}, s32[120]{0:T(128)}, u32[]{:S(2)}) copy-start(s32[120]{0:T(128)} %reshape.161) | copy-start | bytes 1444
  280.9 10.3 %collective-permute-start = (bf16[2,8,1440]{2,1,0:T(8,128)(2,1)S(1)}, bf16[2,8,1440]{2,1,0:T(8,128)(2,1)S(1)}, u32[]{:S(2)}, u32[]{:S(2)}) collective-permute-start(bf16[2,8,1440]{2,1,0:T(8,128)(2,1)S(1)} %get-tuple-element.25), channel_id=1, source_target_pairs={{0,8},{8,16},{16,24},{24,32},{32,40},{40,48},{48,56},{56,64},{64,7... | collective-permute-start | bytes 138248 | tf_op jit(solution)/shard_map/ppermute | solution.py:24
  282.2 9.0 %collective-permute-start.1 = (bf16[2,8,1440]{2,1,0:T(8,128)(2,1)S(1)}, bf16[2,8,1440]{2,1,0:T(8,128)(2,1)S(1)}, u32[]{:S(2)}, u32[]{:S(2)}) collective-permute-start(bf16[2,8,1440]{2,1,0:T(8,128)(2,1)S(1)} %get-tuple-element.26), channel_id=1, source_target_pairs={{8,0},{16,8},{24,16},{32,24},{40,32},{48,40},{56,48},{64,56},{72,6... | collective-permute-start | bytes 138248 | tf_op jit(solution)/shard_map/ppermute | solution.py:25
  292.2 1.9 copy-start.9
  306.7 2.6 copy-start.6
  309.3 3.6 copy-start.4
  312.9 5.2 %copy-start.5 = (bf16[3,20,6,1]{2,0,1,3:T(4,128)(2,1)S(1)}, bf16[3,20,6,1]{2,0,1,3:T(4,128)(2,1)}, u32[]{:S(2)}) copy-start(bf16[3,20,6,1]{2,0,1,3:T(4,128)(2,1)} %copy.48) | copy-start | bytes 2164
  318.1 5.5 %copy-start.2 = (bf16[3,20,6,1]{2,0,1,3:T(4,128)(2,1)S(1)}, bf16[3,20,6,1]{2,0,1,3:T(4,128)(2,1)}, u32[]{:S(2)}) copy-start(bf16[3,20,6,1]{2,0,1,3:T(4,128)(2,1)} %copy.52) | copy-start | bytes 2164
  323.6 5.3 %copy-start.3 = (bf16[3,20,6,1]{2,0,1,3:T(4,128)(2,1)S(1)}, bf16[3,20,6,1]{2,0,1,3:T(4,128)(2,1)}, u32[]{:S(2)}) copy-start(bf16[3,20,6,1]{2,0,1,3:T(4,128)(2,1)} %copy.47) | copy-start | bytes 2164
  338.8 3.2 copy-start.7
Sparse Core Ops, SparseCore 0:
  9.2 75.3 all-gather.1
  364.5 115.2 reduce-scatter.1
where the time goes:
time: 499 us; the launch traced here: 489 us
  waiting for transfers between devices  180 us (36%)
  other arithmetic  113 us (23%)
  local copies, waits for them, and re-layouts  97.3 us (19%)
  matrix products  70.3 us (14%)
  starting transfers between devices  14.2 us (3%)
  between operations  14.2 us (3%)
    reduce_scatter x1, waiting for transfers between devices, per_device(): lax.psum_scatter(jnp.einsum('kcd,kicx->dix', weight_cols, spread, precisi...  115 us
    scatter-add x1, other arithmetic, per_device(): partial_sum = zero_sum.at[:, :, :, order_ids].add(contribution)  61.8 us
    unnamed x40, local copies, waits for them, and re-layouts  48.5 us
    dot_general x9, matrix products, per_device(): jnp.einsum('kiq,iqcx->kicx', kernel_values[:, :, :, offset], rolled, pref...  46.3 us
    all_gather x1, waiting for transfers between devices, per_device(): lax.all_gather(spectrum, 'lat', axis=0, tiled=True)  38 us
    all_to_all x1, waiting for transfers between devices, per_device(): lax.all_to_all(split_sums, 'lat', split_axis=3, concat_axis=3, tiled=True)  20.8 us
    and x1, other arithmetic, per_device(): columns = jnp.take(legendre, order_ids, axis=2)  16.1 us
    slice x8, local copies, waits for them, and re-layouts, per_device(): rolled = jnp.roll(gathered, LON_REACH - offset, axis=3)  14 us
  transfers between devices with their start and end apart: 6, of which 4 were waited for; matrix products, arithmetic and copies ran while one was open for 12% of the time, Pallas kernels for 0%

commit v1 on v0

v1 whole, which is shorter than its diff:
```python
import math

import jax
import jax.numpy as jnp
import ml_dtypes
import numpy as np
from jax import lax
from jax.experimental import pallas as pl
from jax.experimental.pallas import tpu as pltpu
from jax.sharding import PartitionSpec as P

NLAT = 640
NLON = 1440
LMAX = 512
C = 64
ORDER_BLOCK = 16
KER = 3
SLOTS = 6
REACH = 2
LON_REACH = 4
TAPS = 9
STEPS = 256
BLOCKS = 32
LATS = 32
CHS = 8
ROWS = NLAT // LATS
OWN = C // CHS
SUB = ORDER_BLOCK // CHS
HALO_ROWS = ROWS + 2 * REACH
SPREAD = 2 * REACH + 1
PICKS = LATS * SUB
LANES = 128
BF = jnp.bfloat16
F32 = jnp.float32
NT = (((1,), (1,)), ((), ()))
VMEM = pltpu.VMEM


def longitude_table():
    orders = (
        ORDER_BLOCK * np.arange(BLOCKS)[None, :, None]
        + SUB * np.arange(CHS)[:, None, None]
        + np.arange(SUB)[None, None, :]
    ).reshape(CHS, 1, PICKS, 1)
    phases = (orders * np.arange(NLON)) % NLON
    angles = phases * (2.0 * math.pi / NLON)
    weight = np.where(orders == 0, 1.0, 2.0)
    table = np.concatenate([weight * np.cos(angles), -weight * np.sin(angles)], axis=1)
    return table.reshape(CHS * LANES, NLON).astype(ml_dtypes.bfloat16)


PICK_ROWS = 4


def pick_kernel(hot_ref, leg_ref, out_ref, buf, wide, sems):
    copies = []
    for g in range(ROWS // PICK_ROWS):
        rows = pl.ds(g * PICK_ROWS, PICK_ROWS)
        copies.append(pltpu.make_async_copy(leg_ref.at[rows], buf.at[rows], sems.at[g]))
        copies[-1].start()
    for r in range(ROWS):
        if r % PICK_ROWS == 0:
            copies[r // PICK_ROWS].wait()
        picked = lax.dot_general(hot_ref[...], buf[r], NT, preferred_element_type=F32)
        for h in range(STEPS // LANES):
            wide[h, pl.ds(r, PICKS, stride=ROWS), :] = picked[:, h * LANES : (h + 1) * LANES]
    for h in range(STEPS // LANES):
        flat = wide[h].astype(BF)
        out_ref[:, :, h * LANES : (h + 1) * LANES] = flat.reshape(LATS, SUB * ROWS, LANES)


def pick(hot, legendre):
    return pl.pallas_call(
        pick_kernel,
        out_shape=jax.ShapeDtypeStruct((LATS, SUB * ROWS, STEPS), BF),
        in_specs=[pl.BlockSpec(memory_space=VMEM), pl.BlockSpec(memory_space=pl.ANY)],
        out_specs=pl.BlockSpec(memory_space=VMEM),
        scratch_shapes=[
            pltpu.VMEM((ROWS, STEPS, LMAX), BF),
            pltpu.VMEM((STEPS // LANES, PICKS * ROWS, LANES), F32),
            pltpu.SemaphoreType.DMA((ROWS // PICK_ROWS,)),
        ],
        compiler_params=pltpu.CompilerParams(vmem_limit_bytes=40 << 20),
        cost_estimate=pl.CostEstimate(flops=2 * 64 * 512 * 5120, bytes_accessed=6 << 20, transcendentals=0),
        name="pick",
    )(hot, legendre)


def order_kernel(leg_ref, spec_ref, out_ref, raw, leg, specs, full):
    half = NLAT // 2
    for i in range(LATS):
        for h in range(STEPS // LANES):
            lanes = slice(h * LANES, (h + 1) * LANES)
            raw[h, pl.ds(i * SUB * ROWS, SUB * ROWS), :] = leg_ref[i, :, lanes].astype(F32)
    for h in range(STEPS // LANES):
        lanes = slice(h * LANES, (h + 1) * LANES)
        specs[h] = spec_ref[:, :, lanes].reshape(CHS * C, LANES).astype(F32)
    for i in range(LATS):
        for t in range(SUB):
            for h in range(STEPS // LANES):
                leg[t, h, pl.ds(i * ROWS, ROWS), :] = raw[h, pl.ds((i * SUB + t) * ROWS, ROWS), :]
    rows = lax.broadcasted_iota(jnp.int32, (LANES, LANES), 0)
    cols = lax.broadcasted_iota(jnp.int32, (LANES, LANES), 1)
    turn = jnp.where(rows + cols == LANES - 1, 1.0, 0.0).astype(BF)
    stride = 4
    full[...] = jnp.zeros_like(full)
    for t in range(SUB):
        table = jnp.concatenate([leg[t, h] for h in range(STEPS // LANES)], axis=1).astype(BF)
        count = NLAT // LANES
        turned = jnp.concatenate(
            [
                jnp.dot(
                    turn,
                    table[(count - 1 - n) * LANES : (count - n) * LANES],
                    preferred_element_type=F32,
                ).astype(BF)
                for n in range(count)
            ],
            axis=0,
        )
        coeffs = []
        for p in range(2):
            pieces = []
            for x in range(2):
                for j in range(CHS):
                    start = j * C + t * 4 * OWN + p * 2 + x
                    pieces.append(
                        jnp.concatenate(
                            [
                                specs[h, pl.ds(start, OWN, stride=stride), :]
                                for h in range(STEPS // LANES)
                            ],
                            axis=1,
                        )
                    )
            coeffs.append(jnp.concatenate(pieces, axis=0).astype(BF))

        def dot(a, b):
            return lax.dot_general(a, b, NT, preferred_element_type=F32)

        full[t, pl.ds(8, half), :] = dot(table[:half], coeffs[0]) - dot(turned[:half], coeffs[1])
        full[t, pl.ds(8 + half, half), :] = dot(table[half:], coeffs[1]) + dot(turned[half:], coeffs[0])
    for i in range(LATS):
        start = 8 - REACH + i * ROWS
        block = [full[t, pl.ds(start, HALO_ROWS), :] for t in range(SUB)]
        out_ref[i] = jnp.concatenate(block, axis=0).astype(BF)


def order_stage(leg, spec):
    return pl.pallas_call(
        order_kernel,
        out_shape=jax.ShapeDtypeStruct((LATS, SUB * HALO_ROWS, LANES), BF),
        in_specs=[pl.BlockSpec(memory_space=VMEM)] * 2,
        out_specs=pl.BlockSpec(memory_space=VMEM),
        scratch_shapes=[
            pltpu.VMEM((STEPS // LANES, LATS * SUB * ROWS, LANES), F32),
            pltpu.VMEM((SUB, STEPS // LANES, NLAT, LANES), F32),
            pltpu.VMEM((STEPS // LANES, CHS * C, LANES), F32),
            pltpu.VMEM((SUB, NLAT + 16, LANES), F32),
        ],
        compiler_params=pltpu.CompilerParams(vmem_limit_bytes=40 << 20),
        cost_estimate=pl.CostEstimate(flops=700 << 20, bytes_accessed=2 << 20, transcendentals=0),
        name="order_stage",
    )(leg, spec)


def row_kernel(slots_ref, rows_ref, coef_ref, mix_ref, out_ref, field, plain, crossed, wide):
    for i in range(LATS):
        block = slots_ref[i]
        start = pl.multiple_of(block * (SUB * HALO_ROWS), 8)
        field[pl.ds(start, SUB * HALO_ROWS), :] = rows_ref[i].astype(F32)
    low = lax.broadcasted_iota(jnp.int32, (C, LANES), 1) < PICKS
    for r in range(HALO_ROWS):
        one = field[pl.ds(r, PICKS, stride=HALO_ROWS), :]
        both = jnp.concatenate([one, one], axis=0).T
        plain[r] = jnp.where(low, both[:C], both[C:])
        crossed[r] = jnp.where(low, both[C:], both[:C])
    for r in range(ROWS):
        tops, rests = [], []
        for b in range(KER):
            total = None
            for d in range(SPREAD):
                row = (r * KER + b) * SPREAD + d
                term = coef_ref[0, row : row + 1, :] * plain[r + d] + coef_ref[1, row : row + 1, :] * crossed[r + d]
                total = term if total is None else total + term
            top = total.astype(BF)
            tops.append(top)
            rests.append((total - top.astype(F32)).astype(BF))
        both = jnp.concatenate(tops + rests, axis=0)
        mixed = jnp.dot(mix_ref[...], both, preferred_element_type=F32)
        wide[pl.ds(r, C, stride=ROWS), :] = mixed
    out_ref[...] = wide[...].astype(BF).reshape(CHS, OWN * ROWS, LANES)


def row_stage(block_slots, rows, coefs, mix):
    return pl.pallas_call(
        row_kernel,
        out_shape=jax.ShapeDtypeStruct((CHS, OWN * ROWS, LANES), BF),
        in_specs=[pl.BlockSpec(memory_space=pltpu.SMEM)] + [pl.BlockSpec(memory_space=VMEM)] * 3,
        out_specs=pl.BlockSpec(memory_space=VMEM),
        scratch_shapes=[
            pltpu.VMEM((BLOCKS * SUB * HALO_ROWS, LANES), F32),
            pltpu.VMEM((HALO_ROWS, C, LANES), F32),
            pltpu.VMEM((HALO_ROWS, C, LANES), F32),
            pltpu.VMEM((C * ROWS, LANES), F32),
        ],
        compiler_params=pltpu.CompilerParams(vmem_limit_bytes=40 << 20),
        cost_estimate=pl.CostEstimate(flops=200 << 20, bytes_accessed=2 << 20, transcendentals=0),
        name="row_stage",
    )(block_slots, rows, coefs, mix)


def longitude_kernel(rows_ref, table_ref, out_ref, wide):
    lhs = jnp.concatenate([rows_ref[j] for j in range(CHS)], axis=1)
    wide[...] = jnp.dot(lhs, table_ref[...], preferred_element_type=F32)
    for o in range(OWN):
        out_ref[o] = wide[pl.ds(o * ROWS, ROWS), :].astype(BF)


def longitude_stage(rows, table):
    return pl.pallas_call(
        longitude_kernel,
        out_shape=jax.ShapeDtypeStruct((OWN, ROWS, NLON), BF),
        in_specs=[pl.BlockSpec(memory_space=VMEM)] * 2,
        out_specs=pl.BlockSpec(memory_space=VMEM),
        scratch_shapes=[pltpu.VMEM((OWN * ROWS, NLON), F32)],
        compiler_params=pltpu.CompilerParams(vmem_limit_bytes=40 << 20),
        cost_estimate=pl.CostEstimate(flops=480 << 20, bytes_accessed=4 << 20, transcendentals=0),
        name="longitude_stage",
    )(rows, table)


def stencil_coefs(kernel_values, near_rows, lat_index, ch_index):
    own_rows = lat_index * ROWS + jnp.arange(ROWS, dtype=jnp.int32)
    step = near_rows - own_rows[:, None] + REACH
    hit = (step[:, :, None] == jnp.arange(SPREAD, dtype=jnp.int32)).astype(F32)
    taps = jnp.sum(
        hit[None, :, :, :, None] * kernel_values.astype(F32)[:, :, :, None, :], axis=2
    )
    taps = jnp.transpose(taps, (1, 0, 2, 3)).reshape(ROWS * KER * SPREAD, TAPS)
    lane = jnp.arange(LANES, dtype=jnp.int32)
    orders = (lane % PICKS) // SUB * ORDER_BLOCK + lane % SUB + SUB * ch_index
    phases = (orders[None, :] * (jnp.arange(TAPS, dtype=jnp.int32) - LON_REACH)[:, None]) % NLON
    angles = phases.astype(F32) * (2.0 * math.pi / NLON)
    side = jnp.where(lane < PICKS, -1.0, 1.0).astype(F32)
    waves = jnp.stack([jnp.cos(angles), side * jnp.sin(angles)])
    return jnp.einsum("ns,xsl->xnl", taps, waves, precision=lax.Precision.HIGHEST)


def per_device(spectrum, legendre, block_slots, kernel_values, near_rows, mix_weights):
    lat_index = lax.axis_index("lat")
    ch_index = lax.axis_index("ch")
    wanted = (
        block_slots[:, None] * ORDER_BLOCK + SUB * ch_index + jnp.arange(SUB, dtype=jnp.int32)
    ).reshape(PICKS, 1)
    hot = (wanted == jnp.arange(LMAX, dtype=jnp.int32)).astype(BF)
    picked = pick(hot, legendre)
    leg = lax.all_to_all(picked, "lat", 0, 0, tiled=True)
    spec = lax.all_to_all(spectrum.reshape(CHS, C, STEPS), "ch", 0, 0, tiled=True)
    by_order = order_stage(leg, spec)
    by_row = lax.all_to_all(by_order, "lat", 0, 0, tiled=True)
    coefs = stencil_coefs(kernel_values, near_rows, lat_index, ch_index)
    mix = jnp.transpose(mix_weights, (2, 0, 1)).reshape(C, KER * C)
    mixed = row_stage(block_slots, by_row, coefs, jnp.concatenate([mix, mix], axis=1))
    own = lax.all_to_all(mixed, "ch", 0, 0, tiled=True)
    return longitude_stage(own, jnp.asarray(longitude_table()))


def solution(mesh):
    return jax.shard_map(
        per_device,
        mesh=mesh,
        in_specs=(
            P("lat", "ch", None, None, None),
            P("lat", None, None),
            P(),
            P(None, "lat", None, None),
            P("lat", None),
            P(),
        ),
        out_specs=P("ch", "lat", None),
        check_vma=False,
    )
```

time: 499 us -> 90.9 us (0.18); the launches traced: 489 us -> 90.1 us
  waiting for transfers between devices: 180 us -> 27.1 us
  other arithmetic: 113 us -> 4.26 us
  local copies, waits for them, and re-layouts: 97.3 us -> 12.7 us
  matrix products: 70.3 us -> 2.02 us
  blocking collectives: 0 us -> 15.4 us
  between operations: 14.2 us -> 0.13 us
  Pallas kernels: 0 us -> 8.02 us
  starting transfers between devices: 14.2 us -> 20.5 us
    reduce_scatter x1 -> x0, waiting for transfers between devices: 115 us -> none  [per_device(): lax.psum_scatter(jnp.einsum('kcd,kicx->dix', weight_cols, spread, precisi...]
    dot_general x12 -> x1, matrix products: 70.3 us -> 2.02 us  [stencil_coefs(): jnp.einsum('ns,xsl->xnl', taps, waves, precision=lax.Precision.HIGHEST)]
    scatter-add x1 -> x0, other arithmetic: 61.8 us -> none  [per_device(): partial_sum = zero_sum.at[:, :, :, order_ids].add(contribution)]
    unnamed x40 -> x18, local copies, waits for them, and re-layouts: 48.5 us -> 5.85 us
    all_gather x1 -> x0, waiting for transfers between devices: 38 us -> none  [per_device(): lax.all_gather(spectrum, 'lat', axis=0, tiled=True)]
    and x2 -> x0, other arithmetic: 16.1 us -> none  [the longest x1 16.1 us: per_device(): columns = jnp.take(legendre, order_ids, axis=2)]
    all_to_all x0 -> x1, blocking collectives: none -> 15.4 us  [per_device(): own = lax.all_to_all(mixed, 'ch', 0, 0, tiled=True)]
    slice x10 -> x0, local copies, waits for them, and re-layouts: 14.6 us -> none  [the longest x8 14 us: per_device(): rolled = jnp.roll(gathered, LON_REACH - offset, axis=3)]
  transfers between devices with their start and end apart: 6 -> 3, of which waited for: 4 -> 2; matrix products, arithmetic and copies ran while one was open for 12% -> 12% of each run, Pallas kernels for 0% -> 3%
where the time goes in v1:
time: 90.9 us; the launch traced here: 90.1 us
  waiting for transfers between devices  27.1 us (30%)
  starting transfers between devices  20.5 us (23%)
  blocking collectives  15.4 us (17%)
  local copies, waits for them, and re-layouts  12.7 us (14%)
  Pallas kernels  8.02 us (9%)
  other arithmetic  4.26 us (5%)
  matrix products  2.02 us (2%)
    all_to_all x1, blocking collectives, per_device(): own = lax.all_to_all(mixed, 'ch', 0, 0, tiled=True)  15.4 us
    all_to_all x1, waiting for transfers between devices, per_device(): leg = lax.all_to_all(picked, 'lat', 0, 0, tiled=True)  14.9 us
    all_to_all x1, waiting for transfers between devices, per_device(): by_row = lax.all_to_all(by_order, 'lat', 0, 0, tiled=True)  12.2 us
    all_to_all x1, starting transfers between devices, per_device(): leg = lax.all_to_all(picked, 'lat', 0, 0, tiled=True)  9.26 us
    all_to_all x1, starting transfers between devices, per_device(): lax.all_to_all(spectrum.reshape(CHS, C, STEPS), 'ch', 0, 0, tiled=True)  7.38 us
    unnamed x18, local copies, waits for them, and re-layouts  5.85 us
    all_to_all x1, starting transfers between devices, per_device(): by_row = lax.all_to_all(by_order, 'lat', 0, 0, tiled=True)  3.88 us
    pallas_call x1, Pallas kernels, pick(): pl.pallas_call(pick_kernel, out_shape=jax.ShapeDtypeStruct((LATS, SUB * R...  2.68 us
  transfers between devices with their start and end apart: 3, of which 2 were waited for; matrix products, arithmetic and copies ran while one was open for 12% of the time, Pallas kernels for 3%

profile of v1, /device:TPU:8, one launch (start us, length us, event | category | flops | bytes accessed | tf_op | source)
XLA Modules:
  0.0 90.1 jit_solution(3148920987210343107)
XLA Ops:
  0.0 1.8 %reshape.217 = bf16[8,64,256]{2,1,0:T(8,128)(2,1)} reshape(bf16[16,8,2,2,256]{4,3,2,1,0:T(2,128)(2,1)} %param.7) | data formatting | bytes 524288 | tf_op jit(solution)/shard_map/reshape | solution.py:259
  1.8 7.4 %all-to-all-start.1 = ((bf16[8,64,256]{2,1,0:T(8,128)(2,1)}), bf16[8,64,256]{2,1,0:T(8,128)(2,1)S(1)}, u32[]{:S(2)}, u32[]{:S(2)}) async-start(bf16[8,64,256]{2,1,0:T(8,128)(2,1)} %reshape.217), calls=%async_computation.1 | async-start | bytes 524288 | tf_op jit(solution)/shard_map/all_to_all | solution.py:259
  9.1 0.7 multiply_add_fusion
  10.1 2.5 %copy-done = bf16[20,256,512]{2,1,0:T(8,128)(2,1)S(1)} copy-done((bf16[20,256,512]{2,1,0:T(8,128)(2,1)S(1)}, bf16[20,256,512]{2,1,0:T(8,128)(2,1)}, u32[]{:S(2)}) %copy-start) | copy-done | bytes 5242904
  12.6 2.7 %pick.1 = bf16[32,40,256]{2,1,0:T(8,128)(2,1)S(1)} custom-call(bf16[64,512]{1,0:T(8,128)(2,1)S(1)} %fusion.hot_ref, bf16[20,256,512]{2,1,0:T(8,128)(2,1)S(1)} %copy-done), custom_call_target="tpu_custom_call" | custom-call | flops 335544320 | bytes 6291456 | tf_op jit(solution)/shard_map/pick/pallas_call | solution.py:73
  15.3 0.8 copy-done.2
  16.2 9.3 %all-to-all-start = ((bf16[32,40,256]{2,1,0:T(8,128)(2,1)}), bf16[32,40,256]{2,1,0:T(8,128)(2,1)}, u32[]{:S(2)}, u32[]{:S(2)}) async-start(bf16[32,40,256]{2,1,0:T(8,128)(2,1)} %copy-done.2), calls=%async_computation | async-start | bytes 1310720 | tf_op jit(solution)/shard_map/all_to_all | solution.py:258
  26.1 1.1 %multiply_reduce_fusion = f32[3,20,5,9]{1,3,2,0:T(8,128)S(1)} fusion(f32[3,20,6,9]{1,2,3,0:T(8,128)} %convert_element_type.30, f32[20,6,5]{0,1,2:T(8,128)S(1)} %fusion.1), kind=kLoop, calls=%fused_computation.1 | loop fusion | flops 29700 | bytes 26160 | tf_op jit(solution)/shard_map/reduce_sum | solution.py:237
  27.2 0.9 %copy.18 = f32[20,3,5,9]{3,2,1,0:T(8,128)} copy(f32[20,3,5,9]{0,3,2,1:T(8,128)S(1)} %bitcast.7) | data formatting | bytes 21600 | tf_op jit(solution)/shard_map/transpose | solution.py:240
  28.2 1.6 %reshape.223 = f32[300,9,1]{1,0,2:T(8,128)} reshape(f32[20,3,5,9]{3,2,1,0:T(8,128)} %copy.18) | data formatting | bytes 21600 | tf_op jit(solution)/shard_map/reshape | solution.py:240
  29.8 1.5 %copy.20 = bf16[64,192]{1,0:T(8,128)(2,1)} copy(bf16[64,192]{0,1:T(8,128)(2,1)} %bitcast.8) | data formatting | bytes 49152 | tf_op jit(solution)/shard_map/reshape | solution.py:263
  31.3 14.9 %all-to-all-done.leg_ref = bf16[32,40,256]{2,1,0:T(8,128)(2,1)} async-done(((bf16[32,40,256]{2,1,0:T(8,128)(2,1)}), bf16[32,40,256]{2,1,0:T(8,128)(2,1)}, u32[]{:S(2)}, u32[]{:S(2)}) %all-to-all-start) | async-done | bytes 655392 | tf_op jit(solution)/shard_map/all_to_all | solution.py:258
  46.2 2.0 %order_stage.1 = bf16[32,48,128]{2,1,0:T(8,128)(2,1)S(1)} custom-call(bf16[32,40,256]{2,1,0:T(8,128)(2,1)} %all-to-all-done.leg_ref, bf16[8,64,256]{2,1,0:T(8,128)(2,1)S(1)} %all-to-all-done.1.spec_ref), custom_call_target="tpu_custom_call" | custom-call | flops 734003200 | bytes 2097152 | tf_op jit(solution)/shard_map/order_stage/pallas_call | solution.py:150
  48.2 0.7 copy-done.4
  48.9 3.9 %all-to-all-start.2 = ((bf16[32,48,128]{2,1,0:T(8,128)(2,1)}), bf16[32,48,128]{2,1,0:T(8,128)(2,1)S(1)}, u32[]{:S(2)}, u32[]{:S(2)}) async-start(bf16[32,48,128]{2,1,0:T(8,128)(2,1)} %copy-done.4), calls=%async_computation.2 | async-start | bytes 786432 | tf_op jit(solution)/shard_map/all_to_all | solution.py:261
  52.8 1.5 %pad_maximum_fusion.mix_ref = bf16[64,384]{1,0:T(8,128)(2,1)} fusion(bf16[64,192]{1,0:T(8,128)(2,1)} %copy.20), kind=kLoop, calls=%fused_computation.4 | loop fusion | flops 98304 | bytes 73728 | tf_op jit(solution)/shard_map/concatenate | solution.py:264
  54.5 2.0 %convolution_bitcast_fusion.coef_ref = f32[2,300,128]{2,1,0:T(8,128)} fusion(f32[300,9,1]{1,0,2:T(8,128)} %reshape.223, f32[1,9,128]{2,1,0:T(8,128)S(1)} %get-tuple-element.6, f32[1,9,128]{2,1,0:T(8,128)S(1)} %get-tuple-element.5), kind=kOutput, calls=%fused_computation | convolution fusion | flops 8296704 | bytes 327216 | tf_op jit(solution)/shard_map/ns,xsl->xnl/dot_general | solution.py:247
  56.5 12.2 %all-to-all-done.2.rows_ref = bf16[32,48,128]{2,1,0:T(8,128)(2,1)S(1)} async-done(((bf16[32,48,128]{2,1,0:T(8,128)(2,1)}), bf16[32,48,128]{2,1,0:T(8,128)(2,1)S(1)}, u32[]{:S(2)}, u32[]{:S(2)}) %all-to-all-start.2) | async-done | bytes 393248 | tf_op jit(solution)/shard_map/all_to_all | solution.py:261
  68.7 1.0 %copy-done.3 = f32[2,300,128]{2,1,0:T(8,128)S(1)} copy-done((f32[2,300,128]{2,1,0:T(8,128)S(1)}, f32[2,300,128]{2,1,0:T(8,128)}, u32[]{:S(2)}) %copy-start.3) | copy-done | bytes 307224
  69.7 0.8 copy-done.5
  70.5 2.6 %row_stage.1 = bf16[8,160,128]{2,1,0:T(8,128)(2,1)S(1)} custom-call(s32[32]{0:T(128)S(1)} %copy-done.6, bf16[32,48,128]{2,1,0:T(8,128)(2,1)S(1)} %all-to-all-done.2.rows_ref, f32[2,300,128]{2,1,0:T(8,128)S(1)} %copy-done.3, bf16[64,384]{1,0:T(8,128)(2,1)S(1)} %copy-done.5), custom_call_target="tpu_custom_call" | custom-call | flops 209715200 | bytes 2097152 | tf_op jit(solution)/shard_map/row_stage/pallas_call | solution.py:196
  73.1 15.4 %all_to_all.20.rows_ref = bf16[8,160,128]{2,1,0:T(8,128)(2,1)S(1)} all-to-all(bf16[8,160,128]{2,1,0:T(8,128)(2,1)S(1)} %row_stage.1), channel_id=1, replica_groups=mesh['lat'=32,'ch'=8] {'ch'}, dimensions={0} | all-to-all | bytes 655360 | tf_op jit(solution)/shard_map/all_to_all | solution.py:265
  88.5 0.7 longitude_stage.1
  89.2 0.9 %copy.22 = bf16[8,20,1440]{2,0,1:T(8,128)(2,1)} copy(bf16[8,20,1440]{2,1,0:T(8,128)(2,1)S(1)} %longitude_stage.1) | data formatting | bytes 921600 | tf_op jit(solution)/shard_map/longitude_stage/pallas_call | solution.py:221
  (25 shorter events, 1.2 us)
Async XLA Ops:
  0.0 25.4 %copy-start.7 = (bf16[3,20,6,9]{1,2,3,0:T(8,128)(2,1)S(1)}, bf16[3,20,6,9]{1,2,3,0:T(8,128)(2,1)}, u32[]{:S(2)}) copy-start(bf16[3,20,6,9]{1,2,3,0:T(8,128)(2,1)} %param.10) | copy-start | bytes 19444
  0.0 26.1 %copy-start.8 = (s32[20,6]{0,1:T(8,128)S(1)}, s32[20,6]{0,1:T(8,128)}, u32[]{:S(2)}) copy-start(s32[20,6]{0,1:T(8,128)} %param.11) | copy-start | bytes 1444
  1.8 14.4 %all-to-all-start.1 = ((bf16[8,64,256]{2,1,0:T(8,128)(2,1)}), bf16[8,64,256]{2,1,0:T(8,128)(2,1)S(1)}, u32[]{:S(2)}, u32[]{:S(2)}) async-start(bf16[8,64,256]{2,1,0:T(8,128)(2,1)} %reshape.217), calls=%async_computation.1 | async-start | bytes 524288 | tf_op jit(solution)/shard_map/all_to_all | solution.py:259
  10.1 2.5 %copy-start = (bf16[20,256,512]{2,1,0:T(8,128)(2,1)S(1)}, bf16[20,256,512]{2,1,0:T(8,128)(2,1)}, u32[]{:S(2)}) copy-start(bf16[20,256,512]{2,1,0:T(8,128)(2,1)} %leg_ref.1) | copy-start | bytes 15728644
  12.6 56.1 %copy-start.6 = (s32[32]{0:T(128)S(1)}, s32[32]{0:T(128)}, u32[]{:S(2)}) copy-start(s32[32]{0:T(128)} %slots_ref.1) | copy-start | bytes 388
  15.3 0.9 copy-start.2
  16.1 72.4 %copy-start.1 = (bf16[1024,1440]{1,0:T(8,128)(2,1)S(1)}, bf16[1024,1440]{1,0:T(8,128)(2,1)}, u32[]{:S(2)}) copy-start(bf16[1024,1440]{1,0:T(8,128)(2,1)} %constant.79.clone.table_ref) | copy-start | bytes 8847364
  16.2 30.0 %all-to-all-start = ((bf16[32,40,256]{2,1,0:T(8,128)(2,1)}), bf16[32,40,256]{2,1,0:T(8,128)(2,1)}, u32[]{:S(2)}, u32[]{:S(2)}) async-start(bf16[32,40,256]{2,1,0:T(8,128)(2,1)} %copy-done.2), calls=%async_computation | async-start | bytes 1310720 | tf_op jit(solution)/shard_map/all_to_all | solution.py:258
  48.2 0.7 copy-start.4
  48.9 19.8 %all-to-all-start.2 = ((bf16[32,48,128]{2,1,0:T(8,128)(2,1)}), bf16[32,48,128]{2,1,0:T(8,128)(2,1)S(1)}, u32[]{:S(2)}, u32[]{:S(2)}) async-start(bf16[32,48,128]{2,1,0:T(8,128)(2,1)} %copy-done.4), calls=%async_computation.2 | async-start | bytes 786432 | tf_op jit(solution)/shard_map/all_to_all | solution.py:261
  68.7 1.0 %copy-start.3 = (f32[2,300,128]{2,1,0:T(8,128)S(1)}, f32[2,300,128]{2,1,0:T(8,128)}, u32[]{:S(2)}) copy-start(f32[2,300,128]{2,1,0:T(8,128)} %convolution_bitcast_fusion.coef_ref) | copy-start | bytes 921604
  69.7 0.8 copy-start.5

commit v2 on v1

v2 whole, which is shorter than its diff:
```python
import math

import jax
import jax.numpy as jnp
import ml_dtypes
import numpy as np
from jax import lax
from jax.experimental import pallas as pl
from jax.experimental.pallas import tpu as pltpu
from jax.sharding import PartitionSpec as P

NLAT = 640
NLON = 1440
LMAX = 512
C = 64
ORDER_BLOCK = 16
KER = 3
SLOTS = 6
REACH = 2
LON_REACH = 4
TAPS = 9
STEPS = 256
BLOCKS = 32
LATS = 32
CHS = 8
ROWS = NLAT // LATS
OWN = C // CHS
SUB = ORDER_BLOCK // CHS
HALO_ROWS = ROWS + 2 * REACH
SPREAD = 2 * REACH + 1
PICKS = LATS * SUB
LANES = 128
BF = jnp.bfloat16
F32 = jnp.float32
NT = (((1,), (1,)), ((), ()))
TN = (((0,), (0,)), ((), ()))
VMEM = pltpu.VMEM
GRANT = 60 << 20
PAIR = 2
TURNS = CHS // PAIR
LAT_CHUNK = 8


HALF_LON = NLON // 2
WAVE_ROWS = 16


def order_table():
    orders = (
        ORDER_BLOCK * np.arange(BLOCKS)[None, :, None]
        + SUB * np.arange(CHS)[:, None, None]
        + np.arange(SUB)[None, None, :]
    )
    return orders.reshape(CHS, 1, PICKS, 1)


def longitude_table():
    orders = order_table()
    phases = (orders * np.arange(HALF_LON)) % NLON
    angles = phases * (2.0 * math.pi / NLON)
    weight = np.where(orders == 0, 1.0, 2.0)
    table = np.concatenate([weight * np.cos(angles), -weight * np.sin(angles)], axis=1)
    return table.reshape(CHS * LANES, HALF_LON).astype(ml_dtypes.bfloat16)


def wave_table():
    shifts = np.arange(TAPS)[:, None] - LON_REACH
    orders = order_table().reshape(CHS, 1, PICKS)
    angles = ((orders * shifts) % NLON) * (2.0 * math.pi / NLON)
    waves = np.zeros((CHS, WAVE_ROWS, 2 * LANES), np.float32)
    cosine, sine = np.cos(angles), np.sin(angles)
    waves[:, :TAPS] = np.concatenate([cosine, cosine, -sine, sine], axis=2)
    return waves


PICK_ROWS = 2
PICK_AHEAD = 4


def pick_kernel(slots_ref, leg_ref, out_ref, buf, wide, flat, sems, out_sem):
    copies = []
    for g in range(ROWS // PICK_ROWS):
        rows = pl.ds(g * PICK_ROWS, PICK_ROWS)
        copies.append(pltpu.make_async_copy(leg_ref.at[rows], buf.at[rows], sems.at[g]))
    for copy in copies[:PICK_AHEAD]:
        copy.start()
    lines = lax.broadcasted_iota(jnp.int32, (PICKS, LMAX), 0)
    orders = lax.broadcasted_iota(jnp.int32, (PICKS, LMAX), 1)
    blocks = jnp.zeros((PICKS, LMAX), jnp.int32)
    for i in range(LATS):
        blocks = jnp.where(lines // SUB == i, slots_ref[i], blocks)
    wanted = blocks * ORDER_BLOCK + lines % SUB + SUB * lax.axis_index("ch")
    hot = jnp.where(orders == wanted, 1.0, 0.0).astype(BF)
    for r in range(ROWS):
        if r % PICK_ROWS == 0:
            copies[r // PICK_ROWS].wait()
            for copy in copies[r // PICK_ROWS + PICK_AHEAD :][:1]:
                copy.start()
        picked = lax.dot_general(hot, buf[r], NT, preferred_element_type=F32)
        for h in range(STEPS // LANES):
            wide[h, pl.ds(r, PICKS, stride=ROWS), :] = picked[:, h * LANES : (h + 1) * LANES]
    for h in range(STEPS // LANES):
        half = wide[h].astype(BF)
        flat[:, :, h * LANES : (h + 1) * LANES] = half.reshape(LATS, SUB * ROWS, LANES)
    done = pltpu.make_async_copy(flat, out_ref, out_sem)
    done.start()
    done.wait()


def pick(block_slots, legendre):
    return pl.pallas_call(
        pick_kernel,
        out_shape=jax.ShapeDtypeStruct((LATS, SUB * ROWS, STEPS), BF),
        in_specs=[pl.BlockSpec(memory_space=pltpu.SMEM), pl.BlockSpec(memory_space=pltpu.HBM)],
        out_specs=pl.BlockSpec(memory_space=pltpu.HBM),
        scratch_shapes=[
            pltpu.VMEM((ROWS, STEPS, LMAX), BF),
            pltpu.VMEM((STEPS // LANES, PICKS * ROWS, LANES), F32),
            pltpu.VMEM((LATS, SUB * ROWS, STEPS), BF),
            pltpu.SemaphoreType.DMA((ROWS // PICK_ROWS,)),
            pltpu.SemaphoreType.DMA,
        ],
        compiler_params=pltpu.CompilerParams(vmem_limit_bytes=GRANT),
        cost_estimate=pl.CostEstimate(flops=2 * 64 * 512 * 5120, bytes_accessed=6 << 20, transcendentals=0),
        name="pick",
    )(block_slots, legendre)


def order_kernel(leg_ref, *refs):
    pieces_in, (out_ref, got, raw, leg, specs, full, send, sems) = refs[:TURNS], refs[TURNS:]
    half = NLAT // 2
    ch_index = lax.axis_index("ch")
    side = lax.rem(ch_index, PAIR)
    arrivals, departures = [], []
    for g in range(LATS // LAT_CHUNK):
        part = pl.ds(g * LAT_CHUNK, LAT_CHUNK)
        arrivals.append(pltpu.make_async_copy(leg_ref.at[part], got.at[part], sems.at[0, g]))
        arrivals[-1].start()
        departures.append(pltpu.make_async_copy(send.at[part], out_ref.at[part], sems.at[1, g]))
    for d in range(TURNS):
        turn = lax.rem(lax.div(ch_index, PAIR) + (TURNS - d), TURNS)
        for q in range(PAIR):
            source = turn * PAIR + (side if q == 0 else 1 - side)
            for h in range(STEPS // LANES):
                lanes = slice(h * LANES, (h + 1) * LANES)
                start = pl.multiple_of(source * C, C)
                specs[h, pl.ds(start, C), :] = pieces_in[d][q, :, lanes].astype(F32)
    for i in range(LATS):
        if i % LAT_CHUNK == 0:
            arrivals[i // LAT_CHUNK].wait()
        for h in range(STEPS // LANES):
            lanes = slice(h * LANES, (h + 1) * LANES)
            raw[h, pl.ds(i * SUB * ROWS, SUB * ROWS), :] = got[i, :, lanes].astype(F32)
    for i in range(LATS):
        for t in range(SUB):
            for h in range(STEPS // LANES):
                leg[t, h, pl.ds(i * ROWS, ROWS), :] = raw[h, pl.ds((i * SUB + t) * ROWS, ROWS), :]
    rows = lax.broadcasted_iota(jnp.int32, (LANES, LANES), 0)
    cols = lax.broadcasted_iota(jnp.int32, (LANES, LANES), 1)
    turn = jnp.where(rows + cols == LANES - 1, 1.0, 0.0).astype(BF)
    stride = 4
    full[...] = jnp.zeros_like(full)
    for t in range(SUB):
        table = jnp.concatenate([leg[t, h] for h in range(STEPS // LANES)], axis=1).astype(BF)
        count = NLAT // LANES
        turned = jnp.concatenate(
            [
                jnp.dot(
                    turn,
                    table[(count - 1 - n) * LANES : (count - n) * LANES],
                    preferred_element_type=F32,
                ).astype(BF)
                for n in range(count)
            ],
            axis=0,
        )
        coeffs = []
        for p in range(2):
            pieces = []
            for x in range(2):
                for j in range(CHS):
                    start = j * C + t * 4 * OWN + p * 2 + x
                    pieces.append(
                        jnp.concatenate(
                            [
                                specs[h, pl.ds(start, OWN, stride=stride), :]
                                for h in range(STEPS // LANES)
                            ],
                            axis=1,
                        )
                    )
            coeffs.append(jnp.concatenate(pieces, axis=0).astype(BF))

        def dot(a, b):
            return lax.dot_general(a, b, NT, preferred_element_type=F32)

        full[t, pl.ds(8, half), :] = dot(table[:half], coeffs[0]) - dot(turned[:half], coeffs[1])
        full[t, pl.ds(8 + half, half), :] = dot(table[half:], coeffs[1]) + dot(turned[half:], coeffs[0])
    for i in range(LATS):
        start = 8 - REACH + i * ROWS
        block = [full[t, pl.ds(start, HALO_ROWS), :] for t in range(SUB)]
        send[i] = jnp.concatenate(block, axis=0).astype(BF)
        if i % LAT_CHUNK == LAT_CHUNK - 1:
            departures[i // LAT_CHUNK].start()
    for copy in departures:
        copy.wait()


def order_stage(leg, pieces):
    return pl.pallas_call(
        order_kernel,
        out_shape=jax.ShapeDtypeStruct((LATS, SUB * HALO_ROWS, LANES), BF),
        in_specs=[pl.BlockSpec(memory_space=pltpu.HBM)] + [pl.BlockSpec(memory_space=VMEM)] * TURNS,
        out_specs=pl.BlockSpec(memory_space=pltpu.HBM),
        scratch_shapes=[
            pltpu.VMEM((LATS, SUB * ROWS, STEPS), BF),
            pltpu.VMEM((STEPS // LANES, LATS * SUB * ROWS, LANES), F32),
            pltpu.VMEM((SUB, STEPS // LANES, NLAT, LANES), F32),
            pltpu.VMEM((STEPS // LANES, CHS * C, LANES), F32),
            pltpu.VMEM((SUB, NLAT + 16, LANES), F32),
            pltpu.VMEM((LATS, SUB * HALO_ROWS, LANES), BF),
            pltpu.SemaphoreType.DMA((2, LATS // LAT_CHUNK)),
        ],
        compiler_params=pltpu.CompilerParams(vmem_limit_bytes=GRANT),
        cost_estimate=pl.CostEstimate(flops=700 << 20, bytes_accessed=2 << 20, transcendentals=0),
        name="order_stage",
    )(leg, *pieces)


def coef_kernel(values_ref, near_ref, mix_ref, waves_ref, coef_ref, mixed_ref, taps):
    first = lax.axis_index("lat") * ROWS
    step = near_ref[...] - lax.broadcasted_iota(jnp.int32, (SLOTS, ROWS), 1) - (first - REACH)
    taps[...] = jnp.zeros_like(taps)
    for d in range(SPREAD):
        hit = jnp.where(step == d, 1.0, 0.0)
        for b in range(KER):
            for s in range(TAPS):
                value = values_ref[b, s].astype(F32)
                taps[b * SPREAD + d, s : s + 1, :] = jnp.sum(hit * value, axis=0, keepdims=True)
    waves = waves_ref[lax.axis_index("ch")]
    for n in range(KER * SPREAD):
        coef_ref[n] = lax.dot_general(
            taps[n], waves, TN, precision=lax.Precision.HIGHEST, preferred_element_type=F32
        )
    turned = jnp.concatenate([mix_ref[b].astype(F32).T for b in range(KER)], axis=1)
    mixed_ref[...] = jnp.concatenate([turned, turned], axis=1).astype(BF)


def coef_stage(kernel_values, near_rows, mix_weights):
    return pl.pallas_call(
        coef_kernel,
        out_shape=(
            jax.ShapeDtypeStruct((KER * SPREAD, ROWS, 2 * LANES), F32),
            jax.ShapeDtypeStruct((C, 2 * KER * C), BF),
        ),
        in_specs=[pl.BlockSpec(memory_space=VMEM)] * 4,
        out_specs=[pl.BlockSpec(memory_space=VMEM)] * 2,
        scratch_shapes=[pltpu.VMEM((KER * SPREAD, WAVE_ROWS, ROWS), F32)],
        compiler_params=pltpu.CompilerParams(vmem_limit_bytes=16 << 20),
        cost_estimate=pl.CostEstimate(flops=16 << 20, bytes_accessed=1 << 20, transcendentals=0),
        name="coef_stage",
    )(
        jnp.transpose(kernel_values, (0, 3, 2, 1)),
        jnp.transpose(near_rows, (1, 0)),
        mix_weights,
        jnp.asarray(wave_table()),
    )


def row_kernel(slots_ref, rows_ref, coef_ref, mix_ref, out_ref, field, plain, crossed):
    for i in range(LATS):
        block = slots_ref[i]
        start = pl.multiple_of(block * (SUB * HALO_ROWS), 8)
        field[pl.ds(start, SUB * HALO_ROWS), :] = rows_ref[i].astype(F32)
    low = lax.broadcasted_iota(jnp.int32, (C, LANES), 1) < PICKS
    for r in range(HALO_ROWS):
        one = field[pl.ds(r, PICKS, stride=HALO_ROWS), :]
        both = jnp.concatenate([one, one], axis=0).T
        plain[r] = jnp.where(low, both[:C], both[C:])
        crossed[r] = jnp.where(low, both[C:], both[:C])
    for r in range(ROWS):
        tops, rests = [], []
        for b in range(KER):
            total = None
            for d in range(SPREAD):
                n = b * SPREAD + d
                term = coef_ref[n, r : r + 1, :LANES] * plain[r + d]
                term = term + coef_ref[n, r : r + 1, LANES:] * crossed[r + d]
                total = term if total is None else total + term
            top = total.astype(BF)
            tops.append(top)
            rests.append((total - top.astype(F32)).astype(BF))
        both = jnp.concatenate(tops + rests, axis=0)
        mixed = jnp.dot(mix_ref[...], both, preferred_element_type=F32)
        out_ref[:, r * OWN : (r + 1) * OWN, :] = mixed.astype(BF).reshape(CHS, OWN, LANES)


def row_stage(block_slots, rows, coefs, mix):
    return pl.pallas_call(
        row_kernel,
        out_shape=jax.ShapeDtypeStruct((CHS, OWN * ROWS, LANES), BF),
        in_specs=[
            pl.BlockSpec(memory_space=pltpu.SMEM),
            pl.BlockSpec(memory_space=VMEM),
            pl.BlockSpec(memory_space=VMEM),
            pl.BlockSpec(memory_space=VMEM),
        ],
        out_specs=pl.BlockSpec(memory_space=VMEM),
        scratch_shapes=[
            pltpu.VMEM((BLOCKS * SUB * HALO_ROWS, LANES), F32),
            pltpu.VMEM((HALO_ROWS, C, LANES), F32),
            pltpu.VMEM((HALO_ROWS, C, LANES), F32),
        ],
        compiler_params=pltpu.CompilerParams(vmem_limit_bytes=16 << 20),
        cost_estimate=pl.CostEstimate(flops=200 << 20, bytes_accessed=2 << 20, transcendentals=0),
        name="row_stage",
    )(block_slots, rows, coefs, mix)


def longitude_kernel(rows_ref, table_ref, out_ref):
    even = jnp.concatenate([rows_ref[j] for j in range(CHS)], axis=1)
    lane = lax.broadcasted_iota(jnp.int32, even.shape, 1)
    flipped = jnp.where(lane % SUB == 0, even.astype(F32), -even.astype(F32)).astype(BF)
    both = jnp.concatenate([even, flipped], axis=0)
    field = jnp.dot(both, table_ref[...], preferred_element_type=F32)
    count = OWN * ROWS
    whole = jnp.concatenate([field[:count], field[count:]], axis=1)
    out_ref[...] = whole.astype(BF).reshape(ROWS, OWN, NLON)


def longitude_stage(rows, table):
    return pl.pallas_call(
        longitude_kernel,
        out_shape=jax.ShapeDtypeStruct((ROWS, OWN, NLON), BF),
        in_specs=[pl.BlockSpec(memory_space=VMEM)] * 2,
        out_specs=pl.BlockSpec(memory_space=VMEM),
        compiler_params=pltpu.CompilerParams(vmem_limit_bytes=40 << 20),
        cost_estimate=pl.CostEstimate(flops=480 << 20, bytes_accessed=4 << 20, transcendentals=0),
        name="longitude_stage",
    )(rows, table)


def per_device(spectrum, legendre, block_slots, kernel_values, near_rows, mix_weights):
    ch_index = lax.axis_index("ch")
    picked = pick(block_slots, legendre)
    picked, spectrum = lax.optimization_barrier((picked, spectrum))
    leg = lax.all_to_all(picked, "lat", 0, 0, tiled=True)
    blocks = spectrum.reshape(TURNS, PAIR, C, STEPS)
    turn, side = ch_index // PAIR, ch_index % PAIR
    kept = lax.dynamic_index_in_dim(blocks, side, 1, keepdims=False)
    given = lax.dynamic_index_in_dim(blocks, 1 - side, 1, keepdims=False)
    taken = lax.ppermute(given, "ch", [(j, j ^ 1) for j in range(CHS)])
    both = jnp.stack([kept, taken], axis=1)
    pieces = []
    for d in range(TURNS):
        piece = lax.dynamic_index_in_dim(both, (turn + d) % TURNS, 0, keepdims=False)
        shift = [(j, (j + PAIR * d) % CHS) for j in range(CHS)]
        pieces.append(lax.ppermute(piece, "ch", shift) if d else piece)
    by_order = order_stage(leg, pieces)
    by_order, kernel_values, near_rows, mix_weights = lax.optimization_barrier(
        (by_order, kernel_values, near_rows, mix_weights)
    )
    by_row = lax.all_to_all(by_order, "lat", 0, 0, tiled=True)
    coefs, mix = coef_stage(kernel_values, near_rows, mix_weights)
    mixed = row_stage(block_slots, by_row, coefs, mix)
    own = lax.all_to_all(mixed, "ch", 0, 0, tiled=True)
    field = longitude_stage(own, jnp.asarray(longitude_table()))
    return jnp.transpose(field, (1, 0, 2))


def solution(mesh):
    return jax.shard_map(
        per_device,
        mesh=mesh,
        in_specs=(
            P("lat", "ch", None, None, None),
            P("lat", None, None),
            P(),
            P(None, "lat", None, None),
            P("lat", None),
            P(),
        ),
        out_specs=P("ch", "lat", None),
        check_vma=False,
    )
```

time: 90.9 us -> 82.4 us (0.906)
  local copies, waits for them, and re-layouts: 12.7 us -> 1.02 us
  Pallas kernels: 8.02 us -> 14 us
  other arithmetic: 4.26 us -> 0.64 us
  starting transfers between devices: 20.5 us -> 23.7 us
  matrix products: 2.02 us -> 0 us
    all_to_all x1, waiting for transfers between devices: 14.9 us -> 3.23 us  [per_device(): leg = lax.all_to_all(picked, 'lat', 0, 0, tiled=True)]
    ppermute x0 -> x4, waiting for transfers between devices: none -> 8.96 us  [the longest x1 6.4 us: per_device(): taken = lax.ppermute(given, 'ch', [(j, j ^ 1) for j in range(CHS)])]
    ppermute x0 -> x4, starting transfers between devices: none -> 7.74 us  [the longest x3 4.92 us: per_device(): pieces.append(lax.ppermute(piece, 'ch', shift) if d else piece)]
    all_to_all x1 -> x0, starting transfers between devices: 7.38 us -> none  [per_device(): lax.all_to_all(spectrum.reshape(CHS, C, STEPS), 'ch', 0, 0, tiled=True)]
    unnamed x18 -> x22, local copies, waits for them, and re-layouts: 5.85 us -> 0.89 us
    reshape x3 -> x1, local copies, waits for them, and re-layouts: 4.86 us -> 0.1 us  [per_device(): blocks = spectrum.reshape(TURNS, PAIR, C, STEPS)]
    all_to_all x1, waiting for transfers between devices: 12.2 us -> 15.2 us  [per_device(): by_row = lax.all_to_all(by_order, 'lat', 0, 0, tiled=True)]
    pallas_call x1, Pallas kernels: 2.68 us -> 5.7 us  [pick(): pl.pallas_call(pick_kernel, out_shape=jax.ShapeDtypeStruct((LATS, SUB * R...]
  transfers between devices with their start and end apart: 3 -> 6, of which waited for: 2 -> 4; matrix products, arithmetic and copies ran while one was open for 12% -> 1% of each run, Pallas kernels for 3% -> 1%
where the time goes in v2:
time: 82.4 us; the launch traced here: 81.9 us
  waiting for transfers between devices  27.4 us (33%)
  starting transfers between devices  23.7 us (29%)
  blocking collectives  14.9 us (18%)
  Pallas kernels  14 us (17%)
  local copies, waits for them, and re-layouts  1.02 us (1%)
    all_to_all x1, waiting for transfers between devices, per_device(): by_row = lax.all_to_all(by_order, 'lat', 0, 0, tiled=True)  15.2 us
    all_to_all x1, blocking collectives, per_device(): own = lax.all_to_all(mixed, 'ch', 0, 0, tiled=True)  14.9 us
    all_to_all x1, starting transfers between devices, per_device(): leg = lax.all_to_all(picked, 'lat', 0, 0, tiled=True)  9.93 us
    ppermute x1, waiting for transfers between devices, per_device(): taken = lax.ppermute(given, 'ch', [(j, j ^ 1) for j in range(CHS)])  6.4 us
    all_to_all x1, starting transfers between devices, per_device(): by_row = lax.all_to_all(by_order, 'lat', 0, 0, tiled=True)  6.07 us
    pallas_call x1, Pallas kernels, pick(): pl.pallas_call(pick_kernel, out_shape=jax.ShapeDtypeStruct((LATS, SUB * R...  5.7 us
    ppermute x3, starting transfers between devices, per_device(): pieces.append(lax.ppermute(piece, 'ch', shift) if d else piece)  4.92 us
    pallas_call x1, Pallas kernels, order_stage(): pl.pallas_call(order_kernel, out_shape=jax.ShapeDtypeStruct((LATS, SUB *...  3.6 us
  transfers between devices with their start and end apart: 6, of which 4 were waited for; matrix products, arithmetic and copies ran while one was open for 1% of the time, Pallas kernels for 1%

profile of v2, /device:TPU:8, one launch (start us, length us, event | category | flops | bytes accessed | tf_op | source)
XLA Modules:
  0.0 81.9 jit_solution(5202619517410012801)
XLA Ops:
  0.0 0.0 copy-start.2
  0.0 0.0 copy-start.4
  0.0 5.7 %pick.1 = bf16[32,40,256]{2,1,0:T(8,128)(2,1)} custom-call(s32[32]{0:T(128)} %slots_ref.3, bf16[20,256,512]{2,1,0:T(8,128)(2,1)} %leg_ref.1), custom_call_target="tpu_custom_call" | custom-call | flops 335544320 | bytes 6291456 | tf_op jit(solution)/shard_map/pick/pallas_call | solution.py:111
  5.8 0.0 copy-start
  5.8 9.9 %all-to-all-start = ((bf16[32,40,256]{2,1,0:T(8,128)(2,1)}), bf16[32,40,256]{2,1,0:T(8,128)(2,1)S(1)}, u32[]{:S(2)}, u32[]{:S(2)}) async-start(bf16[32,40,256]{2,1,0:T(8,128)(2,1)} %pick.1), calls=%async_computation | async-start | bytes 1310720 | tf_op jit(solution)/shard_map/all_to_all | solution.py:347
  15.7 0.1 reshape.3
  15.9 2.8 %collective-permute-start = (bf16[4,64,256]{2,1,0:T(8,128)(2,1)S(1)}, bf16[4,64,256]{2,1,0:T(8,128)(2,1)S(1)}, u32[]{:S(2)}, u32[]{:S(2)}) collective-permute-start(bf16[4,64,256]{2,1,0:T(8,128)(2,1)S(1)} %get-tuple-element.25), channel_id=1, source_target_pairs={{0,1},{1,0},{2,3},{3,2},{4,5},{5,4},{6,7},{7,6},{8,9},{9,8},{10,11... | collective-permute-start | bytes 393224 | tf_op jit(solution)/shard_map/ppermute | solution.py:352
  18.7 6.4 %collective-permute-done = bf16[4,64,256]{2,1,0:T(8,128)(2,1)S(1)} collective-permute-done((bf16[4,64,256]{2,1,0:T(8,128)(2,1)S(1)}, bf16[4,64,256]{2,1,0:T(8,128)(2,1)S(1)}, u32[]{:S(2)}, u32[]{:S(2)}) %collective-permute-start) | collective-permute-done | bytes 131104 | tf_op jit(solution)/shard_map/ppermute | solution.py:352
  25.1 0.6 fusion.1
  25.7 1.6 %collective-permute-start.1 = (bf16[2,64,256]{2,1,0:T(8,128)(2,1)S(1)}, bf16[2,64,256]{2,1,0:T(8,128)(2,1)S(1)}, u32[]{:S(2)}, u32[]{:S(2)}) collective-permute-start(bf16[2,64,256]{2,1,0:T(8,128)(2,1)S(1)} %get-tuple-element.23), channel_id=1, source_target_pairs={{0,2},{1,3},{2,4},{3,5},{4,6},{5,7},{6,0},{7,1},{8,10},{9,11},{10,... | collective-permute-start | bytes 196616 | tf_op jit(solution)/shard_map/ppermute | solution.py:358
  27.3 0.9 %collective-permute-start.2 = (bf16[2,64,256]{2,1,0:T(8,128)(2,1)S(1)}, bf16[2,64,256]{2,1,0:T(8,128)(2,1)S(1)}, u32[]{:S(2)}, u32[]{:S(2)}) collective-permute-start(bf16[2,64,256]{2,1,0:T(8,128)(2,1)S(1)} %get-tuple-element.24), channel_id=1, source_target_pairs={{0,4},{1,5},{2,6},{3,7},{4,0},{5,1},{6,2},{7,3},{8,12},{9,13},{10,... | collective-permute-start | bytes 196616 | tf_op jit(solution)/shard_map/ppermute | solution.py:358
  28.3 2.4 %collective-permute-start.3 = (bf16[2,64,256]{2,1,0:T(8,128)(2,1)S(1)}, bf16[2,64,256]{2,1,0:T(8,128)(2,1)S(1)}, u32[]{:S(2)}, u32[]{:S(2)}) collective-permute-start(bf16[2,64,256]{2,1,0:T(8,128)(2,1)S(1)} %get-tuple-element.21), channel_id=1, source_target_pairs={{0,6},{1,7},{2,0},{3,1},{4,2},{5,3},{6,4},{7,5},{8,14},{9,15},{10,... | collective-permute-start | bytes 196616 | tf_op jit(solution)/shard_map/ppermute | solution.py:358
  30.7 0.0 collective-permute-done.1.refs_1_
  30.7 2.5 %collective-permute-done.2.refs_2_ = bf16[2,64,256]{2,1,0:T(8,128)(2,1)S(1)} collective-permute-done((bf16[2,64,256]{2,1,0:T(8,128)(2,1)S(1)}, bf16[2,64,256]{2,1,0:T(8,128)(2,1)S(1)}, u32[]{:S(2)}, u32[]{:S(2)}) %collective-permute-start.2) | collective-permute-done | bytes 65568 | tf_op jit(solution)/shard_map/ppermute | solution.py:358
  33.2 0.0 collective-permute-done.3.refs_3_
  33.2 3.2 %all-to-all-done.leg_ref = bf16[32,40,256]{2,1,0:T(8,128)(2,1)S(1)} async-done(((bf16[32,40,256]{2,1,0:T(8,128)(2,1)}), bf16[32,40,256]{2,1,0:T(8,128)(2,1)S(1)}, u32[]{:S(2)}, u32[]{:S(2)}) %all-to-all-start) | async-done | bytes 655392 | tf_op jit(solution)/shard_map/all_to_all | solution.py:347
  36.5 0.8 %copy-done.6 = bf16[32,40,256]{2,1,0:T(8,128)(2,1)} copy-done((bf16[32,40,256]{2,1,0:T(8,128)(2,1)}, bf16[32,40,256]{2,1,0:T(8,128)(2,1)S(1)}, u32[]{:S(2)}) %copy-start.6) | copy-done | bytes 655384
  37.3 3.6 %order_stage.1 = bf16[32,48,128]{2,1,0:T(8,128)(2,1)} custom-call(bf16[32,40,256]{2,1,0:T(8,128)(2,1)} %copy-done.6, bf16[2,64,256]{2,1,0:T(8,128)(2,1)} %get-tuple-element.22.refs_0_, bf16[2,64,256]{2,1,0:T(8,128)(2,1)} %copy-done.8, bf16[2,64,256]{2,1,0:T(8,128)(2,1)} %copy-done.9, bf16[2,64,256]{2,1,0:T(8,128)(2,1)} %copy-done.10), custom_call_target="tpu_custom_call" | custom-call | flops 734003200 | bytes 2097152 | tf_op jit(solution)/shard_map/order_stage/pallas_call | solution.py:210
  40.9 6.1 %all-to-all-start.1 = ((bf16[32,48,128]{2,1,0:T(8,128)(2,1)}), bf16[32,48,128]{2,1,0:T(8,128)(2,1)S(1)}, u32[]{:S(2)}, u32[]{:S(2)}) async-start(bf16[32,48,128]{2,1,0:T(8,128)(2,1)} %order_stage.1), calls=%async_computation.1 | async-start | bytes 786432 | tf_op jit(solution)/shard_map/all_to_all | solution.py:363
  47.0 0.6 coef_stage.1
  47.7 15.2 %all-to-all-done.1.rows_ref = bf16[32,48,128]{2,1,0:T(8,128)(2,1)S(1)} async-done(((bf16[32,48,128]{2,1,0:T(8,128)(2,1)}), bf16[32,48,128]{2,1,0:T(8,128)(2,1)S(1)}, u32[]{:S(2)}, u32[]{:S(2)}) %all-to-all-start.1) | async-done | bytes 393248 | tf_op jit(solution)/shard_map/all_to_all | solution.py:363
  62.9 2.6 %row_stage.1 = bf16[8,160,128]{2,1,0:T(8,128)(2,1)S(1)} custom-call(s32[32]{0:T(128)S(1)} %copy-done.5, bf16[32,48,128]{2,1,0:T(8,128)(2,1)S(1)} %all-to-all-done.1.rows_ref, f32[15,20,256]{2,1,0:T(8,128)S(1)} %get-tuple-element.19.coef_ref, bf16[64,384]{1,0:T(8,128)(2,1)S(1)} %get-tuple-element.20.mix_ref), custom_call_target="tpu_custom_call" | custom-call | flops 209715200 | bytes 2097152 | tf_op jit(solution)/shard_map/row_stage/pallas_call | solution.py:299
  65.5 14.9 %all_to_all.15.rows_ref = bf16[8,160,128]{2,1,0:T(8,128)(2,1)S(1)} all-to-all(bf16[8,160,128]{2,1,0:T(8,128)(2,1)S(1)} %row_stage.1), channel_id=1, replica_groups=mesh['lat'=32,'ch'=8] {'ch'}, dimensions={0} | all-to-all | bytes 655360 | tf_op jit(solution)/shard_map/all_to_all | solution.py:366
  80.4 1.5 %longitude_stage.1 = bf16[20,8,1440]{2,1,0:T(8,128)(2,1)} custom-call(bf16[8,160,128]{2,1,0:T(8,128)(2,1)S(1)} %all_to_all.15.rows_ref, bf16[1024,720]{1,0:T(8,128)(2,1)S(1)} %copy-done), custom_call_target="tpu_custom_call" | custom-call | flops 503316480 | bytes 4194304 | tf_op jit(solution)/shard_map/longitude_stage/pallas_call | solution.py:332
  (19 shorter events, 0.1 us)
Async XLA Ops:
  0.0 47.0 %copy-start.1 = (f32[8,16,256]{2,1,0:T(8,128)S(1)}, f32[8,16,256]{2,1,0:T(8,128)}, u32[]{:S(2)}) copy-start(f32[8,16,256]{2,1,0:T(8,128)} %constant.73.clone.waves_ref) | copy-start | bytes 393220
  0.0 62.9 %copy-start.5 = (s32[32]{0:T(128)S(1)}, s32[32]{0:T(128)}, u32[]{:S(2)}) copy-start(s32[32]{0:T(128)} %slots_ref.3) | copy-start | bytes 388
  0.0 15.7 %copy-start.7 = (bf16[16,8,2,2,256]{4,3,2,1,0:T(2,128)(2,1)S(1)}, bf16[16,8,2,2,256]{4,3,2,1,0:T(2,128)(2,1)}, u32[]{:S(2)}) copy-start(bf16[16,8,2,2,256]{4,3,2,1,0:T(2,128)(2,1)} %param.8) | copy-start | bytes 786436
  0.0 47.0 %copy-start.2 = (bf16[3,20,6,9]{1,2,3,0:T(8,128)(2,1)S(1)}, bf16[3,20,6,9]{1,2,3,0:T(8,128)(2,1)}, u32[]{:S(2)}) copy-start(bf16[3,20,6,9]{1,2,3,0:T(8,128)(2,1)} %param.11) | copy-start | bytes 19444
  0.0 47.0 %copy-start.4 = (s32[20,6]{0,1:T(8,128)S(1)}, s32[20,6]{0,1:T(8,128)}, u32[]{:S(2)}) copy-start(s32[20,6]{0,1:T(8,128)} %param.12) | copy-start | bytes 1444
  0.0 47.0 %copy-start.3 = (bf16[3,64,64]{2,1,0:T(8,128)(2,1)S(1)}, bf16[3,64,64]{2,1,0:T(8,128)(2,1)}, u32[]{:S(2)}) copy-start(bf16[3,64,64]{2,1,0:T(8,128)(2,1)} %mix_ref) | copy-start | bytes 73732
  5.8 74.7 %copy-start = (bf16[1024,720]{1,0:T(8,128)(2,1)S(1)}, bf16[1024,720]{1,0:T(8,128)(2,1)}, u32[]{:S(2)}) copy-start(bf16[1024,720]{1,0:T(8,128)(2,1)} %constant.74.clone.table_ref) | copy-start | bytes 4423684
  5.8 30.7 %all-to-all-start = ((bf16[32,40,256]{2,1,0:T(8,128)(2,1)}), bf16[32,40,256]{2,1,0:T(8,128)(2,1)S(1)}, u32[]{:S(2)}, u32[]{:S(2)}) async-start(bf16[32,40,256]{2,1,0:T(8,128)(2,1)} %pick.1), calls=%async_computation | async-start | bytes 1310720 | tf_op jit(solution)/shard_map/all_to_all | solution.py:347
  15.9 9.2 %collective-permute-start = (bf16[4,64,256]{2,1,0:T(8,128)(2,1)S(1)}, bf16[4,64,256]{2,1,0:T(8,128)(2,1)S(1)}, u32[]{:S(2)}, u32[]{:S(2)}) collective-permute-start(bf16[4,64,256]{2,1,0:T(8,128)(2,1)S(1)} %get-tuple-element.25), channel_id=1, source_target_pairs={{0,1},{1,0},{2,3},{3,2},{4,5},{5,4},{6,7},{7,6},{8,9},{9,8},{10,11... | collective-permute-start | bytes 393224 | tf_op jit(solution)/shard_map/ppermute | solution.py:352
  25.7 4.9 %collective-permute-start.1 = (bf16[2,64,256]{2,1,0:T(8,128)(2,1)S(1)}, bf16[2,64,256]{2,1,0:T(8,128)(2,1)S(1)}, u32[]{:S(2)}, u32[]{:S(2)}) collective-permute-start(bf16[2,64,256]{2,1,0:T(8,128)(2,1)S(1)} %get-tuple-element.23), channel_id=1, source_target_pairs={{0,2},{1,3},{2,4},{3,5},{4,6},{5,7},{6,0},{7,1},{8,10},{9,11},{10,... | collective-permute-start | bytes 196616 | tf_op jit(solution)/shard_map/ppermute | solution.py:358
  27.3 5.9 %collective-permute-start.2 = (bf16[2,64,256]{2,1,0:T(8,128)(2,1)S(1)}, bf16[2,64,256]{2,1,0:T(8,128)(2,1)S(1)}, u32[]{:S(2)}, u32[]{:S(2)}) collective-permute-start(bf16[2,64,256]{2,1,0:T(8,128)(2,1)S(1)} %get-tuple-element.24), channel_id=1, source_target_pairs={{0,4},{1,5},{2,6},{3,7},{4,0},{5,1},{6,2},{7,3},{8,12},{9,13},{10,... | collective-permute-start | bytes 196616 | tf_op jit(solution)/shard_map/ppermute | solution.py:358
  28.3 5.0 %collective-permute-start.3 = (bf16[2,64,256]{2,1,0:T(8,128)(2,1)S(1)}, bf16[2,64,256]{2,1,0:T(8,128)(2,1)S(1)}, u32[]{:S(2)}, u32[]{:S(2)}) collective-permute-start(bf16[2,64,256]{2,1,0:T(8,128)(2,1)S(1)} %get-tuple-element.21), channel_id=1, source_target_pairs={{0,6},{1,7},{2,0},{3,1},{4,2},{5,3},{6,4},{7,5},{8,14},{9,15},{10,... | collective-permute-start | bytes 196616 | tf_op jit(solution)/shard_map/ppermute | solution.py:358
  30.7 5.8 %copy-start.8 = (bf16[2,64,256]{2,1,0:T(8,128)(2,1)}, bf16[2,64,256]{2,1,0:T(8,128)(2,1)S(1)}, u32[]{:S(2)}) copy-start(bf16[2,64,256]{2,1,0:T(8,128)(2,1)S(1)} %collective-permute-done.1.refs_1_) | copy-start | bytes 196612
  33.2 3.3 %copy-start.9 = (bf16[2,64,256]{2,1,0:T(8,128)(2,1)}, bf16[2,64,256]{2,1,0:T(8,128)(2,1)S(1)}, u32[]{:S(2)}) copy-start(bf16[2,64,256]{2,1,0:T(8,128)(2,1)S(1)} %collective-permute-done.2.refs_2_) | copy-start | bytes 196612
  33.2 3.2 %copy-start.10 = (bf16[2,64,256]{2,1,0:T(8,128)(2,1)}, bf16[2,64,256]{2,1,0:T(8,128)(2,1)S(1)}, u32[]{:S(2)}) copy-start(bf16[2,64,256]{2,1,0:T(8,128)(2,1)S(1)} %collective-permute-done.3.refs_3_) | copy-start | bytes 196612
  36.5 0.9 %copy-start.6 = (bf16[32,40,256]{2,1,0:T(8,128)(2,1)}, bf16[32,40,256]{2,1,0:T(8,128)(2,1)S(1)}, u32[]{:S(2)}) copy-start(bf16[32,40,256]{2,1,0:T(8,128)(2,1)S(1)} %all-to-all-done.leg_ref) | copy-start | bytes 1966084
  40.9 22.0 %all-to-all-start.1 = ((bf16[32,48,128]{2,1,0:T(8,128)(2,1)}), bf16[32,48,128]{2,1,0:T(8,128)(2,1)S(1)}, u32[]{:S(2)}, u32[]{:S(2)}) async-start(bf16[32,48,128]{2,1,0:T(8,128)(2,1)} %order_stage.1), calls=%async_computation.1 | async-start | bytes 786432 | tf_op jit(solution)/shard_map/all_to_all | solution.py:363

commit v3 on v2

--- a/solution.py
+++ b/solution.py
@@ -47,9 +47,9 @@
 
 def order_table():
     orders = (
-        ORDER_BLOCK * np.arange(BLOCKS)[None, :, None]
+        ORDER_BLOCK * np.arange(BLOCKS)[None, None, :]
         + SUB * np.arange(CHS)[:, None, None]
-        + np.arange(SUB)[None, None, :]
+        + np.arange(SUB)[None, :, None]
     )
     return orders.reshape(CHS, 1, PICKS, 1)
 
@@ -73,52 +73,62 @@
     return waves
 
 
-PICK_ROWS = 2
-PICK_AHEAD = 4
-
-
-def pick_kernel(slots_ref, leg_ref, out_ref, buf, wide, flat, sems, out_sem):
-    copies = []
-    for g in range(ROWS // PICK_ROWS):
+PICK_ROWS = 4
+PICK_AHEAD = 3
+GROUPS = ROWS // PICK_ROWS
+PICK_LINES = PICK_ROWS * SUB
+EDGE = 12
+
+
+def pick_kernel(slots_ref, leg_ref, out_ref, buf, wide, flat, sems):
+    arrivals, departures = [], []
+    for g in range(GROUPS):
         rows = pl.ds(g * PICK_ROWS, PICK_ROWS)
-        copies.append(pltpu.make_async_copy(leg_ref.at[rows], buf.at[rows], sems.at[g]))
-    for copy in copies[:PICK_AHEAD]:
+        lines = pl.ds(g * PICK_LINES, PICK_LINES)
+        arrivals.append(pltpu.make_async_copy(leg_ref.at[rows], buf.at[rows], sems.at[0, g]))
+        departures.append(pltpu.make_async_copy(flat.at[g], out_ref.at[:, lines, :], sems.at[1, g]))
+    for copy in arrivals[:PICK_AHEAD]:
         copy.start()
-    lines = lax.broadcasted_iota(jnp.int32, (PICKS, LMAX), 0)
-    orders = lax.broadcasted_iota(jnp.int32, (PICKS, LMAX), 1)
+    line = lax.broadcasted_iota(jnp.int32, (PICKS, LMAX), 0)
+    order = lax.broadcasted_iota(jnp.int32, (PICKS, LMAX), 1)
     blocks = jnp.zeros((PICKS, LMAX), jnp.int32)
     for i in range(LATS):
-        blocks = jnp.where(lines // SUB == i, slots_ref[i], blocks)
-    wanted = blocks * ORDER_BLOCK + lines % SUB + SUB * lax.axis_index("ch")
-    hot = jnp.where(orders == wanted, 1.0, 0.0).astype(BF)
-    for r in range(ROWS):
-        if r % PICK_ROWS == 0:
-            copies[r // PICK_ROWS].wait()
-            for copy in copies[r // PICK_ROWS + PICK_AHEAD :][:1]:
-                copy.start()
-        picked = lax.dot_general(hot, buf[r], NT, preferred_element_type=F32)
+        blocks = jnp.where(line % LATS == i, slots_ref[i], blocks)
+    wanted = blocks * ORDER_BLOCK + line // LATS + SUB * lax.axis_index("ch")
+    hot = jnp.where(order == wanted, 1.0, 0.0).astype(BF)
+    for g in range(GROUPS):
+        arrivals[g].wait()
+        for copy in arrivals[g + PICK_AHEAD :][:1]:
+            copy.start()
+        for r in range(PICK_ROWS):
+            picked = lax.dot_general(
+                hot, buf[g * PICK_ROWS + r], NT, preferred_element_type=F32
+            )
+            for t in range(SUB):
+                for h in range(STEPS // LANES):
+                    wide[g, h, pl.ds(r * SUB + t, LATS, stride=PICK_LINES), :] = picked[
+                        t * LATS : (t + 1) * LATS, h * LANES : (h + 1) * LANES
+                    ]
         for h in range(STEPS // LANES):
-            wide[h, pl.ds(r, PICKS, stride=ROWS), :] = picked[:, h * LANES : (h + 1) * LANES]
-    for h in range(STEPS // LANES):
-        half = wide[h].astype(BF)
-        flat[:, :, h * LANES : (h + 1) * LANES] = half.reshape(LATS, SUB * ROWS, LANES)
-    done = pltpu.make_async_copy(flat, out_ref, out_sem)
-    done.start()
-    done.wait()
+            flat[g, :, :, h * LANES : (h + 1) * LANES] = (
+                wide[g, h].reshape(LATS, PICK_LINES, LANES).astype(BF)
+            )
+        departures[g].start()
+    for copy in departures:
+        copy.wait()
 
 
 def pick(block_slots, legendre):
     return pl.pallas_call(
         pick_kernel,
-        out_shape=jax.ShapeDtypeStruct((LATS, SUB * ROWS, STEPS), BF),
+        out_shape=jax.ShapeDtypeStruct((LATS, ROWS * SUB, STEPS), BF),
         in_specs=[pl.BlockSpec(memory_space=pltpu.SMEM), pl.BlockSpec(memory_space=pltpu.HBM)],
         out_specs=pl.BlockSpec(memory_space=pltpu.HBM),
         scratch_shapes=[
             pltpu.VMEM((ROWS, STEPS, LMAX), BF),
-            pltpu.VMEM((STEPS // LANES, PICKS * ROWS, LANES), F32),
-            pltpu.VMEM((LATS, SUB * ROWS, STEPS), BF),
-            pltpu.SemaphoreType.DMA((ROWS // PICK_ROWS,)),
-            pltpu.SemaphoreType.DMA,
+            pltpu.VMEM((GROUPS, STEPS // LANES, LATS * PICK_LINES, LANES), F32),
+            pltpu.VMEM((GROUPS, LATS, PICK_LINES, STEPS), BF),
+            pltpu.SemaphoreType.DMA((2, GROUPS)),
         ],
         compiler_params=pltpu.CompilerParams(vmem_limit_bytes=GRANT),
         cost_estimate=pl.CostEstimate(flops=2 * 64 * 512 * 5120, bytes_accessed=6 << 20, transcendentals=0),
@@ -127,16 +137,14 @@
 
 
 def order_kernel(leg_ref, *refs):
-    pieces_in, (out_ref, got, raw, leg, specs, full, send, sems) = refs[:TURNS], refs[TURNS:]
+    pieces_in, (out_ref, raw, specs, full, send, sems) = refs[:TURNS], refs[TURNS:]
     half = NLAT // 2
     ch_index = lax.axis_index("ch")
     side = lax.rem(ch_index, PAIR)
-    arrivals, departures = [], []
+    departures = []
     for g in range(LATS // LAT_CHUNK):
         part = pl.ds(g * LAT_CHUNK, LAT_CHUNK)
-        arrivals.append(pltpu.make_async_copy(leg_ref.at[part], got.at[part], sems.at[0, g]))
-        arrivals[-1].start()
-        departures.append(pltpu.make_async_copy(send.at[part], out_ref.at[part], sems.at[1, g]))
+        departures.append(pltpu.make_async_copy(send.at[part], out_ref.at[part], sems.at[g]))
     for d in range(TURNS):
         turn = lax.rem(lax.div(ch_index, PAIR) + (TURNS - d), TURNS)
         for q in range(PAIR):
@@ -145,23 +153,19 @@
                 lanes = slice(h * LANES, (h + 1) * LANES)
                 start = pl.multiple_of(source * C, C)
                 specs[h, pl.ds(start, C), :] = pieces_in[d][q, :, lanes].astype(F32)
-    for i in range(LATS):
-        if i % LAT_CHUNK == 0:
-            arrivals[i // LAT_CHUNK].wait()
-        for h in range(STEPS // LANES):
-            lanes = slice(h * LANES, (h + 1) * LANES)
-            raw[h, pl.ds(i * SUB * ROWS, SUB * ROWS), :] = got[i, :, lanes].astype(F32)
-    for i in range(LATS):
-        for t in range(SUB):
-            for h in range(STEPS // LANES):
-                leg[t, h, pl.ds(i * ROWS, ROWS), :] = raw[h, pl.ds((i * SUB + t) * ROWS, ROWS), :]
+    for h in range(STEPS // LANES):
+        lanes = slice(h * LANES, (h + 1) * LANES)
+        raw[h] = leg_ref[:, :, lanes].astype(F32).reshape(LATS * ROWS * SUB, LANES)
     rows = lax.broadcasted_iota(jnp.int32, (LANES, LANES), 0)
     cols = lax.broadcasted_iota(jnp.int32, (LANES, LANES), 1)
     turn = jnp.where(rows + cols == LANES - 1, 1.0, 0.0).astype(BF)
     stride = 4
-    full[...] = jnp.zeros_like(full)
+    full[:16, :] = jnp.zeros((16, LANES), F32)
+    full[SUB * NLAT :, :] = jnp.zeros((2 * EDGE, LANES), F32)
     for t in range(SUB):
-        table = jnp.concatenate([leg[t, h] for h in range(STEPS // LANES)], axis=1).astype(BF)
+        table = jnp.concatenate(
+            [raw[h, pl.ds(t, NLAT, stride=SUB), :] for h in range(STEPS // LANES)], axis=1
+        ).astype(BF)
         count = NLAT // LANES
         turned = jnp.concatenate(
             [
@@ -194,12 +198,13 @@
         def dot(a, b):
             return lax.dot_general(a, b, NT, preferred_element_type=F32)
 
-        full[t, pl.ds(8, half), :] = dot(table[:half], coeffs[0]) - dot(turned[:half], coeffs[1])
-        full[t, pl.ds(8 + half, half), :] = dot(table[half:], coeffs[1]) + dot(turned[half:], coeffs[0])
+        north = dot(table[:half], coeffs[0]) - dot(turned[:half], coeffs[1])
+        south = dot(table[half:], coeffs[1]) + dot(turned[half:], coeffs[0])
+        full[pl.ds(EDGE + t, half, stride=SUB), :] = north
+        full[pl.ds(EDGE + t + SUB * half, half, stride=SUB), :] = south
     for i in range(LATS):
-        start = 8 - REACH + i * ROWS
-        block = [full[t, pl.ds(start, HALO_ROWS), :] for t in range(SUB)]
-        send[i] = jnp.concatenate(block, axis=0).astype(BF)
+        start = EDGE - REACH * SUB + i * ROWS * SUB
+        send[i] = full[start : start + HALO_ROWS * SUB, :].astype(BF)
         if i % LAT_CHUNK == LAT_CHUNK - 1:
             departures[i // LAT_CHUNK].start()
     for copy in departures:
@@ -209,17 +214,15 @@
 def order_stage(leg, pieces):
     return pl.pallas_call(
         order_kernel,
-        out_shape=jax.ShapeDtypeStruct((LATS, SUB * HALO_ROWS, LANES), BF),
-        in_specs=[pl.BlockSpec(memory_space=pltpu.HBM)] + [pl.BlockSpec(memory_space=VMEM)] * TURNS,
+        out_shape=jax.ShapeDtypeStruct((LATS, HALO_ROWS * SUB, LANES), BF),
+        in_specs=[pl.BlockSpec(memory_space=VMEM)] * (1 + TURNS),
         out_specs=pl.BlockSpec(memory_space=pltpu.HBM),
         scratch_shapes=[
-            pltpu.VMEM((LATS, SUB * ROWS, STEPS), BF),
             pltpu.VMEM((STEPS // LANES, LATS * SUB * ROWS, LANES), F32),
-            pltpu.VMEM((SUB, STEPS // LANES, NLAT, LANES), F32),
             pltpu.VMEM((STEPS // LANES, CHS * C, LANES), F32),
-            pltpu.VMEM((SUB, NLAT + 16, LANES), F32),
+            pltpu.VMEM((SUB * NLAT + 2 * EDGE, LANES), F32),
             pltpu.VMEM((LATS, SUB * HALO_ROWS, LANES), BF),
-            pltpu.SemaphoreType.DMA((2, LATS // LAT_CHUNK)),
+            pltpu.SemaphoreType.DMA((LATS // LAT_CHUNK,)),
         ],
         compiler_params=pltpu.CompilerParams(vmem_limit_bytes=GRANT),
         cost_estimate=pl.CostEstimate(flops=700 << 20, bytes_accessed=2 << 20, transcendentals=0),
@@ -274,7 +277,13 @@
         field[pl.ds(start, SUB * HALO_ROWS), :] = rows_ref[i].astype(F32)
     low = lax.broadcasted_iota(jnp.int32, (C, LANES), 1) < PICKS
     for r in range(HALO_ROWS):
-        one = field[pl.ds(r, PICKS, stride=HALO_ROWS), :]
+        one = jnp.concatenate(
+            [
+                field[pl.ds(r * SUB + t, BLOCKS, stride=SUB * HALO_ROWS), :]
+                for t in range(SUB)
+            ],
+            axis=0,
+        )
         both = jnp.concatenate([one, one], axis=0).T
         plain[r] = jnp.where(low, both[:C], both[C:])
         crossed[r] = jnp.where(low, both[C:], both[:C])
@@ -320,7 +329,7 @@
 def longitude_kernel(rows_ref, table_ref, out_ref):
     even = jnp.concatenate([rows_ref[j] for j in range(CHS)], axis=1)
     lane = lax.broadcasted_iota(jnp.int32, even.shape, 1)
-    flipped = jnp.where(lane % SUB == 0, even.astype(F32), -even.astype(F32)).astype(BF)
+    flipped = jnp.where(lane % PICKS < BLOCKS, even.astype(F32), -even.astype(F32)).astype(BF)
     both = jnp.concatenate([even, flipped], axis=0)
     field = jnp.dot(both, table_ref[...], preferred_element_type=F32)
     count = OWN * ROWS

time: 82.4 us -> 80.8 us (0.981)
  Pallas kernels: 14 us -> 12.6 us
    pallas_call x2, Pallas kernels: 9.31 us -> 7.79 us  [the longest x1 5.1 us: pick(): pl.pallas_call(pick_kernel, out_shape=jax.ShapeDtypeStruct((LATS, ROWS *...]
where the time goes in v3:
time: 80.8 us; the launch traced here: 80.5 us
  waiting for transfers between devices  27.4 us (34%)
  starting transfers between devices  23.7 us (29%)
  blocking collectives  14.9 us (18%)
  Pallas kernels  12.6 us (16%)
  local copies, waits for them, and re-layouts  1.02 us (1%)
    all_to_all x1, waiting for transfers between devices, per_device(): by_row = lax.all_to_all(by_order, 'lat', 0, 0, tiled=True)  15.2 us
    all_to_all x1, blocking collectives, per_device(): own = lax.all_to_all(mixed, 'ch', 0, 0, tiled=True)  14.9 us
    all_to_all x1, starting transfers between devices, per_device(): leg = lax.all_to_all(picked, 'lat', 0, 0, tiled=True)  9.92 us
    ppermute x1, waiting for transfers between devices, per_device(): taken = lax.ppermute(given, 'ch', [(j, j ^ 1) for j in range(CHS)])  6.4 us
    all_to_all x1, starting transfers between devices, per_device(): by_row = lax.all_to_all(by_order, 'lat', 0, 0, tiled=True)  6.07 us
    pallas_call x1, Pallas kernels, pick(): pl.pallas_call(pick_kernel, out_shape=jax.ShapeDtypeStruct((LATS, ROWS *...  5.1 us
    ppermute x3, starting transfers between devices, per_device(): pieces.append(lax.ppermute(piece, 'ch', shift) if d else piece)  4.93 us
    all_to_all x1, waiting for transfers between devices, per_device(): leg = lax.all_to_all(picked, 'lat', 0, 0, tiled=True)  3.23 us
  transfers between devices with their start and end apart: 6, of which 4 were waited for; matrix products, arithmetic and copies ran while one was open for 1% of the time, Pallas kernels for 1%

profile of v3, /device:TPU:8, one launch (start us, length us, event | category | flops | bytes accessed | tf_op | source)
XLA Modules:
  0.0 80.5 jit_solution(15636959376323419569)
XLA Ops:
  0.0 5.1 %pick.1 = bf16[32,40,256]{2,1,0:T(8,128)(2,1)} custom-call(s32[32]{0:T(128)} %slots_ref.3, bf16[20,256,512]{2,1,0:T(8,128)(2,1)} %leg_ref.1), custom_call_target="tpu_custom_call" | custom-call | flops 335544320 | bytes 6291456 | tf_op jit(solution)/shard_map/pick/pallas_call | solution.py:122
  5.1 0.0 copy-start
  5.2 9.9 %all-to-all-start = ((bf16[32,40,256]{2,1,0:T(8,128)(2,1)}), bf16[32,40,256]{2,1,0:T(8,128)(2,1)S(1)}, u32[]{:S(2)}, u32[]{:S(2)}) async-start(bf16[32,40,256]{2,1,0:T(8,128)(2,1)} %pick.1), calls=%async_computation | async-start | bytes 1310720 | tf_op jit(solution)/shard_map/all_to_all | solution.py:356
  15.1 0.1 reshape.3
  15.3 2.8 %collective-permute-start = (bf16[4,64,256]{2,1,0:T(8,128)(2,1)S(1)}, bf16[4,64,256]{2,1,0:T(8,128)(2,1)S(1)}, u32[]{:S(2)}, u32[]{:S(2)}) collective-permute-start(bf16[4,64,256]{2,1,0:T(8,128)(2,1)S(1)} %get-tuple-element.25), channel_id=1, source_target_pairs={{0,1},{1,0},{2,3},{3,2},{4,5},{5,4},{6,7},{7,6},{8,9},{9,8},{10,11... | collective-permute-start | bytes 393224 | tf_op jit(solution)/shard_map/ppermute | solution.py:361
  18.1 6.4 %collective-permute-done = bf16[4,64,256]{2,1,0:T(8,128)(2,1)S(1)} collective-permute-done((bf16[4,64,256]{2,1,0:T(8,128)(2,1)S(1)}, bf16[4,64,256]{2,1,0:T(8,128)(2,1)S(1)}, u32[]{:S(2)}, u32[]{:S(2)}) %collective-permute-start) | collective-permute-done | bytes 131104 | tf_op jit(solution)/shard_map/ppermute | solution.py:361
  24.5 0.6 fusion.1
  25.1 1.6 %collective-permute-start.1 = (bf16[2,64,256]{2,1,0:T(8,128)(2,1)S(1)}, bf16[2,64,256]{2,1,0:T(8,128)(2,1)S(1)}, u32[]{:S(2)}, u32[]{:S(2)}) collective-permute-start(bf16[2,64,256]{2,1,0:T(8,128)(2,1)S(1)} %get-tuple-element.23), channel_id=1, source_target_pairs={{0,2},{1,3},{2,4},{3,5},{4,6},{5,7},{6,0},{7,1},{8,10},{9,11},{10,... | collective-permute-start | bytes 196616 | tf_op jit(solution)/shard_map/ppermute | solution.py:367
  26.7 0.9 %collective-permute-start.2 = (bf16[2,64,256]{2,1,0:T(8,128)(2,1)S(1)}, bf16[2,64,256]{2,1,0:T(8,128)(2,1)S(1)}, u32[]{:S(2)}, u32[]{:S(2)}) collective-permute-start(bf16[2,64,256]{2,1,0:T(8,128)(2,1)S(1)} %get-tuple-element.24), channel_id=1, source_target_pairs={{0,4},{1,5},{2,6},{3,7},{4,0},{5,1},{6,2},{7,3},{8,12},{9,13},{10,... | collective-permute-start | bytes 196616 | tf_op jit(solution)/shard_map/ppermute | solution.py:367
  27.6 2.4 %collective-permute-start.3 = (bf16[2,64,256]{2,1,0:T(8,128)(2,1)S(1)}, bf16[2,64,256]{2,1,0:T(8,128)(2,1)S(1)}, u32[]{:S(2)}, u32[]{:S(2)}) collective-permute-start(bf16[2,64,256]{2,1,0:T(8,128)(2,1)S(1)} %get-tuple-element.21), channel_id=1, source_target_pairs={{0,6},{1,7},{2,0},{3,1},{4,2},{5,3},{6,4},{7,5},{8,14},{9,15},{10,... | collective-permute-start | bytes 196616 | tf_op jit(solution)/shard_map/ppermute | solution.py:367
  30.1 0.0 collective-permute-done.1.refs_1_
  30.1 2.5 %collective-permute-done.2.refs_2_ = bf16[2,64,256]{2,1,0:T(8,128)(2,1)S(1)} collective-permute-done((bf16[2,64,256]{2,1,0:T(8,128)(2,1)S(1)}, bf16[2,64,256]{2,1,0:T(8,128)(2,1)S(1)}, u32[]{:S(2)}, u32[]{:S(2)}) %collective-permute-start.2) | collective-permute-done | bytes 65568 | tf_op jit(solution)/shard_map/ppermute | solution.py:367
  32.6 0.0 collective-permute-done.3.refs_3_
  32.6 3.2 %all-to-all-done.leg_ref = bf16[32,40,256]{2,1,0:T(8,128)(2,1)S(1)} async-done(((bf16[32,40,256]{2,1,0:T(8,128)(2,1)}), bf16[32,40,256]{2,1,0:T(8,128)(2,1)S(1)}, u32[]{:S(2)}, u32[]{:S(2)}) %all-to-all-start) | async-done | bytes 655392 | tf_op jit(solution)/shard_map/all_to_all | solution.py:356
  35.9 0.0 copy-done.10
  35.9 0.8 %copy-done.6 = bf16[32,40,256]{2,1,0:T(8,128)(2,1)} copy-done((bf16[32,40,256]{2,1,0:T(8,128)(2,1)}, bf16[32,40,256]{2,1,0:T(8,128)(2,1)S(1)}, u32[]{:S(2)}) %copy-start.6) | copy-done | bytes 655384
  36.7 2.7 %order_stage.1 = bf16[32,48,128]{2,1,0:T(8,128)(2,1)} custom-call(bf16[32,40,256]{2,1,0:T(8,128)(2,1)} %copy-done.6, bf16[2,64,256]{2,1,0:T(8,128)(2,1)} %get-tuple-element.22.refs_0_, bf16[2,64,256]{2,1,0:T(8,128)(2,1)} %copy-done.8, bf16[2,64,256]{2,1,0:T(8,128)(2,1)} %copy-done.9, bf16[2,64,256]{2,1,0:T(8,128)(2,1)} %copy-done.10), custom_call_target="tpu_custom_call" | custom-call | flops 734003200 | bytes 2097152 | tf_op jit(solution)/shard_map/order_stage/pallas_call | solution.py:215
  39.4 6.1 %all-to-all-start.1 = ((bf16[32,48,128]{2,1,0:T(8,128)(2,1)}), bf16[32,48,128]{2,1,0:T(8,128)(2,1)S(1)}, u32[]{:S(2)}, u32[]{:S(2)}) async-start(bf16[32,48,128]{2,1,0:T(8,128)(2,1)} %order_stage.1), calls=%async_computation.1 | async-start | bytes 786432 | tf_op jit(solution)/shard_map/all_to_all | solution.py:372
  45.5 0.0 copy-done.1
  45.5 0.6 coef_stage.1
  46.1 15.2 %all-to-all-done.1.rows_ref = bf16[32,48,128]{2,1,0:T(8,128)(2,1)S(1)} async-done(((bf16[32,48,128]{2,1,0:T(8,128)(2,1)}), bf16[32,48,128]{2,1,0:T(8,128)(2,1)S(1)}, u32[]{:S(2)}, u32[]{:S(2)}) %all-to-all-start.1) | async-done | bytes 393248 | tf_op jit(solution)/shard_map/all_to_all | solution.py:372
  61.4 2.7 %row_stage.1 = bf16[8,160,128]{2,1,0:T(8,128)(2,1)S(1)} custom-call(s32[32]{0:T(128)S(1)} %copy-done.5, bf16[32,48,128]{2,1,0:T(8,128)(2,1)S(1)} %all-to-all-done.1.rows_ref, f32[15,20,256]{2,1,0:T(8,128)S(1)} %get-tuple-element.19.coef_ref, bf16[64,384]{1,0:T(8,128)(2,1)S(1)} %get-tuple-element.20.mix_ref), custom_call_target="tpu_custom_call" | custom-call | flops 209715200 | bytes 2097152 | tf_op jit(solution)/shard_map/row_stage/pallas_call | solution.py:308
  64.1 14.9 %all_to_all.15.rows_ref = bf16[8,160,128]{2,1,0:T(8,128)(2,1)S(1)} all-to-all(bf16[8,160,128]{2,1,0:T(8,128)(2,1)S(1)} %row_stage.1), channel_id=1, replica_groups=mesh['lat'=32,'ch'=8] {'ch'}, dimensions={0} | all-to-all | bytes 655360 | tf_op jit(solution)/shard_map/all_to_all | solution.py:375
  78.9 1.5 %longitude_stage.1 = bf16[20,8,1440]{2,1,0:T(8,128)(2,1)} custom-call(bf16[8,160,128]{2,1,0:T(8,128)(2,1)S(1)} %all_to_all.15.rows_ref, bf16[1024,720]{1,0:T(8,128)(2,1)S(1)} %copy-done), custom_call_target="tpu_custom_call" | custom-call | flops 503316480 | bytes 4194304 | tf_op jit(solution)/shard_map/longitude_stage/pallas_call | solution.py:341
  (19 shorter events, 0.1 us)
Async XLA Ops:
  0.0 45.5 %copy-start.1 = (f32[8,16,256]{2,1,0:T(8,128)S(1)}, f32[8,16,256]{2,1,0:T(8,128)}, u32[]{:S(2)}) copy-start(f32[8,16,256]{2,1,0:T(8,128)} %constant.73.clone.waves_ref) | copy-start | bytes 393220
  0.0 61.4 %copy-start.5 = (s32[32]{0:T(128)S(1)}, s32[32]{0:T(128)}, u32[]{:S(2)}) copy-start(s32[32]{0:T(128)} %slots_ref.3) | copy-start | bytes 388
  0.0 15.1 %copy-start.7 = (bf16[16,8,2,2,256]{4,3,2,1,0:T(2,128)(2,1)S(1)}, bf16[16,8,2,2,256]{4,3,2,1,0:T(2,128)(2,1)}, u32[]{:S(2)}) copy-start(bf16[16,8,2,2,256]{4,3,2,1,0:T(2,128)(2,1)} %param.8) | copy-start | bytes 786436
  0.0 45.5 %copy-start.2 = (bf16[3,20,6,9]{1,2,3,0:T(8,128)(2,1)S(1)}, bf16[3,20,6,9]{1,2,3,0:T(8,128)(2,1)}, u32[]{:S(2)}) copy-start(bf16[3,20,6,9]{1,2,3,0:T(8,128)(2,1)} %param.11) | copy-start | bytes 19444
  0.0 45.5 %copy-start.4 = (s32[20,6]{0,1:T(8,128)S(1)}, s32[20,6]{0,1:T(8,128)}, u32[]{:S(2)}) copy-start(s32[20,6]{0,1:T(8,128)} %param.12) | copy-start | bytes 1444
  0.0 45.5 %copy-start.3 = (bf16[3,64,64]{2,1,0:T(8,128)(2,1)S(1)}, bf16[3,64,64]{2,1,0:T(8,128)(2,1)}, u32[]{:S(2)}) copy-start(bf16[3,64,64]{2,1,0:T(8,128)(2,1)} %mix_ref) | copy-start | bytes 73732
  5.1 73.8 %copy-start = (bf16[1024,720]{1,0:T(8,128)(2,1)S(1)}, bf16[1024,720]{1,0:T(8,128)(2,1)}, u32[]{:S(2)}) copy-start(bf16[1024,720]{1,0:T(8,128)(2,1)} %constant.74.clone.table_ref) | copy-start | bytes 4423684
  5.2 30.7 %all-to-all-start = ((bf16[32,40,256]{2,1,0:T(8,128)(2,1)}), bf16[32,40,256]{2,1,0:T(8,128)(2,1)S(1)}, u32[]{:S(2)}, u32[]{:S(2)}) async-start(bf16[32,40,256]{2,1,0:T(8,128)(2,1)} %pick.1), calls=%async_computation | async-start | bytes 1310720 | tf_op jit(solution)/shard_map/all_to_all | solution.py:356
  15.3 9.2 %collective-permute-start = (bf16[4,64,256]{2,1,0:T(8,128)(2,1)S(1)}, bf16[4,64,256]{2,1,0:T(8,128)(2,1)S(1)}, u32[]{:S(2)}, u32[]{:S(2)}) collective-permute-start(bf16[4,64,256]{2,1,0:T(8,128)(2,1)S(1)} %get-tuple-element.25), channel_id=1, source_target_pairs={{0,1},{1,0},{2,3},{3,2},{4,5},{5,4},{6,7},{7,6},{8,9},{9,8},{10,11... | collective-permute-start | bytes 393224 | tf_op jit(solution)/shard_map/ppermute | solution.py:361
  25.1 4.9 %collective-permute-start.1 = (bf16[2,64,256]{2,1,0:T(8,128)(2,1)S(1)}, bf16[2,64,256]{2,1,0:T(8,128)(2,1)S(1)}, u32[]{:S(2)}, u32[]{:S(2)}) collective-permute-start(bf16[2,64,256]{2,1,0:T(8,128)(2,1)S(1)} %get-tuple-element.23), channel_id=1, source_target_pairs={{0,2},{1,3},{2,4},{3,5},{4,6},{5,7},{6,0},{7,1},{8,10},{9,11},{10,... | collective-permute-start | bytes 196616 | tf_op jit(solution)/shard_map/ppermute | solution.py:367
  26.7 5.9 %collective-permute-start.2 = (bf16[2,64,256]{2,1,0:T(8,128)(2,1)S(1)}, bf16[2,64,256]{2,1,0:T(8,128)(2,1)S(1)}, u32[]{:S(2)}, u32[]{:S(2)}) collective-permute-start(bf16[2,64,256]{2,1,0:T(8,128)(2,1)S(1)} %get-tuple-element.24), channel_id=1, source_target_pairs={{0,4},{1,5},{2,6},{3,7},{4,0},{5,1},{6,2},{7,3},{8,12},{9,13},{10,... | collective-permute-start | bytes 196616 | tf_op jit(solution)/shard_map/ppermute | solution.py:367
  27.6 5.0 %collective-permute-start.3 = (bf16[2,64,256]{2,1,0:T(8,128)(2,1)S(1)}, bf16[2,64,256]{2,1,0:T(8,128)(2,1)S(1)}, u32[]{:S(2)}, u32[]{:S(2)}) collective-permute-start(bf16[2,64,256]{2,1,0:T(8,128)(2,1)S(1)} %get-tuple-element.21), channel_id=1, source_target_pairs={{0,6},{1,7},{2,0},{3,1},{4,2},{5,3},{6,4},{7,5},{8,14},{9,15},{10,... | collective-permute-start | bytes 196616 | tf_op jit(solution)/shard_map/ppermute | solution.py:367
  30.1 5.8 %copy-start.8 = (bf16[2,64,256]{2,1,0:T(8,128)(2,1)}, bf16[2,64,256]{2,1,0:T(8,128)(2,1)S(1)}, u32[]{:S(2)}) copy-start(bf16[2,64,256]{2,1,0:T(8,128)(2,1)S(1)} %collective-permute-done.1.refs_1_) | copy-start | bytes 196612
  32.6 3.3 %copy-start.9 = (bf16[2,64,256]{2,1,0:T(8,128)(2,1)}, bf16[2,64,256]{2,1,0:T(8,128)(2,1)S(1)}, u32[]{:S(2)}) copy-start(bf16[2,64,256]{2,1,0:T(8,128)(2,1)S(1)} %collective-permute-done.2.refs_2_) | copy-start | bytes 196612
  32.6 3.2 %copy-start.10 = (bf16[2,64,256]{2,1,0:T(8,128)(2,1)}, bf16[2,64,256]{2,1,0:T(8,128)(2,1)S(1)}, u32[]{:S(2)}) copy-start(bf16[2,64,256]{2,1,0:T(8,128)(2,1)S(1)} %collective-permute-done.3.refs_3_) | copy-start | bytes 196612
  35.9 0.9 %copy-start.6 = (bf16[32,40,256]{2,1,0:T(8,128)(2,1)}, bf16[32,40,256]{2,1,0:T(8,128)(2,1)S(1)}, u32[]{:S(2)}) copy-start(bf16[32,40,256]{2,1,0:T(8,128)(2,1)S(1)} %all-to-all-done.leg_ref) | copy-start | bytes 1966084
  39.4 22.0 %all-to-all-start.1 = ((bf16[32,48,128]{2,1,0:T(8,128)(2,1)}), bf16[32,48,128]{2,1,0:T(8,128)(2,1)S(1)}, u32[]{:S(2)}, u32[]{:S(2)}) async-start(bf16[32,48,128]{2,1,0:T(8,128)(2,1)} %order_stage.1), calls=%async_computation.1 | async-start | bytes 786432 | tf_op jit(solution)/shard_map/all_to_all | solution.py:372

commit v4 on v3

--- a/solution.py
+++ b/solution.py
@@ -35,7 +35,7 @@
 NT = (((1,), (1,)), ((), ()))
 TN = (((0,), (0,)), ((), ()))
 VMEM = pltpu.VMEM
-GRANT = 60 << 20
+GRANT = 62 << 20
 PAIR = 2
 TURNS = CHS // PAIR
 LAT_CHUNK = 8
@@ -74,10 +74,11 @@
 
 
 PICK_ROWS = 4
-PICK_AHEAD = 3
+PICK_AHEAD = 4
 GROUPS = ROWS // PICK_ROWS
 PICK_LINES = PICK_ROWS * SUB
 EDGE = 12
+ORDER_LIMITS = (LMAX, LMAX - 2 * LANES)
 
 
 def pick_kernel(slots_ref, leg_ref, out_ref, buf, wide, flat, sems):
@@ -85,29 +86,42 @@
     for g in range(GROUPS):
         rows = pl.ds(g * PICK_ROWS, PICK_ROWS)
         lines = pl.ds(g * PICK_LINES, PICK_LINES)
-        arrivals.append(pltpu.make_async_copy(leg_ref.at[rows], buf.at[rows], sems.at[0, g]))
-        departures.append(pltpu.make_async_copy(flat.at[g], out_ref.at[:, lines, :], sems.at[1, g]))
-    for copy in arrivals[:PICK_AHEAD]:
-        copy.start()
-    line = lax.broadcasted_iota(jnp.int32, (PICKS, LMAX), 0)
-    order = lax.broadcasted_iota(jnp.int32, (PICKS, LMAX), 1)
-    blocks = jnp.zeros((PICKS, LMAX), jnp.int32)
+        pair = []
+        for h in range(STEPS // LANES):
+            part = (rows, pl.ds(h * LANES, LANES), pl.ds(0, ORDER_LIMITS[h]))
+            pair.append(pltpu.make_async_copy(leg_ref.at[part], buf.at[part], sems.at[h, g]))
+        arrivals.append(pair)
+        departures.append(pltpu.make_async_copy(flat.at[g], out_ref.at[:, lines, :], sems.at[2, g]))
+    for pair in arrivals[:PICK_AHEAD]:
+        for copy in pair:
+            copy.start()
+    line = lax.broadcasted_iota(jnp.int32, (PICKS, LANES), 0)
+    lane = lax.broadcasted_iota(jnp.int32, (PICKS, LANES), 1)
+    blocks = jnp.zeros((PICKS, LANES), jnp.int32)
     for i in range(LATS):
         blocks = jnp.where(line % LATS == i, slots_ref[i], blocks)
     wanted = blocks * ORDER_BLOCK + line // LATS + SUB * lax.axis_index("ch")
-    hot = jnp.where(order == wanted, 1.0, 0.0).astype(BF)
+    hot = jnp.concatenate(
+        [
+            jnp.where(lane + n * LANES == wanted, 1.0, 0.0).astype(BF)
+            for n in range(LMAX // LANES)
+        ],
+        axis=1,
+    )
     for g in range(GROUPS):
-        arrivals[g].wait()
-        for copy in arrivals[g + PICK_AHEAD :][:1]:
-            copy.start()
+        for copy in arrivals[g]:
+            copy.wait()
+        for pair in arrivals[g + PICK_AHEAD :][:1]:
+            for copy in pair:
+                copy.start()
         for r in range(PICK_ROWS):
-            picked = lax.dot_general(
-                hot, buf[g * PICK_ROWS + r], NT, preferred_element_type=F32
-            )
-            for t in range(SUB):
-                for h in range(STEPS // LANES):
+            for h in range(STEPS // LANES):
+                limit = ORDER_LIMITS[h]
+                block = buf[g * PICK_ROWS + r, h * LANES : (h + 1) * LANES, :limit]
+                picked = lax.dot_general(hot[:, :limit], block, NT, preferred_element_type=F32)
+                for t in range(SUB):
                     wide[g, h, pl.ds(r * SUB + t, LATS, stride=PICK_LINES), :] = picked[
-                        t * LATS : (t + 1) * LATS, h * LANES : (h + 1) * LANES
+                        t * LATS : (t + 1) * LATS
                     ]
         for h in range(STEPS // LANES):
             flat[g, :, :, h * LANES : (h + 1) * LANES] = (
@@ -128,7 +142,7 @@
             pltpu.VMEM((ROWS, STEPS, LMAX), BF),
             pltpu.VMEM((GROUPS, STEPS // LANES, LATS * PICK_LINES, LANES), F32),
             pltpu.VMEM((GROUPS, LATS, PICK_LINES, STEPS), BF),
-            pltpu.SemaphoreType.DMA((2, GROUPS)),
+            pltpu.SemaphoreType.DMA((3, GROUPS)),
         ],
         compiler_params=pltpu.CompilerParams(vmem_limit_bytes=GRANT),
         cost_estimate=pl.CostEstimate(flops=2 * 64 * 512 * 5120, bytes_accessed=6 << 20, transcendentals=0),
@@ -137,14 +151,16 @@
 
 
 def order_kernel(leg_ref, *refs):
-    pieces_in, (out_ref, raw, specs, full, send, sems) = refs[:TURNS], refs[TURNS:]
+    pieces_in, (out_ref, got, raw, specs, full, send, sems) = refs[:TURNS], refs[TURNS:]
     half = NLAT // 2
     ch_index = lax.axis_index("ch")
     side = lax.rem(ch_index, PAIR)
-    departures = []
+    arrivals, departures = [], []
     for g in range(LATS // LAT_CHUNK):
         part = pl.ds(g * LAT_CHUNK, LAT_CHUNK)
-        departures.append(pltpu.make_async_copy(send.at[part], out_ref.at[part], sems.at[g]))
+        arrivals.append(pltpu.make_async_copy(leg_ref.at[part], got.at[part], sems.at[0, g]))
+        arrivals[-1].start()
+        departures.append(pltpu.make_async_copy(send.at[part], out_ref.at[part], sems.at[1, g]))
     for d in range(TURNS):
         turn = lax.rem(lax.div(ch_index, PAIR) + (TURNS - d), TURNS)
         for q in range(PAIR):
@@ -153,9 +169,13 @@
                 lanes = slice(h * LANES, (h + 1) * LANES)
                 start = pl.multiple_of(source * C, C)
                 specs[h, pl.ds(start, C), :] = pieces_in[d][q, :, lanes].astype(F32)
-    for h in range(STEPS // LANES):
-        lanes = slice(h * LANES, (h + 1) * LANES)
-        raw[h] = leg_ref[:, :, lanes].astype(F32).reshape(LATS * ROWS * SUB, LANES)
+    lines = LAT_CHUNK * ROWS * SUB
+    for g in range(LATS // LAT_CHUNK):
+        arrivals[g].wait()
+        part = got[g * LAT_CHUNK : (g + 1) * LAT_CHUNK]
+        for h in range(STEPS // LANES):
+            lanes = slice(h * LANES, (h + 1) * LANES)
+            raw[h, pl.ds(g * lines, lines), :] = part[:, :, lanes].astype(F32).reshape(lines, LANES)
     rows = lax.broadcasted_iota(jnp.int32, (LANES, LANES), 0)
     cols = lax.broadcasted_iota(jnp.int32, (LANES, LANES), 1)
     turn = jnp.where(rows + cols == LANES - 1, 1.0, 0.0).astype(BF)
@@ -215,14 +235,15 @@
     return pl.pallas_call(
         order_kernel,
         out_shape=jax.ShapeDtypeStruct((LATS, HALO_ROWS * SUB, LANES), BF),
-        in_specs=[pl.BlockSpec(memory_space=VMEM)] * (1 + TURNS),
+        in_specs=[pl.BlockSpec(memory_space=pltpu.HBM)] + [pl.BlockSpec(memory_space=VMEM)] * TURNS,
         out_specs=pl.BlockSpec(memory_space=pltpu.HBM),
         scratch_shapes=[
+            pltpu.VMEM((LATS, SUB * ROWS, STEPS), BF),
             pltpu.VMEM((STEPS // LANES, LATS * SUB * ROWS, LANES), F32),
             pltpu.VMEM((STEPS // LANES, CHS * C, LANES), F32),
             pltpu.VMEM((SUB * NLAT + 2 * EDGE, LANES), F32),
             pltpu.VMEM((LATS, SUB * HALO_ROWS, LANES), BF),
-            pltpu.SemaphoreType.DMA((LATS // LAT_CHUNK,)),
+            pltpu.SemaphoreType.DMA((2, LATS // LAT_CHUNK)),
         ],
         compiler_params=pltpu.CompilerParams(vmem_limit_bytes=GRANT),
         cost_estimate=pl.CostEstimate(flops=700 << 20, bytes_accessed=2 << 20, transcendentals=0),
@@ -326,15 +347,27 @@
     )(block_slots, rows, coefs, mix)
 
 
-def longitude_kernel(rows_ref, table_ref, out_ref):
+LON_PARTS = 4
+
+
+def longitude_kernel(rows_ref, table_ref, out_ref, field, whole, sems):
     even = jnp.concatenate([rows_ref[j] for j in range(CHS)], axis=1)
     lane = lax.broadcasted_iota(jnp.int32, even.shape, 1)
     flipped = jnp.where(lane % PICKS < BLOCKS, even.astype(F32), -even.astype(F32)).astype(BF)
     both = jnp.concatenate([even, flipped], axis=0)
-    field = jnp.dot(both, table_ref[...], preferred_element_type=F32)
-    count = OWN * ROWS
-    whole = jnp.concatenate([field[:count], field[count:]], axis=1)
-    out_ref[...] = whole.astype(BF).reshape(ROWS, OWN, NLON)
+    field[...] = jnp.dot(both, table_ref[...], preferred_element_type=F32)
+    count, rows = OWN * ROWS, ROWS // LON_PARTS
+    lines = rows * OWN
+    departures = []
+    for g in range(LON_PARTS):
+        first = field[g * lines : (g + 1) * lines]
+        second = field[count + g * lines : count + (g + 1) * lines]
+        part = pl.ds(g * rows, rows)
+        whole[part] = jnp.concatenate([first, second], axis=1).astype(BF).reshape(rows, OWN, NLON)
+        departures.append(pltpu.make_async_copy(whole.at[part], out_ref.at[part], sems.at[g]))
+        departures[-1].start()
+    for copy in departures:
+        copy.wait()
 
 
 def longitude_stage(rows, table):
@@ -342,7 +375,12 @@
         longitude_kernel,
         out_shape=jax.ShapeDtypeStruct((ROWS, OWN, NLON), BF),
         in_specs=[pl.BlockSpec(memory_space=VMEM)] * 2,
-        out_specs=pl.BlockSpec(memory_space=VMEM),
+        out_specs=pl.BlockSpec(memory_space=pltpu.HBM),
+        scratch_shapes=[
+            pltpu.VMEM((2 * OWN * ROWS, HALF_LON), F32),
+            pltpu.VMEM((ROWS, OWN, NLON), BF),
+            pltpu.SemaphoreType.DMA((LON_PARTS,)),
+        ],
         compiler_params=pltpu.CompilerParams(vmem_limit_bytes=40 << 20),
         cost_estimate=pl.CostEstimate(flops=480 << 20, bytes_accessed=4 << 20, transcendentals=0),
         name="longitude_stage",

time: 80.8 us -> 81.8 us (1.012)
  starting transfers between devices: 23.7 us -> 24.8 us
  waiting for transfers between devices: 27.4 us -> 26.5 us
    reshape x1, local copies, waits for them, and re-layouts: 0.1 us -> 1.05 us  [per_device(): blocks = spectrum.reshape(TURNS, PAIR, C, STEPS)]
    all_to_all x1, starting transfers between devices: 6.07 us -> 7 us  [per_device(): by_row = lax.all_to_all(by_order, 'lat', 0, 0, tiled=True)]
    pallas_call x1, Pallas kernels: 2.69 us -> 3.57 us  [order_stage(): pl.pallas_call(order_kernel, out_shape=jax.ShapeDtypeStruct((LATS, HALO_R...]
    unnamed x22 -> x18, local copies, waits for them, and re-layouts: 0.89 us -> 0.04 us
  transfers between devices with their start and end apart: 6 -> 6, of which waited for: 4 -> 4; matrix products, arithmetic and copies ran while one was open for 1% -> 2% of each run, Pallas kernels for 1% -> 1%
where the time goes in v4:
time: 81.8 us; the launch traced here: 81.3 us
  waiting for transfers between devices  26.5 us (32%)
  starting transfers between devices  24.8 us (30%)
  blocking collectives  15 us (18%)
  Pallas kernels  13.2 us (16%)
  local copies, waits for them, and re-layouts  1.12 us (1%)
    all_to_all x1, waiting for transfers between devices, per_device(): by_row = lax.all_to_all(by_order, 'lat', 0, 0, tiled=True)  15.3 us
    all_to_all x1, blocking collectives, per_device(): own = lax.all_to_all(mixed, 'ch', 0, 0, tiled=True)  15 us
    all_to_all x1, starting transfers between devices, per_device(): leg = lax.all_to_all(picked, 'lat', 0, 0, tiled=True)  10 us
    all_to_all x1, starting transfers between devices, per_device(): by_row = lax.all_to_all(by_order, 'lat', 0, 0, tiled=True)  7 us
    ppermute x1, waiting for transfers between devices, per_device(): taken = lax.ppermute(given, 'ch', [(j, j ^ 1) for j in range(CHS)])  6.13 us
    ppermute x3, starting transfers between devices, per_device(): pieces.append(lax.ppermute(piece, 'ch', shift) if d else piece)  4.92 us
    pallas_call x1, Pallas kernels, pick(): pl.pallas_call(pick_kernel, out_shape=jax.ShapeDtypeStruct((LATS, ROWS *...  4.79 us
    pallas_call x1, Pallas kernels, order_stage(): pl.pallas_call(order_kernel, out_shape=jax.ShapeDtypeStruct((LATS, HALO_R...  3.57 us
  transfers between devices with their start and end apart: 6, of which 4 were waited for; matrix products, arithmetic and copies ran while one was open for 2% of the time, Pallas kernels for 1%

profile of v4, /device:TPU:8, one launch (start us, length us, event | category | flops | bytes accessed | tf_op | source)
XLA Modules:
  0.0 81.3 jit_solution(8240313328277452199)
XLA Ops:
  0.0 0.0 copy-start.4
  0.0 0.0 copy-start.3
  0.0 4.8 %pick.1 = bf16[32,40,256]{2,1,0:T(8,128)(2,1)} custom-call(s32[32]{0:T(128)} %slots_ref.3, bf16[20,256,512]{2,1,0:T(8,128)(2,1)} %leg_ref.1), custom_call_target="tpu_custom_call" | custom-call | flops 335544320 | bytes 6291456 | tf_op jit(solution)/shard_map/pick/pallas_call | solution.py:136
  4.8 0.0 copy-start
  4.8 10.0 %all-to-all-start = ((bf16[32,40,256]{2,1,0:T(8,128)(2,1)}), bf16[32,40,256]{2,1,0:T(8,128)(2,1)}, u32[]{:S(2)}, u32[]{:S(2)}) async-start(bf16[32,40,256]{2,1,0:T(8,128)(2,1)} %pick.1), calls=%async_computation | async-start | bytes 1310720 | tf_op jit(solution)/shard_map/all_to_all | solution.py:394
  14.9 1.1 %reshape.3 = bf16[4,2,64,256]{3,2,1,0:T(8,128)(2,1)S(1)} reshape(bf16[16,8,2,2,256]{4,3,2,1,0:T(2,128)(2,1)} %param.8) | data formatting | bytes 524288 | tf_op jit(solution)/shard_map/reshape | solution.py:395
  16.0 2.8 %collective-permute-start = (bf16[4,64,256]{2,1,0:T(8,128)(2,1)S(1)}, bf16[4,64,256]{2,1,0:T(8,128)(2,1)S(1)}, u32[]{:S(2)}, u32[]{:S(2)}) collective-permute-start(bf16[4,64,256]{2,1,0:T(8,128)(2,1)S(1)} %get-tuple-element.25), channel_id=1, source_target_pairs={{0,1},{1,0},{2,3},{3,2},{4,5},{5,4},{6,7},{7,6},{8,9},{9,8},{10,11... | collective-permute-start | bytes 393224 | tf_op jit(solution)/shard_map/ppermute | solution.py:399
  18.8 6.1 %collective-permute-done = bf16[4,64,256]{2,1,0:T(8,128)(2,1)S(1)} collective-permute-done((bf16[4,64,256]{2,1,0:T(8,128)(2,1)S(1)}, bf16[4,64,256]{2,1,0:T(8,128)(2,1)S(1)}, u32[]{:S(2)}, u32[]{:S(2)}) %collective-permute-start) | collective-permute-done | bytes 131104 | tf_op jit(solution)/shard_map/ppermute | solution.py:399
  25.0 0.6 fusion.1
  25.6 1.6 %collective-permute-start.1 = (bf16[2,64,256]{2,1,0:T(8,128)(2,1)S(1)}, bf16[2,64,256]{2,1,0:T(8,128)(2,1)S(1)}, u32[]{:S(2)}, u32[]{:S(2)}) collective-permute-start(bf16[2,64,256]{2,1,0:T(8,128)(2,1)S(1)} %get-tuple-element.23), channel_id=1, source_target_pairs={{0,2},{1,3},{2,4},{3,5},{4,6},{5,7},{6,0},{7,1},{8,10},{9,11},{10,... | collective-permute-start | bytes 196616 | tf_op jit(solution)/shard_map/ppermute | solution.py:405
  27.2 0.9 %collective-permute-start.2 = (bf16[2,64,256]{2,1,0:T(8,128)(2,1)S(1)}, bf16[2,64,256]{2,1,0:T(8,128)(2,1)S(1)}, u32[]{:S(2)}, u32[]{:S(2)}) collective-permute-start(bf16[2,64,256]{2,1,0:T(8,128)(2,1)S(1)} %get-tuple-element.24), channel_id=1, source_target_pairs={{0,4},{1,5},{2,6},{3,7},{4,0},{5,1},{6,2},{7,3},{8,12},{9,13},{10,... | collective-permute-start | bytes 196616 | tf_op jit(solution)/shard_map/ppermute | solution.py:405
  28.1 2.4 %collective-permute-start.3 = (bf16[2,64,256]{2,1,0:T(8,128)(2,1)S(1)}, bf16[2,64,256]{2,1,0:T(8,128)(2,1)S(1)}, u32[]{:S(2)}, u32[]{:S(2)}) collective-permute-start(bf16[2,64,256]{2,1,0:T(8,128)(2,1)S(1)} %get-tuple-element.21), channel_id=1, source_target_pairs={{0,6},{1,7},{2,0},{3,1},{4,2},{5,3},{6,4},{7,5},{8,14},{9,15},{10,... | collective-permute-start | bytes 196616 | tf_op jit(solution)/shard_map/ppermute | solution.py:405
  30.5 0.0 collective-permute-done.1.refs_1_
  30.5 2.5 %collective-permute-done.2.refs_2_ = bf16[2,64,256]{2,1,0:T(8,128)(2,1)S(1)} collective-permute-done((bf16[2,64,256]{2,1,0:T(8,128)(2,1)S(1)}, bf16[2,64,256]{2,1,0:T(8,128)(2,1)S(1)}, u32[]{:S(2)}, u32[]{:S(2)}) %collective-permute-start.2) | collective-permute-done | bytes 65568 | tf_op jit(solution)/shard_map/ppermute | solution.py:405
  33.1 0.0 collective-permute-done.3.refs_3_
  33.1 2.5 %all-to-all-done.leg_ref = bf16[32,40,256]{2,1,0:T(8,128)(2,1)} async-done(((bf16[32,40,256]{2,1,0:T(8,128)(2,1)}), bf16[32,40,256]{2,1,0:T(8,128)(2,1)}, u32[]{:S(2)}, u32[]{:S(2)}) %all-to-all-start) | async-done | bytes 655392 | tf_op jit(solution)/shard_map/all_to_all | solution.py:394
  35.7 3.6 %order_stage.1 = bf16[32,48,128]{2,1,0:T(8,128)(2,1)} custom-call(bf16[32,40,256]{2,1,0:T(8,128)(2,1)} %all-to-all-done.leg_ref, bf16[2,64,256]{2,1,0:T(8,128)(2,1)} %get-tuple-element.22.refs_0_, bf16[2,64,256]{2,1,0:T(8,128)(2,1)} %copy-done.6, bf16[2,64,256]{2,1,0:T(8,128)(2,1)} %copy-done.7, bf16[2,64,256]{2,1,0:T(8,128)(2,1)} %copy-done.8), custom_call_target="tpu_custom_call" | custom-call | flops 734003200 | bytes 2097152 | tf_op jit(solution)/shard_map/order_stage/pallas_call | solution.py:235
  39.2 7.0 %all-to-all-start.1 = ((bf16[32,48,128]{2,1,0:T(8,128)(2,1)}), bf16[32,48,128]{2,1,0:T(8,128)(2,1)S(1)}, u32[]{:S(2)}, u32[]{:S(2)}) async-start(bf16[32,48,128]{2,1,0:T(8,128)(2,1)} %order_stage.1), calls=%async_computation.1 | async-start | bytes 786432 | tf_op jit(solution)/shard_map/all_to_all | solution.py:410
  46.2 0.0 copy-done.1
  46.3 0.6 coef_stage.1
  46.9 15.3 %all-to-all-done.1.rows_ref = bf16[32,48,128]{2,1,0:T(8,128)(2,1)S(1)} async-done(((bf16[32,48,128]{2,1,0:T(8,128)(2,1)}), bf16[32,48,128]{2,1,0:T(8,128)(2,1)S(1)}, u32[]{:S(2)}, u32[]{:S(2)}) %all-to-all-start.1) | async-done | bytes 393248 | tf_op jit(solution)/shard_map/all_to_all | solution.py:410
  62.1 2.7 %row_stage.1 = bf16[8,160,128]{2,1,0:T(8,128)(2,1)S(1)} custom-call(s32[32]{0:T(128)S(1)} %copy-done.5, bf16[32,48,128]{2,1,0:T(8,128)(2,1)S(1)} %all-to-all-done.1.rows_ref, f32[15,20,256]{2,1,0:T(8,128)S(1)} %get-tuple-element.19.coef_ref, bf16[64,384]{1,0:T(8,128)(2,1)S(1)} %get-tuple-element.20.mix_ref), custom_call_target="tpu_custom_call" | custom-call | flops 209715200 | bytes 2097152 | tf_op jit(solution)/shard_map/row_stage/pallas_call | solution.py:329
  64.8 15.0 %all_to_all.15.rows_ref = bf16[8,160,128]{2,1,0:T(8,128)(2,1)S(1)} all-to-all(bf16[8,160,128]{2,1,0:T(8,128)(2,1)S(1)} %row_stage.1), channel_id=1, replica_groups=mesh['lat'=32,'ch'=8] {'ch'}, dimensions={0} | all-to-all | bytes 655360 | tf_op jit(solution)/shard_map/all_to_all | solution.py:413
  79.8 1.6 %longitude_stage.1 = bf16[20,8,1440]{2,1,0:T(8,128)(2,1)} custom-call(bf16[8,160,128]{2,1,0:T(8,128)(2,1)S(1)} %all_to_all.15.rows_ref, bf16[1024,720]{1,0:T(8,128)(2,1)S(1)} %copy-done), custom_call_target="tpu_custom_call" | custom-call | flops 503316480 | bytes 4194304 | tf_op jit(solution)/shard_map/longitude_stage/pallas_call | solution.py:374
  (15 shorter events, 0.1 us)
Async XLA Ops:
  0.0 46.2 %copy-start.1 = (f32[8,16,256]{2,1,0:T(8,128)S(1)}, f32[8,16,256]{2,1,0:T(8,128)}, u32[]{:S(2)}) copy-start(f32[8,16,256]{2,1,0:T(8,128)} %constant.73.clone.waves_ref) | copy-start | bytes 393220
  0.0 62.1 %copy-start.5 = (s32[32]{0:T(128)S(1)}, s32[32]{0:T(128)}, u32[]{:S(2)}) copy-start(s32[32]{0:T(128)} %slots_ref.3) | copy-start | bytes 388
  0.0 46.3 %copy-start.2 = (bf16[3,20,6,9]{1,2,3,0:T(8,128)(2,1)S(1)}, bf16[3,20,6,9]{1,2,3,0:T(8,128)(2,1)}, u32[]{:S(2)}) copy-start(bf16[3,20,6,9]{1,2,3,0:T(8,128)(2,1)} %param.11) | copy-start | bytes 19444
  0.0 46.3 %copy-start.4 = (s32[20,6]{0,1:T(8,128)S(1)}, s32[20,6]{0,1:T(8,128)}, u32[]{:S(2)}) copy-start(s32[20,6]{0,1:T(8,128)} %param.12) | copy-start | bytes 1444
  0.0 46.3 %copy-start.3 = (bf16[3,64,64]{2,1,0:T(8,128)(2,1)S(1)}, bf16[3,64,64]{2,1,0:T(8,128)(2,1)}, u32[]{:S(2)}) copy-start(bf16[3,64,64]{2,1,0:T(8,128)(2,1)} %mix_ref) | copy-start | bytes 73732
  4.8 75.0 %copy-start = (bf16[1024,720]{1,0:T(8,128)(2,1)S(1)}, bf16[1024,720]{1,0:T(8,128)(2,1)}, u32[]{:S(2)}) copy-start(bf16[1024,720]{1,0:T(8,128)(2,1)} %constant.74.clone.table_ref) | copy-start | bytes 4423684
  4.8 30.8 %all-to-all-start = ((bf16[32,40,256]{2,1,0:T(8,128)(2,1)}), bf16[32,40,256]{2,1,0:T(8,128)(2,1)}, u32[]{:S(2)}, u32[]{:S(2)}) async-start(bf16[32,40,256]{2,1,0:T(8,128)(2,1)} %pick.1), calls=%async_computation | async-start | bytes 1310720 | tf_op jit(solution)/shard_map/all_to_all | solution.py:394
  16.0 9.0 %collective-permute-start = (bf16[4,64,256]{2,1,0:T(8,128)(2,1)S(1)}, bf16[4,64,256]{2,1,0:T(8,128)(2,1)S(1)}, u32[]{:S(2)}, u32[]{:S(2)}) collective-permute-start(bf16[4,64,256]{2,1,0:T(8,128)(2,1)S(1)} %get-tuple-element.25), channel_id=1, source_target_pairs={{0,1},{1,0},{2,3},{3,2},{4,5},{5,4},{6,7},{7,6},{8,9},{9,8},{10,11... | collective-permute-start | bytes 393224 | tf_op jit(solution)/shard_map/ppermute | solution.py:399
  25.6 4.9 %collective-permute-start.1 = (bf16[2,64,256]{2,1,0:T(8,128)(2,1)S(1)}, bf16[2,64,256]{2,1,0:T(8,128)(2,1)S(1)}, u32[]{:S(2)}, u32[]{:S(2)}) collective-permute-start(bf16[2,64,256]{2,1,0:T(8,128)(2,1)S(1)} %get-tuple-element.23), channel_id=1, source_target_pairs={{0,2},{1,3},{2,4},{3,5},{4,6},{5,7},{6,0},{7,1},{8,10},{9,11},{10,... | collective-permute-start | bytes 196616 | tf_op jit(solution)/shard_map/ppermute | solution.py:405
  27.2 5.9 %collective-permute-start.2 = (bf16[2,64,256]{2,1,0:T(8,128)(2,1)S(1)}, bf16[2,64,256]{2,1,0:T(8,128)(2,1)S(1)}, u32[]{:S(2)}, u32[]{:S(2)}) collective-permute-start(bf16[2,64,256]{2,1,0:T(8,128)(2,1)S(1)} %get-tuple-element.24), channel_id=1, source_target_pairs={{0,4},{1,5},{2,6},{3,7},{4,0},{5,1},{6,2},{7,3},{8,12},{9,13},{10,... | collective-permute-start | bytes 196616 | tf_op jit(solution)/shard_map/ppermute | solution.py:405
  28.1 5.0 %collective-permute-start.3 = (bf16[2,64,256]{2,1,0:T(8,128)(2,1)S(1)}, bf16[2,64,256]{2,1,0:T(8,128)(2,1)S(1)}, u32[]{:S(2)}, u32[]{:S(2)}) collective-permute-start(bf16[2,64,256]{2,1,0:T(8,128)(2,1)S(1)} %get-tuple-element.21), channel_id=1, source_target_pairs={{0,6},{1,7},{2,0},{3,1},{4,2},{5,3},{6,4},{7,5},{8,14},{9,15},{10,... | collective-permute-start | bytes 196616 | tf_op jit(solution)/shard_map/ppermute | solution.py:405
  30.5 5.1 %copy-start.6 = (bf16[2,64,256]{2,1,0:T(8,128)(2,1)}, bf16[2,64,256]{2,1,0:T(8,128)(2,1)S(1)}, u32[]{:S(2)}) copy-start(bf16[2,64,256]{2,1,0:T(8,128)(2,1)S(1)} %collective-permute-done.1.refs_1_) | copy-start | bytes 196612
  33.1 2.6 %copy-start.7 = (bf16[2,64,256]{2,1,0:T(8,128)(2,1)}, bf16[2,64,256]{2,1,0:T(8,128)(2,1)S(1)}, u32[]{:S(2)}) copy-start(bf16[2,64,256]{2,1,0:T(8,128)(2,1)S(1)} %collective-permute-done.2.refs_2_) | copy-start | bytes 196612
  33.1 2.6 %copy-start.8 = (bf16[2,64,256]{2,1,0:T(8,128)(2,1)}, bf16[2,64,256]{2,1,0:T(8,128)(2,1)S(1)}, u32[]{:S(2)}) copy-start(bf16[2,64,256]{2,1,0:T(8,128)(2,1)S(1)} %collective-permute-done.3.refs_3_) | copy-start | bytes 196612
  39.2 22.9 %all-to-all-start.1 = ((bf16[32,48,128]{2,1,0:T(8,128)(2,1)}), bf16[32,48,128]{2,1,0:T(8,128)(2,1)S(1)}, u32[]{:S(2)}, u32[]{:S(2)}) async-start(bf16[32,48,128]{2,1,0:T(8,128)(2,1)} %order_stage.1), calls=%async_computation.1 | async-start | bytes 786432 | tf_op jit(solution)/shard_map/all_to_all | solution.py:410

commit v5 on v4

--- a/solution.py
+++ b/solution.py
@@ -38,7 +38,6 @@
 GRANT = 62 << 20
 PAIR = 2
 TURNS = CHS // PAIR
-LAT_CHUNK = 8
 
 
 HALF_LON = NLON // 2
@@ -151,16 +150,10 @@
 
 
 def order_kernel(leg_ref, *refs):
-    pieces_in, (out_ref, got, raw, specs, full, send, sems) = refs[:TURNS], refs[TURNS:]
+    pieces_in, (out_ref, raw, specs, full) = refs[:TURNS], refs[TURNS:]
     half = NLAT // 2
     ch_index = lax.axis_index("ch")
     side = lax.rem(ch_index, PAIR)
-    arrivals, departures = [], []
-    for g in range(LATS // LAT_CHUNK):
-        part = pl.ds(g * LAT_CHUNK, LAT_CHUNK)
-        arrivals.append(pltpu.make_async_copy(leg_ref.at[part], got.at[part], sems.at[0, g]))
-        arrivals[-1].start()
-        departures.append(pltpu.make_async_copy(send.at[part], out_ref.at[part], sems.at[1, g]))
     for d in range(TURNS):
         turn = lax.rem(lax.div(ch_index, PAIR) + (TURNS - d), TURNS)
         for q in range(PAIR):
@@ -169,13 +162,9 @@
                 lanes = slice(h * LANES, (h + 1) * LANES)
                 start = pl.multiple_of(source * C, C)
                 specs[h, pl.ds(start, C), :] = pieces_in[d][q, :, lanes].astype(F32)
-    lines = LAT_CHUNK * ROWS * SUB
-    for g in range(LATS // LAT_CHUNK):
-        arrivals[g].wait()
-        part = got[g * LAT_CHUNK : (g + 1) * LAT_CHUNK]
-        for h in range(STEPS // LANES):
-            lanes = slice(h * LANES, (h + 1) * LANES)
-            raw[h, pl.ds(g * lines, lines), :] = part[:, :, lanes].astype(F32).reshape(lines, LANES)
+    for h in range(STEPS // LANES):
+        lanes = slice(h * LANES, (h + 1) * LANES)
+        raw[h] = leg_ref[:, :, lanes].astype(F32).reshape(LATS * ROWS * SUB, LANES)
     rows = lax.broadcasted_iota(jnp.int32, (LANES, LANES), 0)
     cols = lax.broadcasted_iota(jnp.int32, (LANES, LANES), 1)
     turn = jnp.where(rows + cols == LANES - 1, 1.0, 0.0).astype(BF)
@@ -224,28 +213,21 @@
         full[pl.ds(EDGE + t + SUB * half, half, stride=SUB), :] = south
     for i in range(LATS):
         start = EDGE - REACH * SUB + i * ROWS * SUB
-        send[i] = full[start : start + HALO_ROWS * SUB, :].astype(BF)
-        if i % LAT_CHUNK == LAT_CHUNK - 1:
-            departures[i // LAT_CHUNK].start()
-    for copy in departures:
-        copy.wait()
+        out_ref[i] = full[start : start + HALO_ROWS * SUB, :].astype(BF)
 
 
 def order_stage(leg, pieces):
     return pl.pallas_call(
         order_kernel,
         out_shape=jax.ShapeDtypeStruct((LATS, HALO_ROWS * SUB, LANES), BF),
-        in_specs=[pl.BlockSpec(memory_space=pltpu.HBM)] + [pl.BlockSpec(memory_space=VMEM)] * TURNS,
-        out_specs=pl.BlockSpec(memory_space=pltpu.HBM),
+        in_specs=[pl.BlockSpec(memory_space=VMEM)] * (1 + TURNS),
+        out_specs=pl.BlockSpec(memory_space=VMEM),
         scratch_shapes=[
-            pltpu.VMEM((LATS, SUB * ROWS, STEPS), BF),
             pltpu.VMEM((STEPS // LANES, LATS * SUB * ROWS, LANES), F32),
             pltpu.VMEM((STEPS // LANES, CHS * C, LANES), F32),
             pltpu.VMEM((SUB * NLAT + 2 * EDGE, LANES), F32),
-            pltpu.VMEM((LATS, SUB * HALO_ROWS, LANES), BF),
-            pltpu.SemaphoreType.DMA((2, LATS // LAT_CHUNK)),
-        ],
-        compiler_params=pltpu.CompilerParams(vmem_limit_bytes=GRANT),
+        ],
+        compiler_params=pltpu.CompilerParams(vmem_limit_bytes=24 << 20),
         cost_estimate=pl.CostEstimate(flops=700 << 20, bytes_accessed=2 << 20, transcendentals=0),
         name="order_stage",
     )(leg, *pieces)

time: 81.8 us -> 78 us (0.954)
  Pallas kernels: 13.2 us -> 11.2 us
  starting transfers between devices: 24.8 us -> 23.2 us
  waiting for transfers between devices: 26.5 us -> 28 us
  local copies, waits for them, and re-layouts: 1.12 us -> 0.16 us
    pallas_call x1, Pallas kernels: 3.57 us -> 1.59 us  [order_stage(): pl.pallas_call(order_kernel, out_shape=jax.ShapeDtypeStruct((LATS, HALO_R...]
    all_to_all x1, starting transfers between devices: 7 us -> 5.5 us  [per_device(): by_row = lax.all_to_all(by_order, 'lat', 0, 0, tiled=True)]
    all_to_all x1, waiting for transfers between devices: 2.55 us -> 3.77 us  [per_device(): leg = lax.all_to_all(picked, 'lat', 0, 0, tiled=True)]
    reshape x1, local copies, waits for them, and re-layouts: 1.05 us -> 0.1 us  [per_device(): blocks = spectrum.reshape(TURNS, PAIR, C, STEPS)]
  transfers between devices with their start and end apart: 6 -> 6, of which waited for: 4 -> 4; matrix products, arithmetic and copies ran while one was open for 2% -> 0% of each run, Pallas kernels for 1% -> 1%
where the time goes in v5:
time: 78 us; the launch traced here: 77.7 us
  waiting for transfers between devices  28 us (36%)
  starting transfers between devices  23.2 us (30%)
  blocking collectives  14.9 us (19%)
  Pallas kernels  11.2 us (14%)
    all_to_all x1, waiting for transfers between devices, per_device(): by_row = lax.all_to_all(by_order, 'lat', 0, 0, tiled=True)  15.2 us
    all_to_all x1, blocking collectives, per_device(): own = lax.all_to_all(mixed, 'ch', 0, 0, tiled=True)  14.9 us
    all_to_all x1, starting transfers between devices, per_device(): leg = lax.all_to_all(picked, 'lat', 0, 0, tiled=True)  9.92 us
    ppermute x1, waiting for transfers between devices, per_device(): taken = lax.ppermute(given, 'ch', [(j, j ^ 1) for j in range(CHS)])  6.4 us
    all_to_all x1, starting transfers between devices, per_device(): by_row = lax.all_to_all(by_order, 'lat', 0, 0, tiled=True)  5.5 us
    ppermute x3, starting transfers between devices, per_device(): pieces.append(lax.ppermute(piece, 'ch', shift) if d else piece)  5 us
    pallas_call x1, Pallas kernels, pick(): pl.pallas_call(pick_kernel, out_shape=jax.ShapeDtypeStruct((LATS, ROWS *...  4.81 us
    all_to_all x1, waiting for transfers between devices, per_device(): leg = lax.all_to_all(picked, 'lat', 0, 0, tiled=True)  3.77 us
  transfers between devices with their start and end apart: 6, of which 4 were waited for; matrix products, arithmetic and copies ran while one was open for 0% of the time, Pallas kernels for 1%

profile of v5, /device:TPU:8, one launch (start us, length us, event | category | flops | bytes accessed | tf_op | source)
XLA Modules:
  0.0 77.7 jit_solution(1591053677954292948)
XLA Ops:
  0.0 0.0 copy-start.2
  0.0 0.0 copy-start.4
  0.0 0.0 copy-start.3
  0.0 4.8 %pick.1 = bf16[32,40,256]{2,1,0:T(8,128)(2,1)} custom-call(s32[32]{0:T(128)} %slots_ref.3, bf16[20,256,512]{2,1,0:T(8,128)(2,1)} %leg_ref.1), custom_call_target="tpu_custom_call" | custom-call | flops 335544320 | bytes 6291456 | tf_op jit(solution)/shard_map/pick/pallas_call | solution.py:135
  4.9 0.0 copy-start
  4.9 9.9 %all-to-all-start = ((bf16[32,40,256]{2,1,0:T(8,128)(2,1)}), bf16[32,40,256]{2,1,0:T(8,128)(2,1)S(1)}, u32[]{:S(2)}, u32[]{:S(2)}) async-start(bf16[32,40,256]{2,1,0:T(8,128)(2,1)} %pick.1), calls=%async_computation | async-start | bytes 1310720 | tf_op jit(solution)/shard_map/all_to_all | solution.py:376
  14.8 0.0 copy-done.6
  14.8 0.1 reshape.3
  15.0 2.8 %collective-permute-start = (bf16[4,64,256]{2,1,0:T(8,128)(2,1)S(1)}, bf16[4,64,256]{2,1,0:T(8,128)(2,1)S(1)}, u32[]{:S(2)}, u32[]{:S(2)}) collective-permute-start(bf16[4,64,256]{2,1,0:T(8,128)(2,1)S(1)} %get-tuple-element.25), channel_id=1, source_target_pairs={{0,1},{1,0},{2,3},{3,2},{4,5},{5,4},{6,7},{7,6},{8,9},{9,8},{10,11... | collective-permute-start | bytes 393224 | tf_op jit(solution)/shard_map/ppermute | solution.py:381
  17.8 6.4 %collective-permute-done = bf16[4,64,256]{2,1,0:T(8,128)(2,1)S(1)} collective-permute-done((bf16[4,64,256]{2,1,0:T(8,128)(2,1)S(1)}, bf16[4,64,256]{2,1,0:T(8,128)(2,1)S(1)}, u32[]{:S(2)}, u32[]{:S(2)}) %collective-permute-start) | collective-permute-done | bytes 131104 | tf_op jit(solution)/shard_map/ppermute | solution.py:381
  24.2 1.7 %collective-permute-start.1 = (bf16[2,64,256]{2,1,0:T(8,128)(2,1)S(1)}, bf16[2,64,256]{2,1,0:T(8,128)(2,1)S(1)}, u32[]{:S(2)}, u32[]{:S(2)}) collective-permute-start(bf16[2,64,256]{2,1,0:T(8,128)(2,1)S(1)} %get-tuple-element.23), channel_id=1, source_target_pairs={{0,2},{1,3},{2,4},{3,5},{4,6},{5,7},{6,0},{7,1},{8,10},{9,11},{10,... | collective-permute-start | bytes 196616 | tf_op jit(solution)/shard_map/ppermute | solution.py:387
  25.9 0.9 %collective-permute-start.2 = (bf16[2,64,256]{2,1,0:T(8,128)(2,1)S(1)}, bf16[2,64,256]{2,1,0:T(8,128)(2,1)S(1)}, u32[]{:S(2)}, u32[]{:S(2)}) collective-permute-start(bf16[2,64,256]{2,1,0:T(8,128)(2,1)S(1)} %get-tuple-element.24), channel_id=1, source_target_pairs={{0,4},{1,5},{2,6},{3,7},{4,0},{5,1},{6,2},{7,3},{8,12},{9,13},{10,... | collective-permute-start | bytes 196616 | tf_op jit(solution)/shard_map/ppermute | solution.py:387
  26.8 2.4 %collective-permute-start.3 = (bf16[2,64,256]{2,1,0:T(8,128)(2,1)S(1)}, bf16[2,64,256]{2,1,0:T(8,128)(2,1)S(1)}, u32[]{:S(2)}, u32[]{:S(2)}) collective-permute-start(bf16[2,64,256]{2,1,0:T(8,128)(2,1)S(1)} %get-tuple-element.21), channel_id=1, source_target_pairs={{0,6},{1,7},{2,0},{3,1},{4,2},{5,3},{6,4},{7,5},{8,14},{9,15},{10,... | collective-permute-start | bytes 196616 | tf_op jit(solution)/shard_map/ppermute | solution.py:387
  29.2 0.0 collective-permute-done.1.refs_1_
  29.2 2.5 %collective-permute-done.2.refs_2_ = bf16[2,64,256]{2,1,0:T(8,128)(2,1)S(1)} collective-permute-done((bf16[2,64,256]{2,1,0:T(8,128)(2,1)S(1)}, bf16[2,64,256]{2,1,0:T(8,128)(2,1)S(1)}, u32[]{:S(2)}, u32[]{:S(2)}) %collective-permute-start.2) | collective-permute-done | bytes 65568 | tf_op jit(solution)/shard_map/ppermute | solution.py:387
  31.8 0.0 collective-permute-done.3.refs_3_
  31.8 3.8 %all-to-all-done.leg_ref = bf16[32,40,256]{2,1,0:T(8,128)(2,1)S(1)} async-done(((bf16[32,40,256]{2,1,0:T(8,128)(2,1)}), bf16[32,40,256]{2,1,0:T(8,128)(2,1)S(1)}, u32[]{:S(2)}, u32[]{:S(2)}) %all-to-all-start) | async-done | bytes 655392 | tf_op jit(solution)/shard_map/all_to_all | solution.py:376
  35.6 1.6 %order_stage.1 = bf16[32,48,128]{2,1,0:T(8,128)(2,1)} custom-call(bf16[32,40,256]{2,1,0:T(8,128)(2,1)S(1)} %all-to-all-done.leg_ref, bf16[2,64,256]{2,1,0:T(8,128)(2,1)S(1)} %get-tuple-element.22.refs_0_, bf16[2,64,256]{2,1,0:T(8,128)(2,1)S(1)} %collective-permute-done.1.refs_1_, bf16[2,64,256]{2,1,0:T(8,128)(2,1)S(1)} %collective-permute-done.2.refs_2_, ...), custom_call_target="tpu_custom_call" | custom-call | flops 734003200 | bytes 2097152 | tf_op jit(solution)/shard_map/order_stage/pallas_call | solution.py:220
  37.1 5.5 %all-to-all-start.1 = ((bf16[32,48,128]{2,1,0:T(8,128)(2,1)}), bf16[32,48,128]{2,1,0:T(8,128)(2,1)S(1)}, u32[]{:S(2)}, u32[]{:S(2)}) async-start(bf16[32,48,128]{2,1,0:T(8,128)(2,1)} %order_stage.1), calls=%async_computation.1 | async-start | bytes 786432 | tf_op jit(solution)/shard_map/all_to_all | solution.py:392
  42.7 0.6 coef_stage.1
  43.3 15.2 %all-to-all-done.1.rows_ref = bf16[32,48,128]{2,1,0:T(8,128)(2,1)S(1)} async-done(((bf16[32,48,128]{2,1,0:T(8,128)(2,1)}), bf16[32,48,128]{2,1,0:T(8,128)(2,1)S(1)}, u32[]{:S(2)}, u32[]{:S(2)}) %all-to-all-start.1) | async-done | bytes 393248 | tf_op jit(solution)/shard_map/all_to_all | solution.py:392
  58.5 2.7 %row_stage.1 = bf16[8,160,128]{2,1,0:T(8,128)(2,1)S(1)} custom-call(s32[32]{0:T(128)S(1)} %copy-done.5, bf16[32,48,128]{2,1,0:T(8,128)(2,1)S(1)} %all-to-all-done.1.rows_ref, f32[15,20,256]{2,1,0:T(8,128)S(1)} %get-tuple-element.19.coef_ref, bf16[64,384]{1,0:T(8,128)(2,1)S(1)} %get-tuple-element.20.mix_ref), custom_call_target="tpu_custom_call" | custom-call | flops 209715200 | bytes 2097152 | tf_op jit(solution)/shard_map/row_stage/pallas_call | solution.py:311
  61.2 14.9 %all_to_all.15.rows_ref = bf16[8,160,128]{2,1,0:T(8,128)(2,1)S(1)} all-to-all(bf16[8,160,128]{2,1,0:T(8,128)(2,1)S(1)} %row_stage.1), channel_id=1, replica_groups=mesh['lat'=32,'ch'=8] {'ch'}, dimensions={0} | all-to-all | bytes 655360 | tf_op jit(solution)/shard_map/all_to_all | solution.py:395
  76.1 1.5 %longitude_stage.1 = bf16[20,8,1440]{2,1,0:T(8,128)(2,1)} custom-call(bf16[8,160,128]{2,1,0:T(8,128)(2,1)S(1)} %all_to_all.15.rows_ref, bf16[1024,720]{1,0:T(8,128)(2,1)S(1)} %copy-done), custom_call_target="tpu_custom_call" | custom-call | flops 503316480 | bytes 4194304 | tf_op jit(solution)/shard_map/longitude_stage/pallas_call | solution.py:356
  (11 shorter events, 0.1 us)
Async XLA Ops:
  0.0 42.7 %copy-start.1 = (f32[8,16,256]{2,1,0:T(8,128)S(1)}, f32[8,16,256]{2,1,0:T(8,128)}, u32[]{:S(2)}) copy-start(f32[8,16,256]{2,1,0:T(8,128)} %constant.73.clone.waves_ref) | copy-start | bytes 393220
  0.0 58.5 %copy-start.5 = (s32[32]{0:T(128)S(1)}, s32[32]{0:T(128)}, u32[]{:S(2)}) copy-start(s32[32]{0:T(128)} %slots_ref.3) | copy-start | bytes 388
  0.0 14.8 %copy-start.6 = (bf16[16,8,2,2,256]{4,3,2,1,0:T(2,128)(2,1)S(1)}, bf16[16,8,2,2,256]{4,3,2,1,0:T(2,128)(2,1)}, u32[]{:S(2)}) copy-start(bf16[16,8,2,2,256]{4,3,2,1,0:T(2,128)(2,1)} %param.8) | copy-start | bytes 786436
  0.0 42.7 %copy-start.2 = (bf16[3,20,6,9]{1,2,3,0:T(8,128)(2,1)S(1)}, bf16[3,20,6,9]{1,2,3,0:T(8,128)(2,1)}, u32[]{:S(2)}) copy-start(bf16[3,20,6,9]{1,2,3,0:T(8,128)(2,1)} %param.11) | copy-start | bytes 19444
  0.0 42.7 %copy-start.4 = (s32[20,6]{0,1:T(8,128)S(1)}, s32[20,6]{0,1:T(8,128)}, u32[]{:S(2)}) copy-start(s32[20,6]{0,1:T(8,128)} %param.12) | copy-start | bytes 1444
  0.0 42.7 %copy-start.3 = (bf16[3,64,64]{2,1,0:T(8,128)(2,1)S(1)}, bf16[3,64,64]{2,1,0:T(8,128)(2,1)}, u32[]{:S(2)}) copy-start(bf16[3,64,64]{2,1,0:T(8,128)(2,1)} %mix_ref) | copy-start | bytes 73732
  4.9 71.3 %copy-start = (bf16[1024,720]{1,0:T(8,128)(2,1)S(1)}, bf16[1024,720]{1,0:T(8,128)(2,1)}, u32[]{:S(2)}) copy-start(bf16[1024,720]{1,0:T(8,128)(2,1)} %constant.74.clone.table_ref) | copy-start | bytes 4423684
  4.9 30.7 %all-to-all-start = ((bf16[32,40,256]{2,1,0:T(8,128)(2,1)}), bf16[32,40,256]{2,1,0:T(8,128)(2,1)S(1)}, u32[]{:S(2)}, u32[]{:S(2)}) async-start(bf16[32,40,256]{2,1,0:T(8,128)(2,1)} %pick.1), calls=%async_computation | async-start | bytes 1310720 | tf_op jit(solution)/shard_map/all_to_all | solution.py:376
  15.0 9.2 %collective-permute-start = (bf16[4,64,256]{2,1,0:T(8,128)(2,1)S(1)}, bf16[4,64,256]{2,1,0:T(8,128)(2,1)S(1)}, u32[]{:S(2)}, u32[]{:S(2)}) collective-permute-start(bf16[4,64,256]{2,1,0:T(8,128)(2,1)S(1)} %get-tuple-element.25), channel_id=1, source_target_pairs={{0,1},{1,0},{2,3},{3,2},{4,5},{5,4},{6,7},{7,6},{8,9},{9,8},{10,11... | collective-permute-start | bytes 393224 | tf_op jit(solution)/shard_map/ppermute | solution.py:381
  24.2 5.0 %collective-permute-start.1 = (bf16[2,64,256]{2,1,0:T(8,128)(2,1)S(1)}, bf16[2,64,256]{2,1,0:T(8,128)(2,1)S(1)}, u32[]{:S(2)}, u32[]{:S(2)}) collective-permute-start(bf16[2,64,256]{2,1,0:T(8,128)(2,1)S(1)} %get-tuple-element.23), channel_id=1, source_target_pairs={{0,2},{1,3},{2,4},{3,5},{4,6},{5,7},{6,0},{7,1},{8,10},{9,11},{10,... | collective-permute-start | bytes 196616 | tf_op jit(solution)/shard_map/ppermute | solution.py:387
  25.9 5.9 %collective-permute-start.2 = (bf16[2,64,256]{2,1,0:T(8,128)(2,1)S(1)}, bf16[2,64,256]{2,1,0:T(8,128)(2,1)S(1)}, u32[]{:S(2)}, u32[]{:S(2)}) collective-permute-start(bf16[2,64,256]{2,1,0:T(8,128)(2,1)S(1)} %get-tuple-element.24), channel_id=1, source_target_pairs={{0,4},{1,5},{2,6},{3,7},{4,0},{5,1},{6,2},{7,3},{8,12},{9,13},{10,... | collective-permute-start | bytes 196616 | tf_op jit(solution)/shard_map/ppermute | solution.py:387
  26.8 5.0 %collective-permute-start.3 = (bf16[2,64,256]{2,1,0:T(8,128)(2,1)S(1)}, bf16[2,64,256]{2,1,0:T(8,128)(2,1)S(1)}, u32[]{:S(2)}, u32[]{:S(2)}) collective-permute-start(bf16[2,64,256]{2,1,0:T(8,128)(2,1)S(1)} %get-tuple-element.21), channel_id=1, source_target_pairs={{0,6},{1,7},{2,0},{3,1},{4,2},{5,3},{6,4},{7,5},{8,14},{9,15},{10,... | collective-permute-start | bytes 196616 | tf_op jit(solution)/shard_map/ppermute | solution.py:387
  37.1 21.4 %all-to-all-start.1 = ((bf16[32,48,128]{2,1,0:T(8,128)(2,1)}), bf16[32,48,128]{2,1,0:T(8,128)(2,1)S(1)}, u32[]{:S(2)}, u32[]{:S(2)}) async-start(bf16[32,48,128]{2,1,0:T(8,128)(2,1)} %order_stage.1), calls=%async_computation.1 | async-start | bytes 786432 | tf_op jit(solution)/shard_map/all_to_all | solution.py:392

commit v6 on v5

--- a/solution.py
+++ b/solution.py
@@ -72,28 +72,26 @@
     return waves
 
 
-PICK_ROWS = 4
-PICK_AHEAD = 4
-GROUPS = ROWS // PICK_ROWS
-PICK_LINES = PICK_ROWS * SUB
+PICK_GROUPS = (4, 4, 8, 4)
 EDGE = 12
 ORDER_LIMITS = (LMAX, LMAX - 2 * LANES)
 
 
 def pick_kernel(slots_ref, leg_ref, out_ref, buf, wide, flat, sems):
-    arrivals, departures = [], []
-    for g in range(GROUPS):
-        rows = pl.ds(g * PICK_ROWS, PICK_ROWS)
-        lines = pl.ds(g * PICK_LINES, PICK_LINES)
+    arrivals, departures, firsts = [], [], []
+    for g, count in enumerate(PICK_GROUPS):
+        first = sum(PICK_GROUPS[:g])
+        firsts.append(first)
         pair = []
         for h in range(STEPS // LANES):
-            part = (rows, pl.ds(h * LANES, LANES), pl.ds(0, ORDER_LIMITS[h]))
+            part = (pl.ds(first, count), pl.ds(h * LANES, LANES), pl.ds(0, ORDER_LIMITS[h]))
             pair.append(pltpu.make_async_copy(leg_ref.at[part], buf.at[part], sems.at[h, g]))
+            pair[-1].start()
         arrivals.append(pair)
-        departures.append(pltpu.make_async_copy(flat.at[g], out_ref.at[:, lines, :], sems.at[2, g]))
-    for pair in arrivals[:PICK_AHEAD]:
-        for copy in pair:
-            copy.start()
+        lines = pl.ds(first * SUB, count * SUB)
+        departures.append(
+            pltpu.make_async_copy(flat.at[:, lines, :], out_ref.at[:, lines, :], sems.at[2, g])
+        )
     line = lax.broadcasted_iota(jnp.int32, (PICKS, LANES), 0)
     lane = lax.broadcasted_iota(jnp.int32, (PICKS, LANES), 1)
     blocks = jnp.zeros((PICKS, LANES), jnp.int32)
@@ -107,24 +105,23 @@
         ],
         axis=1,
     )
-    for g in range(GROUPS):
+    for g, count in enumerate(PICK_GROUPS):
         for copy in arrivals[g]:
             copy.wait()
-        for pair in arrivals[g + PICK_AHEAD :][:1]:
-            for copy in pair:
-                copy.start()
-        for r in range(PICK_ROWS):
-            for h in range(STEPS // LANES):
-                limit = ORDER_LIMITS[h]
-                block = buf[g * PICK_ROWS + r, h * LANES : (h + 1) * LANES, :limit]
+        first, size = firsts[g], count * SUB
+        base = first * SUB * LATS
+        for h in range(STEPS // LANES):
+            limit = ORDER_LIMITS[h]
+            lanes = slice(h * LANES, (h + 1) * LANES)
+            for r in range(count):
+                block = buf[first + r, lanes, :limit]
                 picked = lax.dot_general(hot[:, :limit], block, NT, preferred_element_type=F32)
                 for t in range(SUB):
-                    wide[g, h, pl.ds(r * SUB + t, LATS, stride=PICK_LINES), :] = picked[
+                    wide[h, pl.ds(base + r * SUB + t, LATS, stride=size), :] = picked[
                         t * LATS : (t + 1) * LATS
                     ]
-        for h in range(STEPS // LANES):
-            flat[g, :, :, h * LANES : (h + 1) * LANES] = (
-                wide[g, h].reshape(LATS, PICK_LINES, LANES).astype(BF)
+            flat[:, first * SUB : first * SUB + size, lanes] = (
+                wide[h, base : base + LATS * size].reshape(LATS, size, LANES).astype(BF)
             )
         departures[g].start()
     for copy in departures:
@@ -139,9 +136,9 @@
         out_specs=pl.BlockSpec(memory_space=pltpu.HBM),
         scratch_shapes=[
             pltpu.VMEM((ROWS, STEPS, LMAX), BF),
-            pltpu.VMEM((GROUPS, STEPS // LANES, LATS * PICK_LINES, LANES), F32),
-            pltpu.VMEM((GROUPS, LATS, PICK_LINES, STEPS), BF),
-            pltpu.SemaphoreType.DMA((3, GROUPS)),
+            pltpu.VMEM((STEPS // LANES, LATS * ROWS * SUB, LANES), F32),
+            pltpu.VMEM((LATS, ROWS * SUB, STEPS), BF),
+            pltpu.SemaphoreType.DMA((3, len(PICK_GROUPS))),
         ],
         compiler_params=pltpu.CompilerParams(vmem_limit_bytes=GRANT),
         cost_estimate=pl.CostEstimate(flops=2 * 64 * 512 * 5120, bytes_accessed=6 << 20, transcendentals=0),
@@ -248,7 +245,7 @@
         coef_ref[n] = lax.dot_general(
             taps[n], waves, TN, precision=lax.Precision.HIGHEST, preferred_element_type=F32
         )
-    turned = jnp.concatenate([mix_ref[b].astype(F32).T for b in range(KER)], axis=1)
+    turned = jnp.concatenate([mix_ref[b].astype(F32).T for b in range(KER)], axis=0)
     mixed_ref[...] = jnp.concatenate([turned, turned], axis=1).astype(BF)
 
 
@@ -257,7 +254,7 @@
         coef_kernel,
         out_shape=(
             jax.ShapeDtypeStruct((KER * SPREAD, ROWS, 2 * LANES), F32),
-            jax.ShapeDtypeStruct((C, 2 * KER * C), BF),
+            jax.ShapeDtypeStruct((KER * C, 2 * C), BF),
         ),
         in_specs=[pl.BlockSpec(memory_space=VMEM)] * 4,
         out_specs=[pl.BlockSpec(memory_space=VMEM)] * 2,
@@ -273,12 +270,13 @@
     )
 
 
-def row_kernel(slots_ref, rows_ref, coef_ref, mix_ref, out_ref, field, plain, crossed):
+def row_kernel(slots_ref, rows_ref, coef_ref, mix_ref, out_ref, field, mixed):
     for i in range(LATS):
         block = slots_ref[i]
         start = pl.multiple_of(block * (SUB * HALO_ROWS), 8)
         field[pl.ds(start, SUB * HALO_ROWS), :] = rows_ref[i].astype(F32)
-    low = lax.broadcasted_iota(jnp.int32, (C, LANES), 1) < PICKS
+    low = lax.broadcasted_iota(jnp.int32, (PICKS, LANES), 1) < C
+    weights = mix_ref[...]
     for r in range(HALO_ROWS):
         one = jnp.concatenate(
             [
@@ -287,24 +285,20 @@
             ],
             axis=0,
         )
-        both = jnp.concatenate([one, one], axis=0).T
-        plain[r] = jnp.where(low, both[:C], both[C:])
-        crossed[r] = jnp.where(low, both[C:], both[:C])
+        real = jnp.where(low, one, 0.0)
+        imag = jnp.where(low, 0.0, one)
+        both = jnp.concatenate([real, imag, imag, real], axis=0).astype(BF)
+        mixed[r] = lax.dot_general(weights, both, NT, preferred_element_type=F32)
     for r in range(ROWS):
-        tops, rests = [], []
+        total = None
         for b in range(KER):
-            total = None
             for d in range(SPREAD):
                 n = b * SPREAD + d
-                term = coef_ref[n, r : r + 1, :LANES] * plain[r + d]
-                term = term + coef_ref[n, r : r + 1, LANES:] * crossed[r + d]
+                part = mixed[r + d, b * C : (b + 1) * C, :]
+                term = coef_ref[n, r : r + 1, :LANES] * part[:, :LANES]
+                term = term + coef_ref[n, r : r + 1, LANES:] * part[:, LANES:]
                 total = term if total is None else total + term
-            top = total.astype(BF)
-            tops.append(top)
-            rests.append((total - top.astype(F32)).astype(BF))
-        both = jnp.concatenate(tops + rests, axis=0)
-        mixed = jnp.dot(mix_ref[...], both, preferred_element_type=F32)
-        out_ref[:, r * OWN : (r + 1) * OWN, :] = mixed.astype(BF).reshape(CHS, OWN, LANES)
+        out_ref[:, r * OWN : (r + 1) * OWN, :] = total.astype(BF).reshape(CHS, OWN, LANES)
 
 
 def row_stage(block_slots, rows, coefs, mix):
@@ -320,8 +314,7 @@
         out_specs=pl.BlockSpec(memory_space=VMEM),
         scratch_shapes=[
             pltpu.VMEM((BLOCKS * SUB * HALO_ROWS, LANES), F32),
-            pltpu.VMEM((HALO_ROWS, C, LANES), F32),
-            pltpu.VMEM((HALO_ROWS, C, LANES), F32),
+            pltpu.VMEM((HALO_ROWS, KER * C, 2 * LANES), F32),
         ],
         compiler_params=pltpu.CompilerParams(vmem_limit_bytes=16 << 20),
         cost_estimate=pl.CostEstimate(flops=200 << 20, bytes_accessed=2 << 20, transcendentals=0),
@@ -329,23 +322,24 @@
     )(block_slots, rows, coefs, mix)
 
 
-LON_PARTS = 4
-
-
-def longitude_kernel(rows_ref, table_ref, out_ref, field, whole, sems):
-    even = jnp.concatenate([rows_ref[j] for j in range(CHS)], axis=1)
-    lane = lax.broadcasted_iota(jnp.int32, even.shape, 1)
-    flipped = jnp.where(lane % PICKS < BLOCKS, even.astype(F32), -even.astype(F32)).astype(BF)
-    both = jnp.concatenate([even, flipped], axis=0)
-    field[...] = jnp.dot(both, table_ref[...], preferred_element_type=F32)
-    count, rows = OWN * ROWS, ROWS // LON_PARTS
+LON_PARTS = 2
+
+
+def longitude_kernel(rows_ref, table_ref, out_ref, whole, sems):
+    rows = ROWS // LON_PARTS
     lines = rows * OWN
     departures = []
     for g in range(LON_PARTS):
-        first = field[g * lines : (g + 1) * lines]
-        second = field[count + g * lines : count + (g + 1) * lines]
+        even = jnp.concatenate(
+            [rows_ref[j, g * lines : (g + 1) * lines] for j in range(CHS)], axis=1
+        )
+        lane = lax.broadcasted_iota(jnp.int32, even.shape, 1)
+        flipped = jnp.where(lane % PICKS < BLOCKS, even.astype(F32), -even.astype(F32)).astype(BF)
+        both = jnp.concatenate([even, flipped], axis=0)
+        field = jnp.dot(both, table_ref[...], preferred_element_type=F32)
         part = pl.ds(g * rows, rows)
-        whole[part] = jnp.concatenate([first, second], axis=1).astype(BF).reshape(rows, OWN, NLON)
+        halves = jnp.concatenate([field[:lines], field[lines:]], axis=1)
+        whole[part] = halves.astype(BF).reshape(rows, OWN, NLON)
         departures.append(pltpu.make_async_copy(whole.at[part], out_ref.at[part], sems.at[g]))
         departures[-1].start()
     for copy in departures:
@@ -359,7 +353,6 @@
         in_specs=[pl.BlockSpec(memory_space=VMEM)] * 2,
         out_specs=pl.BlockSpec(memory_space=pltpu.HBM),
         scratch_shapes=[
-            pltpu.VMEM((2 * OWN * ROWS, HALF_LON), F32),
             pltpu.VMEM((ROWS, OWN, NLON), BF),
             pltpu.SemaphoreType.DMA((LON_PARTS,)),
         ],

time: 78 us -> 77.4 us (level)
  no operation moved by 1% of the time
where the time goes in v6:
time: 77.4 us; the launch traced here: 77.1 us
  waiting for transfers between devices  28 us (36%)
  starting transfers between devices  23.2 us (30%)
  blocking collectives  14.9 us (19%)
  Pallas kernels  10.6 us (14%)
    all_to_all x1, waiting for transfers between devices, per_device(): by_row = lax.all_to_all(by_order, 'lat', 0, 0, tiled=True)  15.3 us
    all_to_all x1, blocking collectives, per_device(): own = lax.all_to_all(mixed, 'ch', 0, 0, tiled=True)  14.9 us
    all_to_all x1, starting transfers between devices, per_device(): leg = lax.all_to_all(picked, 'lat', 0, 0, tiled=True)  9.93 us
    ppermute x1, waiting for transfers between devices, per_device(): taken = lax.ppermute(given, 'ch', [(j, j ^ 1) for j in range(CHS)])  6.4 us
    all_to_all x1, starting transfers between devices, per_device(): by_row = lax.all_to_all(by_order, 'lat', 0, 0, tiled=True)  5.5 us
    ppermute x3, starting transfers between devices, per_device(): pieces.append(lax.ppermute(piece, 'ch', shift) if d else piece)  5 us
    pallas_call x1, Pallas kernels, pick(): pl.pallas_call(pick_kernel, out_shape=jax.ShapeDtypeStruct((LATS, ROWS *...  4.61 us
    all_to_all x1, waiting for transfers between devices, per_device(): leg = lax.all_to_all(picked, 'lat', 0, 0, tiled=True)  3.77 us
  transfers between devices with their start and end apart: 6, of which 4 were waited for; matrix products, arithmetic and copies ran while one was open for 0% of the time, Pallas kernels for 1%

profile of v6, /device:TPU:8, one launch (start us, length us, event | category | flops | bytes accessed | tf_op | source)
XLA Modules:
  0.0 77.1 jit_solution(11035711934078153632)
XLA Ops:
  0.0 0.0 copy-start.2
  0.0 0.0 copy-start.4
  0.0 0.0 copy-start.3
  0.0 4.6 %pick.1 = bf16[32,40,256]{2,1,0:T(8,128)(2,1)} custom-call(s32[32]{0:T(128)} %slots_ref.3, bf16[20,256,512]{2,1,0:T(8,128)(2,1)} %leg_ref.1), custom_call_target="tpu_custom_call" | custom-call | flops 335544320 | bytes 6291456 | tf_op jit(solution)/shard_map/pick/pallas_call | solution.py:132
  4.7 0.0 copy-start
  4.7 9.9 %all-to-all-start = ((bf16[32,40,256]{2,1,0:T(8,128)(2,1)}), bf16[32,40,256]{2,1,0:T(8,128)(2,1)S(1)}, u32[]{:S(2)}, u32[]{:S(2)}) async-start(bf16[32,40,256]{2,1,0:T(8,128)(2,1)} %pick.1), calls=%async_computation | async-start | bytes 1310720 | tf_op jit(solution)/shard_map/all_to_all | solution.py:369
  14.6 0.1 reshape.3
  14.8 2.8 %collective-permute-start = (bf16[4,64,256]{2,1,0:T(8,128)(2,1)S(1)}, bf16[4,64,256]{2,1,0:T(8,128)(2,1)S(1)}, u32[]{:S(2)}, u32[]{:S(2)}) collective-permute-start(bf16[4,64,256]{2,1,0:T(8,128)(2,1)S(1)} %get-tuple-element.25), channel_id=1, source_target_pairs={{0,1},{1,0},{2,3},{3,2},{4,5},{5,4},{6,7},{7,6},{8,9},{9,8},{10,11... | collective-permute-start | bytes 393224 | tf_op jit(solution)/shard_map/ppermute | solution.py:374
  17.6 6.4 %collective-permute-done = bf16[4,64,256]{2,1,0:T(8,128)(2,1)S(1)} collective-permute-done((bf16[4,64,256]{2,1,0:T(8,128)(2,1)S(1)}, bf16[4,64,256]{2,1,0:T(8,128)(2,1)S(1)}, u32[]{:S(2)}, u32[]{:S(2)}) %collective-permute-start) | collective-permute-done | bytes 131104 | tf_op jit(solution)/shard_map/ppermute | solution.py:374
  24.0 1.7 %collective-permute-start.1 = (bf16[2,64,256]{2,1,0:T(8,128)(2,1)S(1)}, bf16[2,64,256]{2,1,0:T(8,128)(2,1)S(1)}, u32[]{:S(2)}, u32[]{:S(2)}) collective-permute-start(bf16[2,64,256]{2,1,0:T(8,128)(2,1)S(1)} %get-tuple-element.23), channel_id=1, source_target_pairs={{0,2},{1,3},{2,4},{3,5},{4,6},{5,7},{6,0},{7,1},{8,10},{9,11},{10,... | collective-permute-start | bytes 196616 | tf_op jit(solution)/shard_map/ppermute | solution.py:380
  25.7 0.9 %collective-permute-start.2 = (bf16[2,64,256]{2,1,0:T(8,128)(2,1)S(1)}, bf16[2,64,256]{2,1,0:T(8,128)(2,1)S(1)}, u32[]{:S(2)}, u32[]{:S(2)}) collective-permute-start(bf16[2,64,256]{2,1,0:T(8,128)(2,1)S(1)} %get-tuple-element.24), channel_id=1, source_target_pairs={{0,4},{1,5},{2,6},{3,7},{4,0},{5,1},{6,2},{7,3},{8,12},{9,13},{10,... | collective-permute-start | bytes 196616 | tf_op jit(solution)/shard_map/ppermute | solution.py:380
  26.6 2.4 %collective-permute-start.3 = (bf16[2,64,256]{2,1,0:T(8,128)(2,1)S(1)}, bf16[2,64,256]{2,1,0:T(8,128)(2,1)S(1)}, u32[]{:S(2)}, u32[]{:S(2)}) collective-permute-start(bf16[2,64,256]{2,1,0:T(8,128)(2,1)S(1)} %get-tuple-element.21), channel_id=1, source_target_pairs={{0,6},{1,7},{2,0},{3,1},{4,2},{5,3},{6,4},{7,5},{8,14},{9,15},{10,... | collective-permute-start | bytes 196616 | tf_op jit(solution)/shard_map/ppermute | solution.py:380
  29.0 0.0 collective-permute-done.1.refs_1_
  29.0 2.5 %collective-permute-done.2.refs_2_ = bf16[2,64,256]{2,1,0:T(8,128)(2,1)S(1)} collective-permute-done((bf16[2,64,256]{2,1,0:T(8,128)(2,1)S(1)}, bf16[2,64,256]{2,1,0:T(8,128)(2,1)S(1)}, u32[]{:S(2)}, u32[]{:S(2)}) %collective-permute-start.2) | collective-permute-done | bytes 65568 | tf_op jit(solution)/shard_map/ppermute | solution.py:380
  31.6 0.0 collective-permute-done.3.refs_3_
  31.6 3.8 %all-to-all-done.leg_ref = bf16[32,40,256]{2,1,0:T(8,128)(2,1)S(1)} async-done(((bf16[32,40,256]{2,1,0:T(8,128)(2,1)}), bf16[32,40,256]{2,1,0:T(8,128)(2,1)S(1)}, u32[]{:S(2)}, u32[]{:S(2)}) %all-to-all-start) | async-done | bytes 655392 | tf_op jit(solution)/shard_map/all_to_all | solution.py:369
  35.4 1.6 %order_stage.1 = bf16[32,48,128]{2,1,0:T(8,128)(2,1)} custom-call(bf16[32,40,256]{2,1,0:T(8,128)(2,1)S(1)} %all-to-all-done.leg_ref, bf16[2,64,256]{2,1,0:T(8,128)(2,1)S(1)} %get-tuple-element.22.refs_0_, bf16[2,64,256]{2,1,0:T(8,128)(2,1)S(1)} %collective-permute-done.1.refs_1_, bf16[2,64,256]{2,1,0:T(8,128)(2,1)S(1)} %collective-permute-done.2.refs_2_, ...), custom_call_target="tpu_custom_call" | custom-call | flops 734003200 | bytes 2097152 | tf_op jit(solution)/shard_map/order_stage/pallas_call | solution.py:217
  37.0 5.5 %all-to-all-start.1 = ((bf16[32,48,128]{2,1,0:T(8,128)(2,1)}), bf16[32,48,128]{2,1,0:T(8,128)(2,1)S(1)}, u32[]{:S(2)}, u32[]{:S(2)}) async-start(bf16[32,48,128]{2,1,0:T(8,128)(2,1)} %order_stage.1), calls=%async_computation.1 | async-start | bytes 786432 | tf_op jit(solution)/shard_map/all_to_all | solution.py:385
  42.5 0.6 coef_stage.1
  43.1 15.3 %all-to-all-done.1.rows_ref = bf16[32,48,128]{2,1,0:T(8,128)(2,1)S(1)} async-done(((bf16[32,48,128]{2,1,0:T(8,128)(2,1)}), bf16[32,48,128]{2,1,0:T(8,128)(2,1)S(1)}, u32[]{:S(2)}, u32[]{:S(2)}) %all-to-all-start.1) | async-done | bytes 393248 | tf_op jit(solution)/shard_map/all_to_all | solution.py:385
  58.4 2.4 %row_stage.1 = bf16[8,160,128]{2,1,0:T(8,128)(2,1)S(1)} custom-call(s32[32]{0:T(128)S(1)} %copy-done.5, bf16[32,48,128]{2,1,0:T(8,128)(2,1)S(1)} %all-to-all-done.1.rows_ref, f32[15,20,256]{2,1,0:T(8,128)S(1)} %get-tuple-element.19.coef_ref, bf16[192,128]{1,0:T(8,128)(2,1)S(1)} %get-tuple-element.20.mix_ref), custom_call_target="tpu_custom_call" | custom-call | flops 209715200 | bytes 2097152 | tf_op jit(solution)/shard_map/row_stage/pallas_call | solution.py:305
  60.8 14.9 %all_to_all.15.rows_ref = bf16[8,160,128]{2,1,0:T(8,128)(2,1)S(1)} all-to-all(bf16[8,160,128]{2,1,0:T(8,128)(2,1)S(1)} %row_stage.1), channel_id=1, replica_groups=mesh['lat'=32,'ch'=8] {'ch'}, dimensions={0} | all-to-all | bytes 655360 | tf_op jit(solution)/shard_map/all_to_all | solution.py:388
  75.6 0.0 copy-done
  75.6 1.5 %longitude_stage.1 = bf16[20,8,1440]{2,1,0:T(8,128)(2,1)} custom-call(bf16[8,160,128]{2,1,0:T(8,128)(2,1)S(1)} %all_to_all.15.rows_ref, bf16[1024,720]{1,0:T(8,128)(2,1)S(1)} %copy-done), custom_call_target="tpu_custom_call" | custom-call | flops 503316480 | bytes 4194304 | tf_op jit(solution)/shard_map/longitude_stage/pallas_call | solution.py:350
  (11 shorter events, 0.1 us)
Async XLA Ops:
  0.0 42.5 %copy-start.1 = (f32[8,16,256]{2,1,0:T(8,128)S(1)}, f32[8,16,256]{2,1,0:T(8,128)}, u32[]{:S(2)}) copy-start(f32[8,16,256]{2,1,0:T(8,128)} %constant.73.clone.waves_ref) | copy-start | bytes 393220
  0.0 58.4 %copy-start.5 = (s32[32]{0:T(128)S(1)}, s32[32]{0:T(128)}, u32[]{:S(2)}) copy-start(s32[32]{0:T(128)} %slots_ref.3) | copy-start | bytes 388
  0.0 14.6 %copy-start.6 = (bf16[16,8,2,2,256]{4,3,2,1,0:T(2,128)(2,1)S(1)}, bf16[16,8,2,2,256]{4,3,2,1,0:T(2,128)(2,1)}, u32[]{:S(2)}) copy-start(bf16[16,8,2,2,256]{4,3,2,1,0:T(2,128)(2,1)} %param.8) | copy-start | bytes 786436
  0.0 42.5 %copy-start.2 = (bf16[3,20,6,9]{1,2,3,0:T(8,128)(2,1)S(1)}, bf16[3,20,6,9]{1,2,3,0:T(8,128)(2,1)}, u32[]{:S(2)}) copy-start(bf16[3,20,6,9]{1,2,3,0:T(8,128)(2,1)} %param.11) | copy-start | bytes 19444
  0.0 42.5 %copy-start.4 = (s32[20,6]{0,1:T(8,128)S(1)}, s32[20,6]{0,1:T(8,128)}, u32[]{:S(2)}) copy-start(s32[20,6]{0,1:T(8,128)} %param.12) | copy-start | bytes 1444
  0.0 42.5 %copy-start.3 = (bf16[3,64,64]{2,1,0:T(8,128)(2,1)S(1)}, bf16[3,64,64]{2,1,0:T(8,128)(2,1)}, u32[]{:S(2)}) copy-start(bf16[3,64,64]{2,1,0:T(8,128)(2,1)} %mix_ref) | copy-start | bytes 73732
  4.7 71.0 %copy-start = (bf16[1024,720]{1,0:T(8,128)(2,1)S(1)}, bf16[1024,720]{1,0:T(8,128)(2,1)}, u32[]{:S(2)}) copy-start(bf16[1024,720]{1,0:T(8,128)(2,1)} %constant.74.clone.table_ref) | copy-start | bytes 4423684
  4.7 30.7 %all-to-all-start = ((bf16[32,40,256]{2,1,0:T(8,128)(2,1)}), bf16[32,40,256]{2,1,0:T(8,128)(2,1)S(1)}, u32[]{:S(2)}, u32[]{:S(2)}) async-start(bf16[32,40,256]{2,1,0:T(8,128)(2,1)} %pick.1), calls=%async_computation | async-start | bytes 1310720 | tf_op jit(solution)/shard_map/all_to_all | solution.py:369
  14.8 9.2 %collective-permute-start = (bf16[4,64,256]{2,1,0:T(8,128)(2,1)S(1)}, bf16[4,64,256]{2,1,0:T(8,128)(2,1)S(1)}, u32[]{:S(2)}, u32[]{:S(2)}) collective-permute-start(bf16[4,64,256]{2,1,0:T(8,128)(2,1)S(1)} %get-tuple-element.25), channel_id=1, source_target_pairs={{0,1},{1,0},{2,3},{3,2},{4,5},{5,4},{6,7},{7,6},{8,9},{9,8},{10,11... | collective-permute-start | bytes 393224 | tf_op jit(solution)/shard_map/ppermute | solution.py:374
  24.0 5.0 %collective-permute-start.1 = (bf16[2,64,256]{2,1,0:T(8,128)(2,1)S(1)}, bf16[2,64,256]{2,1,0:T(8,128)(2,1)S(1)}, u32[]{:S(2)}, u32[]{:S(2)}) collective-permute-start(bf16[2,64,256]{2,1,0:T(8,128)(2,1)S(1)} %get-tuple-element.23), channel_id=1, source_target_pairs={{0,2},{1,3},{2,4},{3,5},{4,6},{5,7},{6,0},{7,1},{8,10},{9,11},{10,... | collective-permute-start | bytes 196616 | tf_op jit(solution)/shard_map/ppermute | solution.py:380
  25.7 5.9 %collective-permute-start.2 = (bf16[2,64,256]{2,1,0:T(8,128)(2,1)S(1)}, bf16[2,64,256]{2,1,0:T(8,128)(2,1)S(1)}, u32[]{:S(2)}, u32[]{:S(2)}) collective-permute-start(bf16[2,64,256]{2,1,0:T(8,128)(2,1)S(1)} %get-tuple-element.24), channel_id=1, source_target_pairs={{0,4},{1,5},{2,6},{3,7},{4,0},{5,1},{6,2},{7,3},{8,12},{9,13},{10,... | collective-permute-start | bytes 196616 | tf_op jit(solution)/shard_map/ppermute | solution.py:380
  26.6 5.0 %collective-permute-start.3 = (bf16[2,64,256]{2,1,0:T(8,128)(2,1)S(1)}, bf16[2,64,256]{2,1,0:T(8,128)(2,1)S(1)}, u32[]{:S(2)}, u32[]{:S(2)}) collective-permute-start(bf16[2,64,256]{2,1,0:T(8,128)(2,1)S(1)} %get-tuple-element.21), channel_id=1, source_target_pairs={{0,6},{1,7},{2,0},{3,1},{4,2},{5,3},{6,4},{7,5},{8,14},{9,15},{10,... | collective-permute-start | bytes 196616 | tf_op jit(solution)/shard_map/ppermute | solution.py:380
  37.0 21.4 %all-to-all-start.1 = ((bf16[32,48,128]{2,1,0:T(8,128)(2,1)}), bf16[32,48,128]{2,1,0:T(8,128)(2,1)S(1)}, u32[]{:S(2)}, u32[]{:S(2)}) async-start(bf16[32,48,128]{2,1,0:T(8,128)(2,1)} %order_stage.1), calls=%async_computation.1 | async-start | bytes 786432 | tf_op jit(solution)/shard_map/all_to_all | solution.py:385

commit v7 on v6

--- a/solution.py
+++ b/solution.py
@@ -36,6 +36,7 @@
 TN = (((0,), (0,)), ((), ()))
 VMEM = pltpu.VMEM
 GRANT = 62 << 20
+MARGIN = 48
 PAIR = 2
 TURNS = CHS // PAIR
 
@@ -110,16 +111,21 @@
             copy.wait()
         first, size = firsts[g], count * SUB
         base = first * SUB * LATS
-        for h in range(STEPS // LANES):
-            limit = ORDER_LIMITS[h]
-            lanes = slice(h * LANES, (h + 1) * LANES)
-            for r in range(count):
-                block = buf[first + r, lanes, :limit]
-                picked = lax.dot_general(hot[:, :limit], block, NT, preferred_element_type=F32)
+        limit = ORDER_LIMITS[1]
+        for r in range(count):
+            lead = lax.dot_general(
+                hot[:, :limit], buf[first + r, :, :limit], NT, preferred_element_type=F32
+            )
+            rest = lax.dot_general(
+                hot[:, limit:], buf[first + r, :LANES, limit:], NT, preferred_element_type=F32
+            )
+            for h, picked in enumerate((lead[:, :LANES] + rest, lead[:, LANES:])):
                 for t in range(SUB):
                     wide[h, pl.ds(base + r * SUB + t, LATS, stride=size), :] = picked[
                         t * LATS : (t + 1) * LATS
                     ]
+        for h in range(STEPS // LANES):
+            lanes = slice(h * LANES, (h + 1) * LANES)
             flat[:, first * SUB : first * SUB + size, lanes] = (
                 wide[h, base : base + LATS * size].reshape(LATS, size, LANES).astype(BF)
             )
@@ -136,7 +142,7 @@
         out_specs=pl.BlockSpec(memory_space=pltpu.HBM),
         scratch_shapes=[
             pltpu.VMEM((ROWS, STEPS, LMAX), BF),
-            pltpu.VMEM((STEPS // LANES, LATS * ROWS * SUB, LANES), F32),
+            pltpu.VMEM((STEPS // LANES, LATS * ROWS * SUB + MARGIN, LANES), F32),
             pltpu.VMEM((LATS, ROWS * SUB, STEPS), BF),
             pltpu.SemaphoreType.DMA((3, len(PICK_GROUPS))),
         ],
@@ -161,7 +167,8 @@
                 specs[h, pl.ds(start, C), :] = pieces_in[d][q, :, lanes].astype(F32)
     for h in range(STEPS // LANES):
         lanes = slice(h * LANES, (h + 1) * LANES)
-        raw[h] = leg_ref[:, :, lanes].astype(F32).reshape(LATS * ROWS * SUB, LANES)
+        lines = leg_ref[:, :, lanes].astype(F32).reshape(LATS * ROWS * SUB, LANES)
+        raw[h, : LATS * ROWS * SUB, :] = lines
     rows = lax.broadcasted_iota(jnp.int32, (LANES, LANES), 0)
     cols = lax.broadcasted_iota(jnp.int32, (LANES, LANES), 1)
     turn = jnp.where(rows + cols == LANES - 1, 1.0, 0.0).astype(BF)
@@ -220,8 +227,8 @@
         in_specs=[pl.BlockSpec(memory_space=VMEM)] * (1 + TURNS),
         out_specs=pl.BlockSpec(memory_space=VMEM),
         scratch_shapes=[
-            pltpu.VMEM((STEPS // LANES, LATS * SUB * ROWS, LANES), F32),
-            pltpu.VMEM((STEPS // LANES, CHS * C, LANES), F32),
+            pltpu.VMEM((STEPS // LANES, LATS * SUB * ROWS + MARGIN, LANES), F32),
+            pltpu.VMEM((STEPS // LANES, CHS * C + MARGIN, LANES), F32),
             pltpu.VMEM((SUB * NLAT + 2 * EDGE, LANES), F32),
         ],
         compiler_params=pltpu.CompilerParams(vmem_limit_bytes=24 << 20),
@@ -313,7 +320,7 @@
         ],
         out_specs=pl.BlockSpec(memory_space=VMEM),
         scratch_shapes=[
-            pltpu.VMEM((BLOCKS * SUB * HALO_ROWS, LANES), F32),
+            pltpu.VMEM((BLOCKS * SUB * HALO_ROWS + MARGIN, LANES), F32),
             pltpu.VMEM((HALO_ROWS, KER * C, 2 * LANES), F32),
         ],
         compiler_params=pltpu.CompilerParams(vmem_limit_bytes=16 << 20),

time: 77.4 us -> 77.4 us (level)
  no operation moved by 1% of the time
where the time goes in v7:
time: 77.4 us; the launch traced here: 77 us
  waiting for transfers between devices  28 us (36%)
  starting transfers between devices  23.3 us (30%)
  blocking collectives  14.9 us (19%)
  Pallas kernels  10.5 us (14%)
    all_to_all x1, waiting for transfers between devices, per_device(): by_row = lax.all_to_all(by_order, 'lat', 0, 0, tiled=True)  15.3 us
    all_to_all x1, blocking collectives, per_device(): own = lax.all_to_all(mixed, 'ch', 0, 0, tiled=True)  14.9 us
    all_to_all x1, starting transfers between devices, per_device(): leg = lax.all_to_all(picked, 'lat', 0, 0, tiled=True)  9.92 us
    ppermute x1, waiting for transfers between devices, per_device(): taken = lax.ppermute(given, 'ch', [(j, j ^ 1) for j in range(CHS)])  6.4 us
    all_to_all x1, starting transfers between devices, per_device(): by_row = lax.all_to_all(by_order, 'lat', 0, 0, tiled=True)  5.51 us
    ppermute x3, starting transfers between devices, per_device(): pieces.append(lax.ppermute(piece, 'ch', shift) if d else piece)  5 us
    pallas_call x1, Pallas kernels, pick(): pl.pallas_call(pick_kernel, out_shape=jax.ShapeDtypeStruct((LATS, ROWS *...  4.53 us
    all_to_all x1, waiting for transfers between devices, per_device(): leg = lax.all_to_all(picked, 'lat', 0, 0, tiled=True)  3.77 us
  transfers between devices with their start and end apart: 6, of which 4 were waited for; matrix products, arithmetic and copies ran while one was open for 0% of the time, Pallas kernels for 1%

profile of v7, /device:TPU:8, one launch (start us, length us, event | category | flops | bytes accessed | tf_op | source)
XLA Modules:
  0.0 77.0 jit_solution(9457494939872350901)
XLA Ops:
  0.0 0.0 copy-start.2
  0.0 0.0 copy-start.4
  0.0 4.5 %pick.1 = bf16[32,40,256]{2,1,0:T(8,128)(2,1)} custom-call(s32[32]{0:T(128)} %slots_ref.3, bf16[20,256,512]{2,1,0:T(8,128)(2,1)} %leg_ref.1), custom_call_target="tpu_custom_call" | custom-call | flops 335544320 | bytes 6291456 | tf_op jit(solution)/shard_map/pick/pallas_call | solution.py:138
  4.6 0.0 copy-start
  4.6 9.9 %all-to-all-start = ((bf16[32,40,256]{2,1,0:T(8,128)(2,1)}), bf16[32,40,256]{2,1,0:T(8,128)(2,1)S(1)}, u32[]{:S(2)}, u32[]{:S(2)}) async-start(bf16[32,40,256]{2,1,0:T(8,128)(2,1)} %pick.1), calls=%async_computation | async-start | bytes 1310720 | tf_op jit(solution)/shard_map/all_to_all | solution.py:376
  14.5 0.0 copy-done.6
  14.5 0.1 reshape.3
  14.7 2.8 %collective-permute-start = (bf16[4,64,256]{2,1,0:T(8,128)(2,1)S(1)}, bf16[4,64,256]{2,1,0:T(8,128)(2,1)S(1)}, u32[]{:S(2)}, u32[]{:S(2)}) collective-permute-start(bf16[4,64,256]{2,1,0:T(8,128)(2,1)S(1)} %get-tuple-element.25), channel_id=1, source_target_pairs={{0,1},{1,0},{2,3},{3,2},{4,5},{5,4},{6,7},{7,6},{8,9},{9,8},{10,11... | collective-permute-start | bytes 393224 | tf_op jit(solution)/shard_map/ppermute | solution.py:381
  17.5 6.4 %collective-permute-done = bf16[4,64,256]{2,1,0:T(8,128)(2,1)S(1)} collective-permute-done((bf16[4,64,256]{2,1,0:T(8,128)(2,1)S(1)}, bf16[4,64,256]{2,1,0:T(8,128)(2,1)S(1)}, u32[]{:S(2)}, u32[]{:S(2)}) %collective-permute-start) | collective-permute-done | bytes 131104 | tf_op jit(solution)/shard_map/ppermute | solution.py:381
  24.0 1.7 %collective-permute-start.1 = (bf16[2,64,256]{2,1,0:T(8,128)(2,1)S(1)}, bf16[2,64,256]{2,1,0:T(8,128)(2,1)S(1)}, u32[]{:S(2)}, u32[]{:S(2)}) collective-permute-start(bf16[2,64,256]{2,1,0:T(8,128)(2,1)S(1)} %get-tuple-element.23), channel_id=1, source_target_pairs={{0,2},{1,3},{2,4},{3,5},{4,6},{5,7},{6,0},{7,1},{8,10},{9,11},{10,... | collective-permute-start | bytes 196616 | tf_op jit(solution)/shard_map/ppermute | solution.py:387
  25.6 0.9 %collective-permute-start.2 = (bf16[2,64,256]{2,1,0:T(8,128)(2,1)S(1)}, bf16[2,64,256]{2,1,0:T(8,128)(2,1)S(1)}, u32[]{:S(2)}, u32[]{:S(2)}) collective-permute-start(bf16[2,64,256]{2,1,0:T(8,128)(2,1)S(1)} %get-tuple-element.24), channel_id=1, source_target_pairs={{0,4},{1,5},{2,6},{3,7},{4,0},{5,1},{6,2},{7,3},{8,12},{9,13},{10,... | collective-permute-start | bytes 196616 | tf_op jit(solution)/shard_map/ppermute | solution.py:387
  26.5 2.4 %collective-permute-start.3 = (bf16[2,64,256]{2,1,0:T(8,128)(2,1)S(1)}, bf16[2,64,256]{2,1,0:T(8,128)(2,1)S(1)}, u32[]{:S(2)}, u32[]{:S(2)}) collective-permute-start(bf16[2,64,256]{2,1,0:T(8,128)(2,1)S(1)} %get-tuple-element.21), channel_id=1, source_target_pairs={{0,6},{1,7},{2,0},{3,1},{4,2},{5,3},{6,4},{7,5},{8,14},{9,15},{10,... | collective-permute-start | bytes 196616 | tf_op jit(solution)/shard_map/ppermute | solution.py:387
  29.0 0.0 collective-permute-done.1.refs_1_
  29.0 2.5 %collective-permute-done.2.refs_2_ = bf16[2,64,256]{2,1,0:T(8,128)(2,1)S(1)} collective-permute-done((bf16[2,64,256]{2,1,0:T(8,128)(2,1)S(1)}, bf16[2,64,256]{2,1,0:T(8,128)(2,1)S(1)}, u32[]{:S(2)}, u32[]{:S(2)}) %collective-permute-start.2) | collective-permute-done | bytes 65568 | tf_op jit(solution)/shard_map/ppermute | solution.py:387
  31.5 0.0 collective-permute-done.3.refs_3_
  31.5 3.8 %all-to-all-done.leg_ref = bf16[32,40,256]{2,1,0:T(8,128)(2,1)S(1)} async-done(((bf16[32,40,256]{2,1,0:T(8,128)(2,1)}), bf16[32,40,256]{2,1,0:T(8,128)(2,1)S(1)}, u32[]{:S(2)}, u32[]{:S(2)}) %all-to-all-start) | async-done | bytes 655392 | tf_op jit(solution)/shard_map/all_to_all | solution.py:376
  35.3 1.6 %order_stage.1 = bf16[32,48,128]{2,1,0:T(8,128)(2,1)} custom-call(bf16[32,40,256]{2,1,0:T(8,128)(2,1)S(1)} %all-to-all-done.leg_ref, bf16[2,64,256]{2,1,0:T(8,128)(2,1)S(1)} %get-tuple-element.22.refs_0_, bf16[2,64,256]{2,1,0:T(8,128)(2,1)S(1)} %collective-permute-done.1.refs_1_, bf16[2,64,256]{2,1,0:T(8,128)(2,1)S(1)} %collective-permute-done.2.refs_2_, ...), custom_call_target="tpu_custom_call" | custom-call | flops 734003200 | bytes 2097152 | tf_op jit(solution)/shard_map/order_stage/pallas_call | solution.py:224
  36.9 5.5 %all-to-all-start.1 = ((bf16[32,48,128]{2,1,0:T(8,128)(2,1)}), bf16[32,48,128]{2,1,0:T(8,128)(2,1)S(1)}, u32[]{:S(2)}, u32[]{:S(2)}) async-start(bf16[32,48,128]{2,1,0:T(8,128)(2,1)} %order_stage.1), calls=%async_computation.1 | async-start | bytes 786432 | tf_op jit(solution)/shard_map/all_to_all | solution.py:392
  42.4 0.6 coef_stage.1
  43.0 15.3 %all-to-all-done.1.rows_ref = bf16[32,48,128]{2,1,0:T(8,128)(2,1)S(1)} async-done(((bf16[32,48,128]{2,1,0:T(8,128)(2,1)}), bf16[32,48,128]{2,1,0:T(8,128)(2,1)S(1)}, u32[]{:S(2)}, u32[]{:S(2)}) %all-to-all-start.1) | async-done | bytes 393248 | tf_op jit(solution)/shard_map/all_to_all | solution.py:392
  58.3 0.0 copy-done.5
  58.3 2.4 %row_stage.1 = bf16[8,160,128]{2,1,0:T(8,128)(2,1)S(1)} custom-call(s32[32]{0:T(128)S(1)} %copy-done.5, bf16[32,48,128]{2,1,0:T(8,128)(2,1)S(1)} %all-to-all-done.1.rows_ref, f32[15,20,256]{2,1,0:T(8,128)S(1)} %get-tuple-element.19.coef_ref, bf16[192,128]{1,0:T(8,128)(2,1)S(1)} %get-tuple-element.20.mix_ref), custom_call_target="tpu_custom_call" | custom-call | flops 209715200 | bytes 2097152 | tf_op jit(solution)/shard_map/row_stage/pallas_call | solution.py:312
  60.7 14.9 %all_to_all.15.rows_ref = bf16[8,160,128]{2,1,0:T(8,128)(2,1)S(1)} all-to-all(bf16[8,160,128]{2,1,0:T(8,128)(2,1)S(1)} %row_stage.1), channel_id=1, replica_groups=mesh['lat'=32,'ch'=8] {'ch'}, dimensions={0} | all-to-all | bytes 655360 | tf_op jit(solution)/shard_map/all_to_all | solution.py:395
  75.6 1.5 %longitude_stage.1 = bf16[20,8,1440]{2,1,0:T(8,128)(2,1)} custom-call(bf16[8,160,128]{2,1,0:T(8,128)(2,1)S(1)} %all_to_all.15.rows_ref, bf16[1024,720]{1,0:T(8,128)(2,1)S(1)} %copy-done), custom_call_target="tpu_custom_call" | custom-call | flops 503316480 | bytes 4194304 | tf_op jit(solution)/shard_map/longitude_stage/pallas_call | solution.py:357
  (11 shorter events, 0.1 us)
Async XLA Ops:
  0.0 42.4 %copy-start.1 = (f32[8,16,256]{2,1,0:T(8,128)S(1)}, f32[8,16,256]{2,1,0:T(8,128)}, u32[]{:S(2)}) copy-start(f32[8,16,256]{2,1,0:T(8,128)} %constant.73.clone.waves_ref) | copy-start | bytes 393220
  0.0 58.3 %copy-start.5 = (s32[32]{0:T(128)S(1)}, s32[32]{0:T(128)}, u32[]{:S(2)}) copy-start(s32[32]{0:T(128)} %slots_ref.3) | copy-start | bytes 388
  0.0 14.5 %copy-start.6 = (bf16[16,8,2,2,256]{4,3,2,1,0:T(2,128)(2,1)S(1)}, bf16[16,8,2,2,256]{4,3,2,1,0:T(2,128)(2,1)}, u32[]{:S(2)}) copy-start(bf16[16,8,2,2,256]{4,3,2,1,0:T(2,128)(2,1)} %param.8) | copy-start | bytes 786436
  0.0 42.4 %copy-start.2 = (bf16[3,20,6,9]{1,2,3,0:T(8,128)(2,1)S(1)}, bf16[3,20,6,9]{1,2,3,0:T(8,128)(2,1)}, u32[]{:S(2)}) copy-start(bf16[3,20,6,9]{1,2,3,0:T(8,128)(2,1)} %param.11) | copy-start | bytes 19444
  0.0 42.4 %copy-start.4 = (s32[20,6]{0,1:T(8,128)S(1)}, s32[20,6]{0,1:T(8,128)}, u32[]{:S(2)}) copy-start(s32[20,6]{0,1:T(8,128)} %param.12) | copy-start | bytes 1444
  0.0 42.4 %copy-start.3 = (bf16[3,64,64]{2,1,0:T(8,128)(2,1)S(1)}, bf16[3,64,64]{2,1,0:T(8,128)(2,1)}, u32[]{:S(2)}) copy-start(bf16[3,64,64]{2,1,0:T(8,128)(2,1)} %mix_ref) | copy-start | bytes 73732
  4.6 71.0 %copy-start = (bf16[1024,720]{1,0:T(8,128)(2,1)S(1)}, bf16[1024,720]{1,0:T(8,128)(2,1)}, u32[]{:S(2)}) copy-start(bf16[1024,720]{1,0:T(8,128)(2,1)} %constant.74.clone.table_ref) | copy-start | bytes 4423684
  4.6 30.7 %all-to-all-start = ((bf16[32,40,256]{2,1,0:T(8,128)(2,1)}), bf16[32,40,256]{2,1,0:T(8,128)(2,1)S(1)}, u32[]{:S(2)}, u32[]{:S(2)}) async-start(bf16[32,40,256]{2,1,0:T(8,128)(2,1)} %pick.1), calls=%async_computation | async-start | bytes 1310720 | tf_op jit(solution)/shard_map/all_to_all | solution.py:376
  14.7 9.2 %collective-permute-start = (bf16[4,64,256]{2,1,0:T(8,128)(2,1)S(1)}, bf16[4,64,256]{2,1,0:T(8,128)(2,1)S(1)}, u32[]{:S(2)}, u32[]{:S(2)}) collective-permute-start(bf16[4,64,256]{2,1,0:T(8,128)(2,1)S(1)} %get-tuple-element.25), channel_id=1, source_target_pairs={{0,1},{1,0},{2,3},{3,2},{4,5},{5,4},{6,7},{7,6},{8,9},{9,8},{10,11... | collective-permute-start | bytes 393224 | tf_op jit(solution)/shard_map/ppermute | solution.py:381
  24.0 5.0 %collective-permute-start.1 = (bf16[2,64,256]{2,1,0:T(8,128)(2,1)S(1)}, bf16[2,64,256]{2,1,0:T(8,128)(2,1)S(1)}, u32[]{:S(2)}, u32[]{:S(2)}) collective-permute-start(bf16[2,64,256]{2,1,0:T(8,128)(2,1)S(1)} %get-tuple-element.23), channel_id=1, source_target_pairs={{0,2},{1,3},{2,4},{3,5},{4,6},{5,7},{6,0},{7,1},{8,10},{9,11},{10,... | collective-permute-start | bytes 196616 | tf_op jit(solution)/shard_map/ppermute | solution.py:387
  25.6 5.9 %collective-permute-start.2 = (bf16[2,64,256]{2,1,0:T(8,128)(2,1)S(1)}, bf16[2,64,256]{2,1,0:T(8,128)(2,1)S(1)}, u32[]{:S(2)}, u32[]{:S(2)}) collective-permute-start(bf16[2,64,256]{2,1,0:T(8,128)(2,1)S(1)} %get-tuple-element.24), channel_id=1, source_target_pairs={{0,4},{1,5},{2,6},{3,7},{4,0},{5,1},{6,2},{7,3},{8,12},{9,13},{10,... | collective-permute-start | bytes 196616 | tf_op jit(solution)/shard_map/ppermute | solution.py:387
  26.5 5.0 %collective-permute-start.3 = (bf16[2,64,256]{2,1,0:T(8,128)(2,1)S(1)}, bf16[2,64,256]{2,1,0:T(8,128)(2,1)S(1)}, u32[]{:S(2)}, u32[]{:S(2)}) collective-permute-start(bf16[2,64,256]{2,1,0:T(8,128)(2,1)S(1)} %get-tuple-element.21), channel_id=1, source_target_pairs={{0,6},{1,7},{2,0},{3,1},{4,2},{5,3},{6,4},{7,5},{8,14},{9,15},{10,... | collective-permute-start | bytes 196616 | tf_op jit(solution)/shard_map/ppermute | solution.py:387
  36.9 21.4 %all-to-all-start.1 = ((bf16[32,48,128]{2,1,0:T(8,128)(2,1)}), bf16[32,48,128]{2,1,0:T(8,128)(2,1)S(1)}, u32[]{:S(2)}, u32[]{:S(2)}) async-start(bf16[32,48,128]{2,1,0:T(8,128)(2,1)} %order_stage.1), calls=%async_computation.1 | async-start | bytes 786432 | tf_op jit(solution)/shard_map/all_to_all | solution.py:392

commit v8 on v7

--- a/solution.py
+++ b/solution.py
@@ -153,7 +153,7 @@
 
 
 def order_kernel(leg_ref, *refs):
-    pieces_in, (out_ref, raw, specs, full) = refs[:TURNS], refs[TURNS:]
+    pieces_in, (out_ref, raw, specs, full) = refs[:PAIR], refs[PAIR:]
     half = NLAT // 2
     ch_index = lax.axis_index("ch")
     side = lax.rem(ch_index, PAIR)
@@ -164,7 +164,7 @@
             for h in range(STEPS // LANES):
                 lanes = slice(h * LANES, (h + 1) * LANES)
                 start = pl.multiple_of(source * C, C)
-                specs[h, pl.ds(start, C), :] = pieces_in[d][q, :, lanes].astype(F32)
+                specs[h, pl.ds(start, C), :] = pieces_in[q][d, :, lanes].astype(F32)
     for h in range(STEPS // LANES):
         lanes = slice(h * LANES, (h + 1) * LANES)
         lines = leg_ref[:, :, lanes].astype(F32).reshape(LATS * ROWS * SUB, LANES)
@@ -224,7 +224,7 @@
     return pl.pallas_call(
         order_kernel,
         out_shape=jax.ShapeDtypeStruct((LATS, HALO_ROWS * SUB, LANES), BF),
-        in_specs=[pl.BlockSpec(memory_space=VMEM)] * (1 + TURNS),
+        in_specs=[pl.BlockSpec(memory_space=VMEM)] * (1 + PAIR),
         out_specs=pl.BlockSpec(memory_space=VMEM),
         scratch_shapes=[
             pltpu.VMEM((STEPS // LANES, LATS * SUB * ROWS + MARGIN, LANES), F32),
@@ -376,15 +376,16 @@
     leg = lax.all_to_all(picked, "lat", 0, 0, tiled=True)
     blocks = spectrum.reshape(TURNS, PAIR, C, STEPS)
     turn, side = ch_index // PAIR, ch_index % PAIR
-    kept = lax.dynamic_index_in_dim(blocks, side, 1, keepdims=False)
-    given = lax.dynamic_index_in_dim(blocks, 1 - side, 1, keepdims=False)
-    taken = lax.ppermute(given, "ch", [(j, j ^ 1) for j in range(CHS)])
-    both = jnp.stack([kept, taken], axis=1)
     pieces = []
     for d in range(TURNS):
-        piece = lax.dynamic_index_in_dim(both, (turn + d) % TURNS, 0, keepdims=False)
+        piece = lax.dynamic_index_in_dim(blocks, (turn + d) % TURNS, 0, keepdims=False)
         shift = [(j, (j + PAIR * d) % CHS) for j in range(CHS)]
         pieces.append(lax.ppermute(piece, "ch", shift) if d else piece)
+    both = jnp.stack(pieces, axis=0)
+    kept = lax.dynamic_index_in_dim(both, side, 1, keepdims=False)
+    given = lax.dynamic_index_in_dim(both, 1 - side, 1, keepdims=False)
+    taken = lax.ppermute(given, "ch", [(j, j ^ 1) for j in range(CHS)])
+    pieces = [kept, taken]
     by_order = order_stage(leg, pieces)
     by_order, kernel_values, near_rows, mix_weights = lax.optimization_barrier(
         (by_order, kernel_values, near_rows, mix_weights)

time: 77.4 us -> 75.6 us (0.977)
  starting transfers between devices: 23.3 us -> 21.6 us
    all_to_all x1, starting transfers between devices: 5.51 us -> 3.88 us  [per_device(): by_row = lax.all_to_all(by_order, 'lat', 0, 0, tiled=True)]
  transfers between devices with their start and end apart: 6 -> 6, of which waited for: 4 -> 5; matrix products, arithmetic and copies ran while one was open for 0% -> 0% of each run, Pallas kernels for 1% -> 1%
where the time goes in v8:
time: 75.6 us; the launch traced here: 75.3 us
  waiting for transfers between devices  27.9 us (37%)
  starting transfers between devices  21.6 us (29%)
  blocking collectives  14.8 us (20%)
  Pallas kernels  10.6 us (14%)
    all_to_all x1, waiting for transfers between devices, per_device(): by_row = lax.all_to_all(by_order, 'lat', 0, 0, tiled=True)  15.3 us
    all_to_all x1, blocking collectives, per_device(): own = lax.all_to_all(mixed, 'ch', 0, 0, tiled=True)  14.8 us
    all_to_all x1, starting transfers between devices, per_device(): leg = lax.all_to_all(picked, 'lat', 0, 0, tiled=True)  9.92 us
    ppermute x1, waiting for transfers between devices, per_device(): taken = lax.ppermute(given, 'ch', [(j, j ^ 1) for j in range(CHS)])  5.98 us
    ppermute x3, starting transfers between devices, per_device(): pieces.append(lax.ppermute(piece, 'ch', shift) if d else piece)  5 us
    pallas_call x1, Pallas kernels, pick(): pl.pallas_call(pick_kernel, out_shape=jax.ShapeDtypeStruct((LATS, ROWS *...  4.53 us
    all_to_all x1, waiting for transfers between devices, per_device(): leg = lax.all_to_all(picked, 'lat', 0, 0, tiled=True)  4.08 us
    all_to_all x1, starting transfers between devices, per_device(): by_row = lax.all_to_all(by_order, 'lat', 0, 0, tiled=True)  3.88 us
  transfers between devices with their start and end apart: 6, of which 5 were waited for; matrix products, arithmetic and copies ran while one was open for 0% of the time, Pallas kernels for 1%

profile of v8, /device:TPU:8, one launch (start us, length us, event | category | flops | bytes accessed | tf_op | source)
XLA Modules:
  0.0 75.3 jit_solution(3463115351528310647)
XLA Ops:
  0.0 0.0 copy-start.2
  0.0 0.0 copy-start.4
  0.0 0.0 copy-start.3
  0.0 4.5 %pick.1 = bf16[32,40,256]{2,1,0:T(8,128)(2,1)} custom-call(s32[32]{0:T(128)} %slots_ref.3, bf16[20,256,512]{2,1,0:T(8,128)(2,1)} %leg_ref.1), custom_call_target="tpu_custom_call" | custom-call | flops 335544320 | bytes 6291456 | tf_op jit(solution)/shard_map/pick/pallas_call | solution.py:138
  4.6 0.0 copy-start
  4.6 9.9 %all-to-all-start = ((bf16[32,40,256]{2,1,0:T(8,128)(2,1)}), bf16[32,40,256]{2,1,0:T(8,128)(2,1)S(1)}, u32[]{:S(2)}, u32[]{:S(2)}) async-start(bf16[32,40,256]{2,1,0:T(8,128)(2,1)} %pick.1), calls=%async_computation | async-start | bytes 1310720 | tf_op jit(solution)/shard_map/all_to_all | solution.py:376
  14.6 0.1 reshape.3
  14.8 0.5 collective-permute-start.2
  15.3 2.6 %collective-permute-start.1 = (bf16[2,64,256]{2,1,0:T(8,128)(2,1)S(1)}, bf16[2,64,256]{2,1,0:T(8,128)(2,1)S(1)}, u32[]{:S(2)}, u32[]{:S(2)}) collective-permute-start(bf16[2,64,256]{2,1,0:T(8,128)(2,1)S(1)} %get-tuple-element.25), channel_id=1, source_target_pairs={{0,4},{1,5},{2,6},{3,7},{4,0},{5,1},{6,2},{7,3},{8,12},{9,13},{10,... | collective-permute-start | bytes 196616 | tf_op jit(solution)/shard_map/ppermute | solution.py:383
  17.9 1.9 %collective-permute-start = (bf16[2,64,256]{2,1,0:T(8,128)(2,1)S(1)}, bf16[2,64,256]{2,1,0:T(8,128)(2,1)S(1)}, u32[]{:S(2)}, u32[]{:S(2)}) collective-permute-start(bf16[2,64,256]{2,1,0:T(8,128)(2,1)S(1)} %get-tuple-element.26), channel_id=1, source_target_pairs={{0,2},{1,3},{2,4},{3,5},{4,6},{5,7},{6,0},{7,1},{8,10},{9,11},{10,... | collective-permute-start | bytes 196616 | tf_op jit(solution)/shard_map/ppermute | solution.py:383
  19.8 0.0 collective-permute-done.2
  19.8 1.8 %collective-permute-done.1 = bf16[2,64,256]{2,1,0:T(8,128)(2,1)S(1)} collective-permute-done((bf16[2,64,256]{2,1,0:T(8,128)(2,1)S(1)}, bf16[2,64,256]{2,1,0:T(8,128)(2,1)S(1)}, u32[]{:S(2)}, u32[]{:S(2)}) %collective-permute-start.1) | collective-permute-done | bytes 65568 | tf_op jit(solution)/shard_map/ppermute | solution.py:383
  21.5 0.8 %collective-permute-done = bf16[2,64,256]{2,1,0:T(8,128)(2,1)S(1)} collective-permute-done((bf16[2,64,256]{2,1,0:T(8,128)(2,1)S(1)}, bf16[2,64,256]{2,1,0:T(8,128)(2,1)S(1)}, u32[]{:S(2)}, u32[]{:S(2)}) %collective-permute-start) | collective-permute-done | bytes 65568 | tf_op jit(solution)/shard_map/ppermute | solution.py:383
  22.4 2.8 %collective-permute-start.3 = (bf16[4,64,256]{2,1,0:T(8,128)(2,1)S(1)}, bf16[4,64,256]{2,1,0:T(8,128)(2,1)S(1)}, u32[]{:S(2)}, u32[]{:S(2)}) collective-permute-start(bf16[4,64,256]{2,1,0:T(8,128)(2,1)S(1)} %get-tuple-element.21), channel_id=1, source_target_pairs={{0,1},{1,0},{2,3},{3,2},{4,5},{5,4},{6,7},{7,6},{8,9},{9,8},{10,11... | collective-permute-start | bytes 393224 | tf_op jit(solution)/shard_map/ppermute | solution.py:387
  25.2 6.0 %collective-permute-done.3.refs_1_ = bf16[4,64,256]{2,1,0:T(8,128)(2,1)S(1)} collective-permute-done((bf16[4,64,256]{2,1,0:T(8,128)(2,1)S(1)}, bf16[4,64,256]{2,1,0:T(8,128)(2,1)S(1)}, u32[]{:S(2)}, u32[]{:S(2)}) %collective-permute-start.3) | collective-permute-done | bytes 131104 | tf_op jit(solution)/shard_map/ppermute | solution.py:387
  31.2 4.1 %all-to-all-done.leg_ref = bf16[32,40,256]{2,1,0:T(8,128)(2,1)S(1)} async-done(((bf16[32,40,256]{2,1,0:T(8,128)(2,1)}), bf16[32,40,256]{2,1,0:T(8,128)(2,1)S(1)}, u32[]{:S(2)}, u32[]{:S(2)}) %all-to-all-start) | async-done | bytes 655392 | tf_op jit(solution)/shard_map/all_to_all | solution.py:376
  35.3 1.6 %order_stage.1 = bf16[32,48,128]{2,1,0:T(8,128)(2,1)} custom-call(bf16[32,40,256]{2,1,0:T(8,128)(2,1)S(1)} %all-to-all-done.leg_ref, bf16[4,64,256]{2,1,0:T(8,128)(2,1)S(1)} %get-tuple-element.22.refs_0_, bf16[4,64,256]{2,1,0:T(8,128)(2,1)S(1)} %collective-permute-done.3.refs_1_), custom_call_target="tpu_custom_call" | custom-call | flops 734003200 | bytes 2097152 | tf_op jit(solution)/shard_map/order_stage/pallas_call | solution.py:224
  36.9 3.9 %all-to-all-start.1 = ((bf16[32,48,128]{2,1,0:T(8,128)(2,1)}), bf16[32,48,128]{2,1,0:T(8,128)(2,1)S(1)}, u32[]{:S(2)}, u32[]{:S(2)}) async-start(bf16[32,48,128]{2,1,0:T(8,128)(2,1)} %order_stage.1), calls=%async_computation.1 | async-start | bytes 786432 | tf_op jit(solution)/shard_map/all_to_all | solution.py:393
  40.8 0.6 coef_stage.1
  41.4 15.3 %all-to-all-done.1.rows_ref = bf16[32,48,128]{2,1,0:T(8,128)(2,1)S(1)} async-done(((bf16[32,48,128]{2,1,0:T(8,128)(2,1)}), bf16[32,48,128]{2,1,0:T(8,128)(2,1)S(1)}, u32[]{:S(2)}, u32[]{:S(2)}) %all-to-all-start.1) | async-done | bytes 393248 | tf_op jit(solution)/shard_map/all_to_all | solution.py:393
  56.7 0.0 copy-done.5
  56.7 2.4 %row_stage.1 = bf16[8,160,128]{2,1,0:T(8,128)(2,1)S(1)} custom-call(s32[32]{0:T(128)S(1)} %copy-done.5, bf16[32,48,128]{2,1,0:T(8,128)(2,1)S(1)} %all-to-all-done.1.rows_ref, f32[15,20,256]{2,1,0:T(8,128)S(1)} %get-tuple-element.19.coef_ref, bf16[192,128]{1,0:T(8,128)(2,1)S(1)} %get-tuple-element.20.mix_ref), custom_call_target="tpu_custom_call" | custom-call | flops 209715200 | bytes 2097152 | tf_op jit(solution)/shard_map/row_stage/pallas_call | solution.py:312
  59.1 14.8 %all_to_all.15.rows_ref = bf16[8,160,128]{2,1,0:T(8,128)(2,1)S(1)} all-to-all(bf16[8,160,128]{2,1,0:T(8,128)(2,1)S(1)} %row_stage.1), channel_id=1, replica_groups=mesh['lat'=32,'ch'=8] {'ch'}, dimensions={0} | all-to-all | bytes 655360 | tf_op jit(solution)/shard_map/all_to_all | solution.py:396
  73.8 1.5 %longitude_stage.1 = bf16[20,8,1440]{2,1,0:T(8,128)(2,1)} custom-call(bf16[8,160,128]{2,1,0:T(8,128)(2,1)S(1)} %all_to_all.15.rows_ref, bf16[1024,720]{1,0:T(8,128)(2,1)S(1)} %copy-done), custom_call_target="tpu_custom_call" | custom-call | flops 503316480 | bytes 4194304 | tf_op jit(solution)/shard_map/longitude_stage/pallas_call | solution.py:357
  (12 shorter events, 0.1 us)
Async XLA Ops:
  0.0 40.8 %copy-start.1 = (f32[8,16,256]{2,1,0:T(8,128)S(1)}, f32[8,16,256]{2,1,0:T(8,128)}, u32[]{:S(2)}) copy-start(f32[8,16,256]{2,1,0:T(8,128)} %constant.73.clone.waves_ref) | copy-start | bytes 393220
  0.0 56.7 %copy-start.5 = (s32[32]{0:T(128)S(1)}, s32[32]{0:T(128)}, u32[]{:S(2)}) copy-start(s32[32]{0:T(128)} %slots_ref.3) | copy-start | bytes 388
  0.0 14.6 %copy-start.6 = (bf16[16,8,2,2,256]{4,3,2,1,0:T(2,128)(2,1)S(1)}, bf16[16,8,2,2,256]{4,3,2,1,0:T(2,128)(2,1)}, u32[]{:S(2)}) copy-start(bf16[16,8,2,2,256]{4,3,2,1,0:T(2,128)(2,1)} %param.8) | copy-start | bytes 786436
  0.0 40.8 %copy-start.2 = (bf16[3,20,6,9]{1,2,3,0:T(8,128)(2,1)S(1)}, bf16[3,20,6,9]{1,2,3,0:T(8,128)(2,1)}, u32[]{:S(2)}) copy-start(bf16[3,20,6,9]{1,2,3,0:T(8,128)(2,1)} %param.11) | copy-start | bytes 19444
  0.0 40.8 %copy-start.4 = (s32[20,6]{0,1:T(8,128)S(1)}, s32[20,6]{0,1:T(8,128)}, u32[]{:S(2)}) copy-start(s32[20,6]{0,1:T(8,128)} %param.12) | copy-start | bytes 1444
  0.0 40.8 %copy-start.3 = (bf16[3,64,64]{2,1,0:T(8,128)(2,1)S(1)}, bf16[3,64,64]{2,1,0:T(8,128)(2,1)}, u32[]{:S(2)}) copy-start(bf16[3,64,64]{2,1,0:T(8,128)(2,1)} %mix_ref) | copy-start | bytes 73732
  4.6 69.3 %copy-start = (bf16[1024,720]{1,0:T(8,128)(2,1)S(1)}, bf16[1024,720]{1,0:T(8,128)(2,1)}, u32[]{:S(2)}) copy-start(bf16[1024,720]{1,0:T(8,128)(2,1)} %constant.74.clone.table_ref) | copy-start | bytes 4423684
  4.6 30.7 %all-to-all-start = ((bf16[32,40,256]{2,1,0:T(8,128)(2,1)}), bf16[32,40,256]{2,1,0:T(8,128)(2,1)S(1)}, u32[]{:S(2)}, u32[]{:S(2)}) async-start(bf16[32,40,256]{2,1,0:T(8,128)(2,1)} %pick.1), calls=%async_computation | async-start | bytes 1310720 | tf_op jit(solution)/shard_map/all_to_all | solution.py:376
  14.8 5.0 %collective-permute-start.2 = (bf16[2,64,256]{2,1,0:T(8,128)(2,1)S(1)}, bf16[2,64,256]{2,1,0:T(8,128)(2,1)S(1)}, u32[]{:S(2)}, u32[]{:S(2)}) collective-permute-start(bf16[2,64,256]{2,1,0:T(8,128)(2,1)S(1)} %get-tuple-element.24), channel_id=1, source_target_pairs={{0,6},{1,7},{2,0},{3,1},{4,2},{5,3},{6,4},{7,5},{8,14},{9,15},{10,... | collective-permute-start | bytes 196616 | tf_op jit(solution)/shard_map/ppermute | solution.py:383
  15.3 6.2 %collective-permute-start.1 = (bf16[2,64,256]{2,1,0:T(8,128)(2,1)S(1)}, bf16[2,64,256]{2,1,0:T(8,128)(2,1)S(1)}, u32[]{:S(2)}, u32[]{:S(2)}) collective-permute-start(bf16[2,64,256]{2,1,0:T(8,128)(2,1)S(1)} %get-tuple-element.25), channel_id=1, source_target_pairs={{0,4},{1,5},{2,6},{3,7},{4,0},{5,1},{6,2},{7,3},{8,12},{9,13},{10,... | collective-permute-start | bytes 196616 | tf_op jit(solution)/shard_map/ppermute | solution.py:383
  17.9 4.4 %collective-permute-start = (bf16[2,64,256]{2,1,0:T(8,128)(2,1)S(1)}, bf16[2,64,256]{2,1,0:T(8,128)(2,1)S(1)}, u32[]{:S(2)}, u32[]{:S(2)}) collective-permute-start(bf16[2,64,256]{2,1,0:T(8,128)(2,1)S(1)} %get-tuple-element.26), channel_id=1, source_target_pairs={{0,2},{1,3},{2,4},{3,5},{4,6},{5,7},{6,0},{7,1},{8,10},{9,11},{10,... | collective-permute-start | bytes 196616 | tf_op jit(solution)/shard_map/ppermute | solution.py:383
  22.4 8.8 %collective-permute-start.3 = (bf16[4,64,256]{2,1,0:T(8,128)(2,1)S(1)}, bf16[4,64,256]{2,1,0:T(8,128)(2,1)S(1)}, u32[]{:S(2)}, u32[]{:S(2)}) collective-permute-start(bf16[4,64,256]{2,1,0:T(8,128)(2,1)S(1)} %get-tuple-element.21), channel_id=1, source_target_pairs={{0,1},{1,0},{2,3},{3,2},{4,5},{5,4},{6,7},{7,6},{8,9},{9,8},{10,11... | collective-permute-start | bytes 393224 | tf_op jit(solution)/shard_map/ppermute | solution.py:387
  36.9 19.8 %all-to-all-start.1 = ((bf16[32,48,128]{2,1,0:T(8,128)(2,1)}), bf16[32,48,128]{2,1,0:T(8,128)(2,1)S(1)}, u32[]{:S(2)}, u32[]{:S(2)}) async-start(bf16[32,48,128]{2,1,0:T(8,128)(2,1)} %order_stage.1), calls=%async_computation.1 | async-start | bytes 786432 | tf_op jit(solution)/shard_map/all_to_all | solution.py:393

commit v9 on v8

--- a/solution.py
+++ b/solution.py
@@ -152,9 +152,8 @@
     )(block_slots, legendre)
 
 
-def order_kernel(leg_ref, *refs):
-    pieces_in, (out_ref, raw, specs, full) = refs[:PAIR], refs[PAIR:]
-    half = NLAT // 2
+def spec_kernel(*refs):
+    pieces_in, (out_ref, specs) = refs[:PAIR], refs[PAIR:]
     ch_index = lax.axis_index("ch")
     side = lax.rem(ch_index, PAIR)
     for d in range(TURNS):
@@ -165,6 +164,39 @@
                 lanes = slice(h * LANES, (h + 1) * LANES)
                 start = pl.multiple_of(source * C, C)
                 specs[h, pl.ds(start, C), :] = pieces_in[q][d, :, lanes].astype(F32)
+    for t in range(SUB):
+        for p in range(2):
+            pieces = []
+            for x in range(2):
+                for j in range(CHS):
+                    start = j * C + t * 4 * OWN + p * 2 + x
+                    pieces.append(
+                        jnp.concatenate(
+                            [
+                                specs[h, pl.ds(start, OWN, stride=4), :]
+                                for h in range(STEPS // LANES)
+                            ],
+                            axis=1,
+                        )
+                    )
+            out_ref[t, p] = jnp.concatenate(pieces, axis=0).astype(BF)
+
+
+def spec_stage(pieces):
+    return pl.pallas_call(
+        spec_kernel,
+        out_shape=jax.ShapeDtypeStruct((SUB, 2, LANES, STEPS), BF),
+        in_specs=[pl.BlockSpec(memory_space=VMEM)] * PAIR,
+        out_specs=pl.BlockSpec(memory_space=VMEM),
+        scratch_shapes=[pltpu.VMEM((STEPS // LANES, CHS * C + MARGIN, LANES), F32)],
+        compiler_params=pltpu.CompilerParams(vmem_limit_bytes=8 << 20),
+        cost_estimate=pl.CostEstimate(flops=1 << 20, bytes_accessed=1 << 19, transcendentals=0),
+        name="spec_stage",
+    )(*pieces)
+
+
+def order_kernel(leg_ref, spec_ref, out_ref, raw, full):
+    half = NLAT // 2
     for h in range(STEPS // LANES):
         lanes = slice(h * LANES, (h + 1) * LANES)
         lines = leg_ref[:, :, lanes].astype(F32).reshape(LATS * ROWS * SUB, LANES)
@@ -172,7 +204,6 @@
     rows = lax.broadcasted_iota(jnp.int32, (LANES, LANES), 0)
     cols = lax.broadcasted_iota(jnp.int32, (LANES, LANES), 1)
     turn = jnp.where(rows + cols == LANES - 1, 1.0, 0.0).astype(BF)
-    stride = 4
     full[:16, :] = jnp.zeros((16, LANES), F32)
     full[SUB * NLAT :, :] = jnp.zeros((2 * EDGE, LANES), F32)
     for t in range(SUB):
@@ -191,22 +222,7 @@
             ],
             axis=0,
         )
-        coeffs = []
-        for p in range(2):
-            pieces = []
-            for x in range(2):
-                for j in range(CHS):
-                    start = j * C + t * 4 * OWN + p * 2 + x
-                    pieces.append(
-                        jnp.concatenate(
-                            [
-                                specs[h, pl.ds(start, OWN, stride=stride), :]
-                                for h in range(STEPS // LANES)
-                            ],
-                            axis=1,
-                        )
-                    )
-            coeffs.append(jnp.concatenate(pieces, axis=0).astype(BF))
+        coeffs = [spec_ref[t, p] for p in range(2)]
 
         def dot(a, b):
             return lax.dot_general(a, b, NT, preferred_element_type=F32)
@@ -220,21 +236,20 @@
         out_ref[i] = full[start : start + HALO_ROWS * SUB, :].astype(BF)
 
 
-def order_stage(leg, pieces):
+def order_stage(leg, spec):
     return pl.pallas_call(
         order_kernel,
         out_shape=jax.ShapeDtypeStruct((LATS, HALO_ROWS * SUB, LANES), BF),
-        in_specs=[pl.BlockSpec(memory_space=VMEM)] * (1 + PAIR),
+        in_specs=[pl.BlockSpec(memory_space=VMEM)] * 2,
         out_specs=pl.BlockSpec(memory_space=VMEM),
         scratch_shapes=[
             pltpu.VMEM((STEPS // LANES, LATS * SUB * ROWS + MARGIN, LANES), F32),
-            pltpu.VMEM((STEPS // LANES, CHS * C + MARGIN, LANES), F32),
             pltpu.VMEM((SUB * NLAT + 2 * EDGE, LANES), F32),
         ],
         compiler_params=pltpu.CompilerParams(vmem_limit_bytes=24 << 20),
         cost_estimate=pl.CostEstimate(flops=700 << 20, bytes_accessed=2 << 20, transcendentals=0),
         name="order_stage",
-    )(leg, *pieces)
+    )(leg, spec)
 
 
 def coef_kernel(values_ref, near_ref, mix_ref, waves_ref, coef_ref, mixed_ref, taps):
@@ -385,8 +400,7 @@
     kept = lax.dynamic_index_in_dim(both, side, 1, keepdims=False)
     given = lax.dynamic_index_in_dim(both, 1 - side, 1, keepdims=False)
     taken = lax.ppermute(given, "ch", [(j, j ^ 1) for j in range(CHS)])
-    pieces = [kept, taken]
-    by_order = order_stage(leg, pieces)
+    by_order = order_stage(leg, spec_stage([kept, taken]))
     by_order, kernel_values, near_rows, mix_weights = lax.optimization_barrier(
         (by_order, kernel_values, near_rows, mix_weights)
     )

time: 75.6 us -> 75.7 us (level)
  no operation moved by 1% of the time
where the time goes in v9:
time: 75.7 us; the launch traced here: 75.4 us
  waiting for transfers between devices  27.8 us (37%)
  starting transfers between devices  21.6 us (29%)
  blocking collectives  14.8 us (20%)
  Pallas kernels  10.6 us (14%)
    all_to_all x1, waiting for transfers between devices, per_device(): by_row = lax.all_to_all(by_order, 'lat', 0, 0, tiled=True)  15.3 us
    all_to_all x1, blocking collectives, per_device(): own = lax.all_to_all(mixed, 'ch', 0, 0, tiled=True)  14.8 us
    all_to_all x1, starting transfers between devices, per_device(): leg = lax.all_to_all(picked, 'lat', 0, 0, tiled=True)  9.93 us
    ppermute x1, waiting for transfers between devices, per_device(): taken = lax.ppermute(given, 'ch', [(j, j ^ 1) for j in range(CHS)])  5.99 us
    ppermute x3, starting transfers between devices, per_device(): pieces.append(lax.ppermute(piece, 'ch', shift) if d else piece)  5 us
    pallas_call x1, Pallas kernels, pick(): pl.pallas_call(pick_kernel, out_shape=jax.ShapeDtypeStruct((LATS, ROWS *...  4.53 us
    all_to_all x1, waiting for transfers between devices, per_device(): leg = lax.all_to_all(picked, 'lat', 0, 0, tiled=True)  4.01 us
    all_to_all x1, starting transfers between devices, per_device(): by_row = lax.all_to_all(by_order, 'lat', 0, 0, tiled=True)  3.88 us
  transfers between devices with their start and end apart: 6, of which 5 were waited for; matrix products, arithmetic and copies ran while one was open for 0% of the time, Pallas kernels for 1%

profile of v9, /device:TPU:8, one launch (start us, length us, event | category | flops | bytes accessed | tf_op | source)
XLA Modules:
  0.0 75.4 jit_solution(6816408261151747679)
XLA Ops:
  0.0 4.5 %pick.1 = bf16[32,40,256]{2,1,0:T(8,128)(2,1)} custom-call(s32[32]{0:T(128)} %slots_ref.3, bf16[20,256,512]{2,1,0:T(8,128)(2,1)} %leg_ref.1), custom_call_target="tpu_custom_call" | custom-call | flops 335544320 | bytes 6291456 | tf_op jit(solution)/shard_map/pick/pallas_call | solution.py:138
  4.5 0.0 copy-start.1
  4.5 0.0 copy-start.2
  4.6 0.0 copy-start.3
  4.6 0.0 copy-start.4
  4.6 0.0 copy-start
  4.6 9.9 %all-to-all-start = ((bf16[32,40,256]{2,1,0:T(8,128)(2,1)}), bf16[32,40,256]{2,1,0:T(8,128)(2,1)S(1)}, u32[]{:S(2)}, u32[]{:S(2)}) async-start(bf16[32,40,256]{2,1,0:T(8,128)(2,1)} %pick.1), calls=%async_computation | async-start | bytes 1310720 | tf_op jit(solution)/shard_map/all_to_all | solution.py:391
  14.6 0.1 reshape.3
  14.8 0.5 collective-permute-start.2
  15.3 2.6 %collective-permute-start.1 = (bf16[2,64,256]{2,1,0:T(8,128)(2,1)S(1)}, bf16[2,64,256]{2,1,0:T(8,128)(2,1)S(1)}, u32[]{:S(2)}, u32[]{:S(2)}) collective-permute-start(bf16[2,64,256]{2,1,0:T(8,128)(2,1)S(1)} %get-tuple-element.25), channel_id=1, source_target_pairs={{0,4},{1,5},{2,6},{3,7},{4,0},{5,1},{6,2},{7,3},{8,12},{9,13},{10,... | collective-permute-start | bytes 196616 | tf_op jit(solution)/shard_map/ppermute | solution.py:398
  17.9 1.9 %collective-permute-start = (bf16[2,64,256]{2,1,0:T(8,128)(2,1)S(1)}, bf16[2,64,256]{2,1,0:T(8,128)(2,1)S(1)}, u32[]{:S(2)}, u32[]{:S(2)}) collective-permute-start(bf16[2,64,256]{2,1,0:T(8,128)(2,1)S(1)} %get-tuple-element.26), channel_id=1, source_target_pairs={{0,2},{1,3},{2,4},{3,5},{4,6},{5,7},{6,0},{7,1},{8,10},{9,11},{10,... | collective-permute-start | bytes 196616 | tf_op jit(solution)/shard_map/ppermute | solution.py:398
  19.8 1.8 %collective-permute-done.1 = bf16[2,64,256]{2,1,0:T(8,128)(2,1)S(1)} collective-permute-done((bf16[2,64,256]{2,1,0:T(8,128)(2,1)S(1)}, bf16[2,64,256]{2,1,0:T(8,128)(2,1)S(1)}, u32[]{:S(2)}, u32[]{:S(2)}) %collective-permute-start.1) | collective-permute-done | bytes 65568 | tf_op jit(solution)/shard_map/ppermute | solution.py:398
  21.6 0.8 %collective-permute-done = bf16[2,64,256]{2,1,0:T(8,128)(2,1)S(1)} collective-permute-done((bf16[2,64,256]{2,1,0:T(8,128)(2,1)S(1)}, bf16[2,64,256]{2,1,0:T(8,128)(2,1)S(1)}, u32[]{:S(2)}, u32[]{:S(2)}) %collective-permute-start) | collective-permute-done | bytes 65568 | tf_op jit(solution)/shard_map/ppermute | solution.py:398
  22.4 2.8 %collective-permute-start.3 = (bf16[4,64,256]{2,1,0:T(8,128)(2,1)S(1)}, bf16[4,64,256]{2,1,0:T(8,128)(2,1)S(1)}, u32[]{:S(2)}, u32[]{:S(2)}) collective-permute-start(bf16[4,64,256]{2,1,0:T(8,128)(2,1)S(1)} %get-tuple-element.21), channel_id=1, source_target_pairs={{0,1},{1,0},{2,3},{3,2},{4,5},{5,4},{6,7},{7,6},{8,9},{9,8},{10,11... | collective-permute-start | bytes 393224 | tf_op jit(solution)/shard_map/ppermute | solution.py:402
  25.2 6.0 %collective-permute-done.3.refs_1_ = bf16[4,64,256]{2,1,0:T(8,128)(2,1)S(1)} collective-permute-done((bf16[4,64,256]{2,1,0:T(8,128)(2,1)S(1)}, bf16[4,64,256]{2,1,0:T(8,128)(2,1)S(1)}, u32[]{:S(2)}, u32[]{:S(2)}) %collective-permute-start.3) | collective-permute-done | bytes 131104 | tf_op jit(solution)/shard_map/ppermute | solution.py:402
  31.2 0.1 spec_stage.1.spec_ref
  31.3 4.0 %all-to-all-done.leg_ref = bf16[32,40,256]{2,1,0:T(8,128)(2,1)S(1)} async-done(((bf16[32,40,256]{2,1,0:T(8,128)(2,1)}), bf16[32,40,256]{2,1,0:T(8,128)(2,1)S(1)}, u32[]{:S(2)}, u32[]{:S(2)}) %all-to-all-start) | async-done | bytes 655392 | tf_op jit(solution)/shard_map/all_to_all | solution.py:391
  35.3 1.6 %order_stage.1 = bf16[32,48,128]{2,1,0:T(8,128)(2,1)} custom-call(bf16[32,40,256]{2,1,0:T(8,128)(2,1)S(1)} %all-to-all-done.leg_ref, bf16[2,2,128,256]{3,2,1,0:T(8,128)(2,1)S(1)} %spec_stage.1.spec_ref), custom_call_target="tpu_custom_call" | custom-call | flops 734003200 | bytes 2097152 | tf_op jit(solution)/shard_map/order_stage/pallas_call | solution.py:240
  36.9 3.9 %all-to-all-start.1 = ((bf16[32,48,128]{2,1,0:T(8,128)(2,1)}), bf16[32,48,128]{2,1,0:T(8,128)(2,1)S(1)}, u32[]{:S(2)}, u32[]{:S(2)}) async-start(bf16[32,48,128]{2,1,0:T(8,128)(2,1)} %order_stage.1), calls=%async_computation.1 | async-start | bytes 786432 | tf_op jit(solution)/shard_map/all_to_all | solution.py:407
  40.8 0.6 coef_stage.1
  41.4 15.3 %all-to-all-done.1.rows_ref = bf16[32,48,128]{2,1,0:T(8,128)(2,1)S(1)} async-done(((bf16[32,48,128]{2,1,0:T(8,128)(2,1)}), bf16[32,48,128]{2,1,0:T(8,128)(2,1)S(1)}, u32[]{:S(2)}, u32[]{:S(2)}) %all-to-all-start.1) | async-done | bytes 393248 | tf_op jit(solution)/shard_map/all_to_all | solution.py:407
  56.7 2.4 %row_stage.1 = bf16[8,160,128]{2,1,0:T(8,128)(2,1)S(1)} custom-call(s32[32]{0:T(128)S(1)} %copy-done.5, bf16[32,48,128]{2,1,0:T(8,128)(2,1)S(1)} %all-to-all-done.1.rows_ref, f32[15,20,256]{2,1,0:T(8,128)S(1)} %get-tuple-element.19.coef_ref, bf16[192,128]{1,0:T(8,128)(2,1)S(1)} %get-tuple-element.20.mix_ref), custom_call_target="tpu_custom_call" | custom-call | flops 209715200 | bytes 2097152 | tf_op jit(solution)/shard_map/row_stage/pallas_call | solution.py:327
  59.1 14.8 %all_to_all.15.rows_ref = bf16[8,160,128]{2,1,0:T(8,128)(2,1)S(1)} all-to-all(bf16[8,160,128]{2,1,0:T(8,128)(2,1)S(1)} %row_stage.1), channel_id=1, replica_groups=mesh['lat'=32,'ch'=8] {'ch'}, dimensions={0} | all-to-all | bytes 655360 | tf_op jit(solution)/shard_map/all_to_all | solution.py:410
  73.9 1.5 %longitude_stage.1 = bf16[20,8,1440]{2,1,0:T(8,128)(2,1)} custom-call(bf16[8,160,128]{2,1,0:T(8,128)(2,1)S(1)} %all_to_all.15.rows_ref, bf16[1024,720]{1,0:T(8,128)(2,1)S(1)} %copy-done), custom_call_target="tpu_custom_call" | custom-call | flops 503316480 | bytes 4194304 | tf_op jit(solution)/shard_map/longitude_stage/pallas_call | solution.py:372
  (13 shorter events, 0.1 us)
Async XLA Ops:
  0.0 14.6 %copy-start.6 = (bf16[16,8,2,2,256]{4,3,2,1,0:T(2,128)(2,1)S(1)}, bf16[16,8,2,2,256]{4,3,2,1,0:T(2,128)(2,1)}, u32[]{:S(2)}) copy-start(bf16[16,8,2,2,256]{4,3,2,1,0:T(2,128)(2,1)} %param.8) | copy-start | bytes 786436
  4.5 36.2 %copy-start.1 = (f32[8,16,256]{2,1,0:T(8,128)S(1)}, f32[8,16,256]{2,1,0:T(8,128)}, u32[]{:S(2)}) copy-start(f32[8,16,256]{2,1,0:T(8,128)} %constant.73.clone.waves_ref) | copy-start | bytes 393220
  4.5 36.2 %copy-start.2 = (bf16[3,20,6,9]{1,2,3,0:T(8,128)(2,1)S(1)}, bf16[3,20,6,9]{1,2,3,0:T(8,128)(2,1)}, u32[]{:S(2)}) copy-start(bf16[3,20,6,9]{1,2,3,0:T(8,128)(2,1)} %param.11) | copy-start | bytes 19444
  4.6 36.2 %copy-start.3 = (bf16[3,64,64]{2,1,0:T(8,128)(2,1)S(1)}, bf16[3,64,64]{2,1,0:T(8,128)(2,1)}, u32[]{:S(2)}) copy-start(bf16[3,64,64]{2,1,0:T(8,128)(2,1)} %mix_ref) | copy-start | bytes 73732
  4.6 36.2 %copy-start.4 = (s32[20,6]{0,1:T(8,128)S(1)}, s32[20,6]{0,1:T(8,128)}, u32[]{:S(2)}) copy-start(s32[20,6]{0,1:T(8,128)} %param.12) | copy-start | bytes 1444
  4.6 52.1 %copy-start.5 = (s32[32]{0:T(128)S(1)}, s32[32]{0:T(128)}, u32[]{:S(2)}) copy-start(s32[32]{0:T(128)} %slots_ref.3) | copy-start | bytes 388
  4.6 69.3 %copy-start = (bf16[1024,720]{1,0:T(8,128)(2,1)S(1)}, bf16[1024,720]{1,0:T(8,128)(2,1)}, u32[]{:S(2)}) copy-start(bf16[1024,720]{1,0:T(8,128)(2,1)} %constant.74.clone.table_ref) | copy-start | bytes 4423684
  4.6 30.7 %all-to-all-start = ((bf16[32,40,256]{2,1,0:T(8,128)(2,1)}), bf16[32,40,256]{2,1,0:T(8,128)(2,1)S(1)}, u32[]{:S(2)}, u32[]{:S(2)}) async-start(bf16[32,40,256]{2,1,0:T(8,128)(2,1)} %pick.1), calls=%async_computation | async-start | bytes 1310720 | tf_op jit(solution)/shard_map/all_to_all | solution.py:391
  14.8 5.0 %collective-permute-start.2 = (bf16[2,64,256]{2,1,0:T(8,128)(2,1)S(1)}, bf16[2,64,256]{2,1,0:T(8,128)(2,1)S(1)}, u32[]{:S(2)}, u32[]{:S(2)}) collective-permute-start(bf16[2,64,256]{2,1,0:T(8,128)(2,1)S(1)} %get-tuple-element.24), channel_id=1, source_target_pairs={{0,6},{1,7},{2,0},{3,1},{4,2},{5,3},{6,4},{7,5},{8,14},{9,15},{10,... | collective-permute-start | bytes 196616 | tf_op jit(solution)/shard_map/ppermute | solution.py:398
  15.3 6.2 %collective-permute-start.1 = (bf16[2,64,256]{2,1,0:T(8,128)(2,1)S(1)}, bf16[2,64,256]{2,1,0:T(8,128)(2,1)S(1)}, u32[]{:S(2)}, u32[]{:S(2)}) collective-permute-start(bf16[2,64,256]{2,1,0:T(8,128)(2,1)S(1)} %get-tuple-element.25), channel_id=1, source_target_pairs={{0,4},{1,5},{2,6},{3,7},{4,0},{5,1},{6,2},{7,3},{8,12},{9,13},{10,... | collective-permute-start | bytes 196616 | tf_op jit(solution)/shard_map/ppermute | solution.py:398
  17.9 4.4 %collective-permute-start = (bf16[2,64,256]{2,1,0:T(8,128)(2,1)S(1)}, bf16[2,64,256]{2,1,0:T(8,128)(2,1)S(1)}, u32[]{:S(2)}, u32[]{:S(2)}) collective-permute-start(bf16[2,64,256]{2,1,0:T(8,128)(2,1)S(1)} %get-tuple-element.26), channel_id=1, source_target_pairs={{0,2},{1,3},{2,4},{3,5},{4,6},{5,7},{6,0},{7,1},{8,10},{9,11},{10,... | collective-permute-start | bytes 196616 | tf_op jit(solution)/shard_map/ppermute | solution.py:398
  22.4 8.8 %collective-permute-start.3 = (bf16[4,64,256]{2,1,0:T(8,128)(2,1)S(1)}, bf16[4,64,256]{2,1,0:T(8,128)(2,1)S(1)}, u32[]{:S(2)}, u32[]{:S(2)}) collective-permute-start(bf16[4,64,256]{2,1,0:T(8,128)(2,1)S(1)} %get-tuple-element.21), channel_id=1, source_target_pairs={{0,1},{1,0},{2,3},{3,2},{4,5},{5,4},{6,7},{7,6},{8,9},{9,8},{10,11... | collective-permute-start | bytes 393224 | tf_op jit(solution)/shard_map/ppermute | solution.py:402
  36.9 19.8 %all-to-all-start.1 = ((bf16[32,48,128]{2,1,0:T(8,128)(2,1)}), bf16[32,48,128]{2,1,0:T(8,128)(2,1)S(1)}, u32[]{:S(2)}, u32[]{:S(2)}) async-start(bf16[32,48,128]{2,1,0:T(8,128)(2,1)} %order_stage.1), calls=%async_computation.1 | async-start | bytes 786432 | tf_op jit(solution)/shard_map/all_to_all | solution.py:407

commit v10 on v8

--- a/solution.py
+++ b/solution.py
@@ -51,7 +51,7 @@
         + SUB * np.arange(CHS)[:, None, None]
         + np.arange(SUB)[None, :, None]
     )
-    return orders.reshape(CHS, 1, PICKS, 1)
+    return orders.reshape(CHS, SUB, 1, BLOCKS, 1)
 
 
 def longitude_table():
@@ -59,17 +59,21 @@
     phases = (orders * np.arange(HALF_LON)) % NLON
     angles = phases * (2.0 * math.pi / NLON)
     weight = np.where(orders == 0, 1.0, 2.0)
-    table = np.concatenate([weight * np.cos(angles), -weight * np.sin(angles)], axis=1)
-    return table.reshape(CHS * LANES, HALF_LON).astype(ml_dtypes.bfloat16)
+    table = np.concatenate([weight * np.cos(angles), -weight * np.sin(angles)], axis=2)
+    table = np.swapaxes(table, 0, 1)
+    return table.reshape(SUB, CHS * PICKS, HALF_LON).astype(ml_dtypes.bfloat16)
 
 
 def wave_table():
     shifts = np.arange(TAPS)[:, None] - LON_REACH
-    orders = order_table().reshape(CHS, 1, PICKS)
+    orders = order_table().reshape(CHS, 1, SUB, 1, BLOCKS)
+    shifts = shifts.reshape(TAPS, 1, 1, 1)
     angles = ((orders * shifts) % NLON) * (2.0 * math.pi / NLON)
     waves = np.zeros((CHS, WAVE_ROWS, 2 * LANES), np.float32)
     cosine, sine = np.cos(angles), np.sin(angles)
-    waves[:, :TAPS] = np.concatenate([cosine, cosine, -sine, sine], axis=2)
+    for n, parts in enumerate(([cosine, cosine], [-sine, sine])):
+        both = np.concatenate(parts, axis=3).reshape(CHS, TAPS, LANES)
+        waves[:, :TAPS, n * LANES : (n + 1) * LANES] = both
     return waves
 
 
@@ -294,7 +298,9 @@
         )
         real = jnp.where(low, one, 0.0)
         imag = jnp.where(low, 0.0, one)
-        both = jnp.concatenate([real, imag, imag, real], axis=0).astype(BF)
+        turns = [real[:BLOCKS], imag[:BLOCKS], real[BLOCKS:], imag[BLOCKS:]]
+        swaps = [imag[:BLOCKS], real[:BLOCKS], imag[BLOCKS:], real[BLOCKS:]]
+        both = jnp.concatenate(turns + swaps, axis=0).astype(BF)
         mixed[r] = lax.dot_general(weights, both, NT, preferred_element_type=F32)
     for r in range(ROWS):
         total = None
@@ -337,15 +343,14 @@
     lines = rows * OWN
     departures = []
     for g in range(LON_PARTS):
-        even = jnp.concatenate(
-            [rows_ref[j, g * lines : (g + 1) * lines] for j in range(CHS)], axis=1
-        )
-        lane = lax.broadcasted_iota(jnp.int32, even.shape, 1)
-        flipped = jnp.where(lane % PICKS < BLOCKS, even.astype(F32), -even.astype(F32)).astype(BF)
-        both = jnp.concatenate([even, flipped], axis=0)
-        field = jnp.dot(both, table_ref[...], preferred_element_type=F32)
+        parts = []
+        for t in range(SUB):
+            lanes = slice(t * PICKS, (t + 1) * PICKS)
+            own = [rows_ref[j, g * lines : (g + 1) * lines, lanes] for j in range(CHS)]
+            lhs = jnp.concatenate(own, axis=1)
+            parts.append(jnp.dot(lhs, table_ref[t], preferred_element_type=F32))
         part = pl.ds(g * rows, rows)
-        halves = jnp.concatenate([field[:lines], field[lines:]], axis=1)
+        halves = jnp.concatenate([parts[0] + parts[1], parts[0] - parts[1]], axis=1)
         whole[part] = halves.astype(BF).reshape(rows, OWN, NLON)
         departures.append(pltpu.make_async_copy(whole.at[part], out_ref.at[part], sems.at[g]))
         departures[-1].start()

time: 75.6 us -> 75.7 us (level)
  no operation moved by 1% of the time
where the time goes in v10:
time: 75.7 us; the launch traced here: 75.3 us
  waiting for transfers between devices  27.9 us (37%)
  starting transfers between devices  21.6 us (29%)
  blocking collectives  14.8 us (20%)
  Pallas kernels  10.6 us (14%)
    all_to_all x1, waiting for transfers between devices, per_device(): by_row = lax.all_to_all(by_order, 'lat', 0, 0, tiled=True)  15.3 us
    all_to_all x1, blocking collectives, per_device(): own = lax.all_to_all(mixed, 'ch', 0, 0, tiled=True)  14.8 us
    all_to_all x1, starting transfers between devices, per_device(): leg = lax.all_to_all(picked, 'lat', 0, 0, tiled=True)  9.92 us
    ppermute x1, waiting for transfers between devices, per_device(): taken = lax.ppermute(given, 'ch', [(j, j ^ 1) for j in range(CHS)])  5.98 us
    ppermute x3, starting transfers between devices, per_device(): pieces.append(lax.ppermute(piece, 'ch', shift) if d else piece)  5 us
    pallas_call x1, Pallas kernels, pick(): pl.pallas_call(pick_kernel, out_shape=jax.ShapeDtypeStruct((LATS, ROWS *...  4.53 us
    all_to_all x1, waiting for transfers between devices, per_device(): leg = lax.all_to_all(picked, 'lat', 0, 0, tiled=True)  4.08 us
    all_to_all x1, starting transfers between devices, per_device(): by_row = lax.all_to_all(by_order, 'lat', 0, 0, tiled=True)  3.88 us
  transfers between devices with their start and end apart: 6, of which 5 were waited for; matrix products, arithmetic and copies ran while one was open for 0% of the time, Pallas kernels for 1%

profile of v10, /device:TPU:8, one launch (start us, length us, event | category | flops | bytes accessed | tf_op | source)
XLA Modules:
  0.0 75.3 jit_solution(2338816629377481289)
XLA Ops:
  0.0 0.0 copy-start.2
  0.0 0.0 copy-start.4
  0.0 0.0 copy-start.3
  0.0 4.5 %pick.1 = bf16[32,40,256]{2,1,0:T(8,128)(2,1)} custom-call(s32[32]{0:T(128)} %slots_ref.3, bf16[20,256,512]{2,1,0:T(8,128)(2,1)} %leg_ref.1), custom_call_target="tpu_custom_call" | custom-call | flops 335544320 | bytes 6291456 | tf_op jit(solution)/shard_map/pick/pallas_call | solution.py:142
  4.6 0.0 copy-start
  4.6 9.9 %all-to-all-start = ((bf16[32,40,256]{2,1,0:T(8,128)(2,1)}), bf16[32,40,256]{2,1,0:T(8,128)(2,1)S(1)}, u32[]{:S(2)}, u32[]{:S(2)}) async-start(bf16[32,40,256]{2,1,0:T(8,128)(2,1)} %pick.1), calls=%async_computation | async-start | bytes 1310720 | tf_op jit(solution)/shard_map/all_to_all | solution.py:381
  14.6 0.0 copy-done.6
  14.6 0.1 reshape.3
  14.8 0.5 collective-permute-start.2
  15.3 2.6 %collective-permute-start.1 = (bf16[2,64,256]{2,1,0:T(8,128)(2,1)S(1)}, bf16[2,64,256]{2,1,0:T(8,128)(2,1)S(1)}, u32[]{:S(2)}, u32[]{:S(2)}) collective-permute-start(bf16[2,64,256]{2,1,0:T(8,128)(2,1)S(1)} %get-tuple-element.25), channel_id=1, source_target_pairs={{0,4},{1,5},{2,6},{3,7},{4,0},{5,1},{6,2},{7,3},{8,12},{9,13},{10,... | collective-permute-start | bytes 196616 | tf_op jit(solution)/shard_map/ppermute | solution.py:388
  17.9 1.9 %collective-permute-start = (bf16[2,64,256]{2,1,0:T(8,128)(2,1)S(1)}, bf16[2,64,256]{2,1,0:T(8,128)(2,1)S(1)}, u32[]{:S(2)}, u32[]{:S(2)}) collective-permute-start(bf16[2,64,256]{2,1,0:T(8,128)(2,1)S(1)} %get-tuple-element.26), channel_id=1, source_target_pairs={{0,2},{1,3},{2,4},{3,5},{4,6},{5,7},{6,0},{7,1},{8,10},{9,11},{10,... | collective-permute-start | bytes 196616 | tf_op jit(solution)/shard_map/ppermute | solution.py:388
  19.8 0.0 collective-permute-done.2
  19.8 1.8 %collective-permute-done.1 = bf16[2,64,256]{2,1,0:T(8,128)(2,1)S(1)} collective-permute-done((bf16[2,64,256]{2,1,0:T(8,128)(2,1)S(1)}, bf16[2,64,256]{2,1,0:T(8,128)(2,1)S(1)}, u32[]{:S(2)}, u32[]{:S(2)}) %collective-permute-start.1) | collective-permute-done | bytes 65568 | tf_op jit(solution)/shard_map/ppermute | solution.py:388
  21.5 0.8 %collective-permute-done = bf16[2,64,256]{2,1,0:T(8,128)(2,1)S(1)} collective-permute-done((bf16[2,64,256]{2,1,0:T(8,128)(2,1)S(1)}, bf16[2,64,256]{2,1,0:T(8,128)(2,1)S(1)}, u32[]{:S(2)}, u32[]{:S(2)}) %collective-permute-start) | collective-permute-done | bytes 65568 | tf_op jit(solution)/shard_map/ppermute | solution.py:388
  22.4 2.8 %collective-permute-start.3 = (bf16[4,64,256]{2,1,0:T(8,128)(2,1)S(1)}, bf16[4,64,256]{2,1,0:T(8,128)(2,1)S(1)}, u32[]{:S(2)}, u32[]{:S(2)}) collective-permute-start(bf16[4,64,256]{2,1,0:T(8,128)(2,1)S(1)} %get-tuple-element.21), channel_id=1, source_target_pairs={{0,1},{1,0},{2,3},{3,2},{4,5},{5,4},{6,7},{7,6},{8,9},{9,8},{10,11... | collective-permute-start | bytes 393224 | tf_op jit(solution)/shard_map/ppermute | solution.py:392
  25.2 6.0 %collective-permute-done.3.refs_1_ = bf16[4,64,256]{2,1,0:T(8,128)(2,1)S(1)} collective-permute-done((bf16[4,64,256]{2,1,0:T(8,128)(2,1)S(1)}, bf16[4,64,256]{2,1,0:T(8,128)(2,1)S(1)}, u32[]{:S(2)}, u32[]{:S(2)}) %collective-permute-start.3) | collective-permute-done | bytes 131104 | tf_op jit(solution)/shard_map/ppermute | solution.py:392
  31.2 4.1 %all-to-all-done.leg_ref = bf16[32,40,256]{2,1,0:T(8,128)(2,1)S(1)} async-done(((bf16[32,40,256]{2,1,0:T(8,128)(2,1)}), bf16[32,40,256]{2,1,0:T(8,128)(2,1)S(1)}, u32[]{:S(2)}, u32[]{:S(2)}) %all-to-all-start) | async-done | bytes 655392 | tf_op jit(solution)/shard_map/all_to_all | solution.py:381
  35.3 1.6 %order_stage.1 = bf16[32,48,128]{2,1,0:T(8,128)(2,1)} custom-call(bf16[32,40,256]{2,1,0:T(8,128)(2,1)S(1)} %all-to-all-done.leg_ref, bf16[4,64,256]{2,1,0:T(8,128)(2,1)S(1)} %get-tuple-element.22.refs_0_, bf16[4,64,256]{2,1,0:T(8,128)(2,1)S(1)} %collective-permute-done.3.refs_1_), custom_call_target="tpu_custom_call" | custom-call | flops 734003200 | bytes 2097152 | tf_op jit(solution)/shard_map/order_stage/pallas_call | solution.py:228
  36.9 3.9 %all-to-all-start.1 = ((bf16[32,48,128]{2,1,0:T(8,128)(2,1)}), bf16[32,48,128]{2,1,0:T(8,128)(2,1)S(1)}, u32[]{:S(2)}, u32[]{:S(2)}) async-start(bf16[32,48,128]{2,1,0:T(8,128)(2,1)} %order_stage.1), calls=%async_computation.1 | async-start | bytes 786432 | tf_op jit(solution)/shard_map/all_to_all | solution.py:398
  40.8 0.6 coef_stage.1
  41.4 15.3 %all-to-all-done.1.rows_ref = bf16[32,48,128]{2,1,0:T(8,128)(2,1)S(1)} async-done(((bf16[32,48,128]{2,1,0:T(8,128)(2,1)}), bf16[32,48,128]{2,1,0:T(8,128)(2,1)S(1)}, u32[]{:S(2)}, u32[]{:S(2)}) %all-to-all-start.1) | async-done | bytes 393248 | tf_op jit(solution)/shard_map/all_to_all | solution.py:398
  56.7 2.4 %row_stage.1 = bf16[8,160,128]{2,1,0:T(8,128)(2,1)S(1)} custom-call(s32[32]{0:T(128)S(1)} %copy-done.5, bf16[32,48,128]{2,1,0:T(8,128)(2,1)S(1)} %all-to-all-done.1.rows_ref, f32[15,20,256]{2,1,0:T(8,128)S(1)} %get-tuple-element.19.coef_ref, bf16[192,128]{1,0:T(8,128)(2,1)S(1)} %get-tuple-element.20.mix_ref), custom_call_target="tpu_custom_call" | custom-call | flops 209715200 | bytes 2097152 | tf_op jit(solution)/shard_map/row_stage/pallas_call | solution.py:318
  59.1 14.8 %all_to_all.15.rows_ref = bf16[8,160,128]{2,1,0:T(8,128)(2,1)S(1)} all-to-all(bf16[8,160,128]{2,1,0:T(8,128)(2,1)S(1)} %row_stage.1), channel_id=1, replica_groups=mesh['lat'=32,'ch'=8] {'ch'}, dimensions={0} | all-to-all | bytes 655360 | tf_op jit(solution)/shard_map/all_to_all | solution.py:401
  73.9 1.5 %longitude_stage.1 = bf16[20,8,1440]{2,1,0:T(8,128)(2,1)} custom-call(bf16[8,160,128]{2,1,0:T(8,128)(2,1)S(1)} %all_to_all.15.rows_ref, bf16[2,512,720]{2,1,0:T(8,128)(2,1)S(1)} %copy-done), custom_call_target="tpu_custom_call" | custom-call | flops 503316480 | bytes 4194304 | tf_op jit(solution)/shard_map/longitude_stage/pallas_call | solution.py:362
  (12 shorter events, 0.1 us)
Async XLA Ops:
  0.0 40.8 %copy-start.1 = (f32[8,16,256]{2,1,0:T(8,128)S(1)}, f32[8,16,256]{2,1,0:T(8,128)}, u32[]{:S(2)}) copy-start(f32[8,16,256]{2,1,0:T(8,128)} %constant.73.clone.waves_ref) | copy-start | bytes 393220
  0.0 56.7 %copy-start.5 = (s32[32]{0:T(128)S(1)}, s32[32]{0:T(128)}, u32[]{:S(2)}) copy-start(s32[32]{0:T(128)} %slots_ref.3) | copy-start | bytes 388
  0.0 14.6 %copy-start.6 = (bf16[16,8,2,2,256]{4,3,2,1,0:T(2,128)(2,1)S(1)}, bf16[16,8,2,2,256]{4,3,2,1,0:T(2,128)(2,1)}, u32[]{:S(2)}) copy-start(bf16[16,8,2,2,256]{4,3,2,1,0:T(2,128)(2,1)} %param.8) | copy-start | bytes 786436
  0.0 40.8 %copy-start.2 = (bf16[3,20,6,9]{1,2,3,0:T(8,128)(2,1)S(1)}, bf16[3,20,6,9]{1,2,3,0:T(8,128)(2,1)}, u32[]{:S(2)}) copy-start(bf16[3,20,6,9]{1,2,3,0:T(8,128)(2,1)} %param.11) | copy-start | bytes 19444
  0.0 40.8 %copy-start.4 = (s32[20,6]{0,1:T(8,128)S(1)}, s32[20,6]{0,1:T(8,128)}, u32[]{:S(2)}) copy-start(s32[20,6]{0,1:T(8,128)} %param.12) | copy-start | bytes 1444
  0.0 40.8 %copy-start.3 = (bf16[3,64,64]{2,1,0:T(8,128)(2,1)S(1)}, bf16[3,64,64]{2,1,0:T(8,128)(2,1)}, u32[]{:S(2)}) copy-start(bf16[3,64,64]{2,1,0:T(8,128)(2,1)} %mix_ref) | copy-start | bytes 73732
  4.6 69.3 %copy-start = (bf16[2,512,720]{2,1,0:T(8,128)(2,1)S(1)}, bf16[2,512,720]{2,1,0:T(8,128)(2,1)}, u32[]{:S(2)}) copy-start(bf16[2,512,720]{2,1,0:T(8,128)(2,1)} %constant.74.clone.table_ref) | copy-start | bytes 4423684
  4.6 30.7 %all-to-all-start = ((bf16[32,40,256]{2,1,0:T(8,128)(2,1)}), bf16[32,40,256]{2,1,0:T(8,128)(2,1)S(1)}, u32[]{:S(2)}, u32[]{:S(2)}) async-start(bf16[32,40,256]{2,1,0:T(8,128)(2,1)} %pick.1), calls=%async_computation | async-start | bytes 1310720 | tf_op jit(solution)/shard_map/all_to_all | solution.py:381
  14.8 5.0 %collective-permute-start.2 = (bf16[2,64,256]{2,1,0:T(8,128)(2,1)S(1)}, bf16[2,64,256]{2,1,0:T(8,128)(2,1)S(1)}, u32[]{:S(2)}, u32[]{:S(2)}) collective-permute-start(bf16[2,64,256]{2,1,0:T(8,128)(2,1)S(1)} %get-tuple-element.24), channel_id=1, source_target_pairs={{0,6},{1,7},{2,0},{3,1},{4,2},{5,3},{6,4},{7,5},{8,14},{9,15},{10,... | collective-permute-start | bytes 196616 | tf_op jit(solution)/shard_map/ppermute | solution.py:388
  15.3 6.2 %collective-permute-start.1 = (bf16[2,64,256]{2,1,0:T(8,128)(2,1)S(1)}, bf16[2,64,256]{2,1,0:T(8,128)(2,1)S(1)}, u32[]{:S(2)}, u32[]{:S(2)}) collective-permute-start(bf16[2,64,256]{2,1,0:T(8,128)(2,1)S(1)} %get-tuple-element.25), channel_id=1, source_target_pairs={{0,4},{1,5},{2,6},{3,7},{4,0},{5,1},{6,2},{7,3},{8,12},{9,13},{10,... | collective-permute-start | bytes 196616 | tf_op jit(solution)/shard_map/ppermute | solution.py:388
  17.9 4.4 %collective-permute-start = (bf16[2,64,256]{2,1,0:T(8,128)(2,1)S(1)}, bf16[2,64,256]{2,1,0:T(8,128)(2,1)S(1)}, u32[]{:S(2)}, u32[]{:S(2)}) collective-permute-start(bf16[2,64,256]{2,1,0:T(8,128)(2,1)S(1)} %get-tuple-element.26), channel_id=1, source_target_pairs={{0,2},{1,3},{2,4},{3,5},{4,6},{5,7},{6,0},{7,1},{8,10},{9,11},{10,... | collective-permute-start | bytes 196616 | tf_op jit(solution)/shard_map/ppermute | solution.py:388
  22.4 8.8 %collective-permute-start.3 = (bf16[4,64,256]{2,1,0:T(8,128)(2,1)S(1)}, bf16[4,64,256]{2,1,0:T(8,128)(2,1)S(1)}, u32[]{:S(2)}, u32[]{:S(2)}) collective-permute-start(bf16[4,64,256]{2,1,0:T(8,128)(2,1)S(1)} %get-tuple-element.21), channel_id=1, source_target_pairs={{0,1},{1,0},{2,3},{3,2},{4,5},{5,4},{6,7},{7,6},{8,9},{9,8},{10,11... | collective-permute-start | bytes 393224 | tf_op jit(solution)/shard_map/ppermute | solution.py:392
  36.9 19.8 %all-to-all-start.1 = ((bf16[32,48,128]{2,1,0:T(8,128)(2,1)}), bf16[32,48,128]{2,1,0:T(8,128)(2,1)S(1)}, u32[]{:S(2)}, u32[]{:S(2)}) async-start(bf16[32,48,128]{2,1,0:T(8,128)(2,1)} %order_stage.1), calls=%async_computation.1 | async-start | bytes 786432 | tf_op jit(solution)/shard_map/all_to_all | solution.py:398

commit v11 on v8

--- a/solution.py
+++ b/solution.py
@@ -73,7 +73,7 @@
     return waves
 
 
-PICK_GROUPS = (4, 4, 8, 4)
+PICK_GROUPS = (8, 8, 4)
 EDGE = 12
 ORDER_LIMITS = (LMAX, LMAX - 2 * LANES)
 

time: 75.6 us -> 75.8 us (level)
  no operation moved by 1% of the time
where the time goes in v11:
time: 75.8 us; the launch traced here: 75.5 us
  waiting for transfers between devices  27.9 us (37%)
  starting transfers between devices  21.6 us (28%)
  blocking collectives  14.8 us (20%)
  Pallas kernels  10.7 us (14%)
    all_to_all x1, waiting for transfers between devices, per_device(): by_row = lax.all_to_all(by_order, 'lat', 0, 0, tiled=True)  15.3 us
    all_to_all x1, blocking collectives, per_device(): own = lax.all_to_all(mixed, 'ch', 0, 0, tiled=True)  14.8 us
    all_to_all x1, starting transfers between devices, per_device(): leg = lax.all_to_all(picked, 'lat', 0, 0, tiled=True)  9.93 us
    ppermute x1, waiting for transfers between devices, per_device(): taken = lax.ppermute(given, 'ch', [(j, j ^ 1) for j in range(CHS)])  5.99 us
    ppermute x3, starting transfers between devices, per_device(): pieces.append(lax.ppermute(piece, 'ch', shift) if d else piece)  5 us
    pallas_call x1, Pallas kernels, pick(): pl.pallas_call(pick_kernel, out_shape=jax.ShapeDtypeStruct((LATS, ROWS *...  4.71 us
    all_to_all x1, waiting for transfers between devices, per_device(): leg = lax.all_to_all(picked, 'lat', 0, 0, tiled=True)  4.08 us
    all_to_all x1, starting transfers between devices, per_device(): by_row = lax.all_to_all(by_order, 'lat', 0, 0, tiled=True)  3.88 us
  transfers between devices with their start and end apart: 6, of which 5 were waited for; matrix products, arithmetic and copies ran while one was open for 0% of the time, Pallas kernels for 1%

profile of v11, /device:TPU:8, one launch (start us, length us, event | category | flops | bytes accessed | tf_op | source)
XLA Modules:
  0.0 75.5 jit_solution(12165643760707379899)
XLA Ops:
  0.0 0.0 copy-start.2
  0.0 0.0 copy-start.4
  0.0 0.0 copy-start.3
  0.0 4.7 %pick.1 = bf16[32,40,256]{2,1,0:T(8,128)(2,1)} custom-call(s32[32]{0:T(128)} %slots_ref.3, bf16[20,256,512]{2,1,0:T(8,128)(2,1)} %leg_ref.1), custom_call_target="tpu_custom_call" | custom-call | flops 335544320 | bytes 6291456 | tf_op jit(solution)/shard_map/pick/pallas_call | solution.py:138
  4.8 0.0 copy-start
  4.8 9.9 %all-to-all-start = ((bf16[32,40,256]{2,1,0:T(8,128)(2,1)}), bf16[32,40,256]{2,1,0:T(8,128)(2,1)S(1)}, u32[]{:S(2)}, u32[]{:S(2)}) async-start(bf16[32,40,256]{2,1,0:T(8,128)(2,1)} %pick.1), calls=%async_computation | async-start | bytes 1310720 | tf_op jit(solution)/shard_map/all_to_all | solution.py:376
  14.8 0.0 copy-done.6
  14.8 0.1 reshape.3
  15.0 0.5 collective-permute-start.2
  15.5 2.6 %collective-permute-start.1 = (bf16[2,64,256]{2,1,0:T(8,128)(2,1)S(1)}, bf16[2,64,256]{2,1,0:T(8,128)(2,1)S(1)}, u32[]{:S(2)}, u32[]{:S(2)}) collective-permute-start(bf16[2,64,256]{2,1,0:T(8,128)(2,1)S(1)} %get-tuple-element.25), channel_id=1, source_target_pairs={{0,4},{1,5},{2,6},{3,7},{4,0},{5,1},{6,2},{7,3},{8,12},{9,13},{10,... | collective-permute-start | bytes 196616 | tf_op jit(solution)/shard_map/ppermute | solution.py:383
  18.1 1.9 %collective-permute-start = (bf16[2,64,256]{2,1,0:T(8,128)(2,1)S(1)}, bf16[2,64,256]{2,1,0:T(8,128)(2,1)S(1)}, u32[]{:S(2)}, u32[]{:S(2)}) collective-permute-start(bf16[2,64,256]{2,1,0:T(8,128)(2,1)S(1)} %get-tuple-element.26), channel_id=1, source_target_pairs={{0,2},{1,3},{2,4},{3,5},{4,6},{5,7},{6,0},{7,1},{8,10},{9,11},{10,... | collective-permute-start | bytes 196616 | tf_op jit(solution)/shard_map/ppermute | solution.py:383
  20.0 0.0 collective-permute-done.2
  20.0 1.8 %collective-permute-done.1 = bf16[2,64,256]{2,1,0:T(8,128)(2,1)S(1)} collective-permute-done((bf16[2,64,256]{2,1,0:T(8,128)(2,1)S(1)}, bf16[2,64,256]{2,1,0:T(8,128)(2,1)S(1)}, u32[]{:S(2)}, u32[]{:S(2)}) %collective-permute-start.1) | collective-permute-done | bytes 65568 | tf_op jit(solution)/shard_map/ppermute | solution.py:383
  21.7 0.8 %collective-permute-done = bf16[2,64,256]{2,1,0:T(8,128)(2,1)S(1)} collective-permute-done((bf16[2,64,256]{2,1,0:T(8,128)(2,1)S(1)}, bf16[2,64,256]{2,1,0:T(8,128)(2,1)S(1)}, u32[]{:S(2)}, u32[]{:S(2)}) %collective-permute-start) | collective-permute-done | bytes 65568 | tf_op jit(solution)/shard_map/ppermute | solution.py:383
  22.6 2.8 %collective-permute-start.3 = (bf16[4,64,256]{2,1,0:T(8,128)(2,1)S(1)}, bf16[4,64,256]{2,1,0:T(8,128)(2,1)S(1)}, u32[]{:S(2)}, u32[]{:S(2)}) collective-permute-start(bf16[4,64,256]{2,1,0:T(8,128)(2,1)S(1)} %get-tuple-element.21), channel_id=1, source_target_pairs={{0,1},{1,0},{2,3},{3,2},{4,5},{5,4},{6,7},{7,6},{8,9},{9,8},{10,11... | collective-permute-start | bytes 393224 | tf_op jit(solution)/shard_map/ppermute | solution.py:387
  25.4 6.0 %collective-permute-done.3.refs_1_ = bf16[4,64,256]{2,1,0:T(8,128)(2,1)S(1)} collective-permute-done((bf16[4,64,256]{2,1,0:T(8,128)(2,1)S(1)}, bf16[4,64,256]{2,1,0:T(8,128)(2,1)S(1)}, u32[]{:S(2)}, u32[]{:S(2)}) %collective-permute-start.3) | collective-permute-done | bytes 131104 | tf_op jit(solution)/shard_map/ppermute | solution.py:387
  31.4 4.1 %all-to-all-done.leg_ref = bf16[32,40,256]{2,1,0:T(8,128)(2,1)S(1)} async-done(((bf16[32,40,256]{2,1,0:T(8,128)(2,1)}), bf16[32,40,256]{2,1,0:T(8,128)(2,1)S(1)}, u32[]{:S(2)}, u32[]{:S(2)}) %all-to-all-start) | async-done | bytes 655392 | tf_op jit(solution)/shard_map/all_to_all | solution.py:376
  35.5 1.6 %order_stage.1 = bf16[32,48,128]{2,1,0:T(8,128)(2,1)} custom-call(bf16[32,40,256]{2,1,0:T(8,128)(2,1)S(1)} %all-to-all-done.leg_ref, bf16[4,64,256]{2,1,0:T(8,128)(2,1)S(1)} %get-tuple-element.22.refs_0_, bf16[4,64,256]{2,1,0:T(8,128)(2,1)S(1)} %collective-permute-done.3.refs_1_), custom_call_target="tpu_custom_call" | custom-call | flops 734003200 | bytes 2097152 | tf_op jit(solution)/shard_map/order_stage/pallas_call | solution.py:224
  37.1 3.9 %all-to-all-start.1 = ((bf16[32,48,128]{2,1,0:T(8,128)(2,1)}), bf16[32,48,128]{2,1,0:T(8,128)(2,1)S(1)}, u32[]{:S(2)}, u32[]{:S(2)}) async-start(bf16[32,48,128]{2,1,0:T(8,128)(2,1)} %order_stage.1), calls=%async_computation.1 | async-start | bytes 786432 | tf_op jit(solution)/shard_map/all_to_all | solution.py:393
  41.0 0.6 coef_stage.1
  41.6 15.3 %all-to-all-done.1.rows_ref = bf16[32,48,128]{2,1,0:T(8,128)(2,1)S(1)} async-done(((bf16[32,48,128]{2,1,0:T(8,128)(2,1)}), bf16[32,48,128]{2,1,0:T(8,128)(2,1)S(1)}, u32[]{:S(2)}, u32[]{:S(2)}) %all-to-all-start.1) | async-done | bytes 393248 | tf_op jit(solution)/shard_map/all_to_all | solution.py:393
  56.9 2.4 %row_stage.1 = bf16[8,160,128]{2,1,0:T(8,128)(2,1)S(1)} custom-call(s32[32]{0:T(128)S(1)} %copy-done.5, bf16[32,48,128]{2,1,0:T(8,128)(2,1)S(1)} %all-to-all-done.1.rows_ref, f32[15,20,256]{2,1,0:T(8,128)S(1)} %get-tuple-element.19.coef_ref, bf16[192,128]{1,0:T(8,128)(2,1)S(1)} %get-tuple-element.20.mix_ref), custom_call_target="tpu_custom_call" | custom-call | flops 209715200 | bytes 2097152 | tf_op jit(solution)/shard_map/row_stage/pallas_call | solution.py:312
  59.3 14.8 %all_to_all.15.rows_ref = bf16[8,160,128]{2,1,0:T(8,128)(2,1)S(1)} all-to-all(bf16[8,160,128]{2,1,0:T(8,128)(2,1)S(1)} %row_stage.1), channel_id=1, replica_groups=mesh['lat'=32,'ch'=8] {'ch'}, dimensions={0} | all-to-all | bytes 655360 | tf_op jit(solution)/shard_map/all_to_all | solution.py:396
  74.0 1.5 %longitude_stage.1 = bf16[20,8,1440]{2,1,0:T(8,128)(2,1)} custom-call(bf16[8,160,128]{2,1,0:T(8,128)(2,1)S(1)} %all_to_all.15.rows_ref, bf16[1024,720]{1,0:T(8,128)(2,1)S(1)} %copy-done), custom_call_target="tpu_custom_call" | custom-call | flops 503316480 | bytes 4194304 | tf_op jit(solution)/shard_map/longitude_stage/pallas_call | solution.py:357
  (12 shorter events, 0.1 us)
Async XLA Ops:
  0.0 41.0 %copy-start.1 = (f32[8,16,256]{2,1,0:T(8,128)S(1)}, f32[8,16,256]{2,1,0:T(8,128)}, u32[]{:S(2)}) copy-start(f32[8,16,256]{2,1,0:T(8,128)} %constant.73.clone.waves_ref) | copy-start | bytes 393220
  0.0 56.8 %copy-start.5 = (s32[32]{0:T(128)S(1)}, s32[32]{0:T(128)}, u32[]{:S(2)}) copy-start(s32[32]{0:T(128)} %slots_ref.3) | copy-start | bytes 388
  0.0 14.8 %copy-start.6 = (bf16[16,8,2,2,256]{4,3,2,1,0:T(2,128)(2,1)S(1)}, bf16[16,8,2,2,256]{4,3,2,1,0:T(2,128)(2,1)}, u32[]{:S(2)}) copy-start(bf16[16,8,2,2,256]{4,3,2,1,0:T(2,128)(2,1)} %param.8) | copy-start | bytes 786436
  0.0 41.0 %copy-start.2 = (bf16[3,20,6,9]{1,2,3,0:T(8,128)(2,1)S(1)}, bf16[3,20,6,9]{1,2,3,0:T(8,128)(2,1)}, u32[]{:S(2)}) copy-start(bf16[3,20,6,9]{1,2,3,0:T(8,128)(2,1)} %param.11) | copy-start | bytes 19444
  0.0 41.0 %copy-start.4 = (s32[20,6]{0,1:T(8,128)S(1)}, s32[20,6]{0,1:T(8,128)}, u32[]{:S(2)}) copy-start(s32[20,6]{0,1:T(8,128)} %param.12) | copy-start | bytes 1444
  0.0 41.0 %copy-start.3 = (bf16[3,64,64]{2,1,0:T(8,128)(2,1)S(1)}, bf16[3,64,64]{2,1,0:T(8,128)(2,1)}, u32[]{:S(2)}) copy-start(bf16[3,64,64]{2,1,0:T(8,128)(2,1)} %mix_ref) | copy-start | bytes 73732
  4.8 69.3 %copy-start = (bf16[1024,720]{1,0:T(8,128)(2,1)S(1)}, bf16[1024,720]{1,0:T(8,128)(2,1)}, u32[]{:S(2)}) copy-start(bf16[1024,720]{1,0:T(8,128)(2,1)} %constant.74.clone.table_ref) | copy-start | bytes 4423684
  4.8 30.7 %all-to-all-start = ((bf16[32,40,256]{2,1,0:T(8,128)(2,1)}), bf16[32,40,256]{2,1,0:T(8,128)(2,1)S(1)}, u32[]{:S(2)}, u32[]{:S(2)}) async-start(bf16[32,40,256]{2,1,0:T(8,128)(2,1)} %pick.1), calls=%async_computation | async-start | bytes 1310720 | tf_op jit(solution)/shard_map/all_to_all | solution.py:376
  15.0 5.0 %collective-permute-start.2 = (bf16[2,64,256]{2,1,0:T(8,128)(2,1)S(1)}, bf16[2,64,256]{2,1,0:T(8,128)(2,1)S(1)}, u32[]{:S(2)}, u32[]{:S(2)}) collective-permute-start(bf16[2,64,256]{2,1,0:T(8,128)(2,1)S(1)} %get-tuple-element.24), channel_id=1, source_target_pairs={{0,6},{1,7},{2,0},{3,1},{4,2},{5,3},{6,4},{7,5},{8,14},{9,15},{10,... | collective-permute-start | bytes 196616 | tf_op jit(solution)/shard_map/ppermute | solution.py:383
  15.5 6.2 %collective-permute-start.1 = (bf16[2,64,256]{2,1,0:T(8,128)(2,1)S(1)}, bf16[2,64,256]{2,1,0:T(8,128)(2,1)S(1)}, u32[]{:S(2)}, u32[]{:S(2)}) collective-permute-start(bf16[2,64,256]{2,1,0:T(8,128)(2,1)S(1)} %get-tuple-element.25), channel_id=1, source_target_pairs={{0,4},{1,5},{2,6},{3,7},{4,0},{5,1},{6,2},{7,3},{8,12},{9,13},{10,... | collective-permute-start | bytes 196616 | tf_op jit(solution)/shard_map/ppermute | solution.py:383
  18.1 4.4 %collective-permute-start = (bf16[2,64,256]{2,1,0:T(8,128)(2,1)S(1)}, bf16[2,64,256]{2,1,0:T(8,128)(2,1)S(1)}, u32[]{:S(2)}, u32[]{:S(2)}) collective-permute-start(bf16[2,64,256]{2,1,0:T(8,128)(2,1)S(1)} %get-tuple-element.26), channel_id=1, source_target_pairs={{0,2},{1,3},{2,4},{3,5},{4,6},{5,7},{6,0},{7,1},{8,10},{9,11},{10,... | collective-permute-start | bytes 196616 | tf_op jit(solution)/shard_map/ppermute | solution.py:383
  22.6 8.8 %collective-permute-start.3 = (bf16[4,64,256]{2,1,0:T(8,128)(2,1)S(1)}, bf16[4,64,256]{2,1,0:T(8,128)(2,1)S(1)}, u32[]{:S(2)}, u32[]{:S(2)}) collective-permute-start(bf16[4,64,256]{2,1,0:T(8,128)(2,1)S(1)} %get-tuple-element.21), channel_id=1, source_target_pairs={{0,1},{1,0},{2,3},{3,2},{4,5},{5,4},{6,7},{7,6},{8,9},{9,8},{10,11... | collective-permute-start | bytes 393224 | tf_op jit(solution)/shard_map/ppermute | solution.py:387
  37.1 19.8 %all-to-all-start.1 = ((bf16[32,48,128]{2,1,0:T(8,128)(2,1)}), bf16[32,48,128]{2,1,0:T(8,128)(2,1)S(1)}, u32[]{:S(2)}, u32[]{:S(2)}) async-start(bf16[32,48,128]{2,1,0:T(8,128)(2,1)} %order_stage.1), calls=%async_computation.1 | async-start | bytes 786432 | tf_op jit(solution)/shard_map/all_to_all | solution.py:393
